TPU v7x, 32 devices: a whole 2x2x4 slice. The times are simulated.
32 devices in a mesh: comp: 2 (over core), tile: 16 (over z, y, x).
Axes of the slice: x: 2, y: 2, z: 4, core: 2. Of those that a mesh axis runs over, the one named last changes fastest.
Arguments:
- state: float32 [2, 8, 256, 1024], P('comp', None, 'tile'), may hold values from -80 to 80, as said below
- basis: bfloat16 [12, 2, 8, 256, 1024], P(None, 'comp', None, 'tile'), may hold values from -4 to 4
- kappa: float32 [2, 256, 1024], P('comp', 'tile'), may hold values from 0.05 to 0.22
- vmix: float32 [2, 8, 8], P('comp'), may hold values from -1 to 1
- land_mask: int32 [256, 1024], P('tile'), may hold values 0 or 1
- send_rows: int32 [2, 16, 16, 8], P('comp', 'tile'), may hold values from 0 to 127
- recv_slots: int32 [2, 16, 128, 4], P('comp', 'tile'), may hold values from 0 to 127
- recv_weights: float32 [2, 16, 128, 4], P('comp', 'tile'), may hold values from 0.1 to 0.4
Outputs:
- direction: float32 [2, 8, 256, 1024], P('comp', None, 'tile')
- coefs: float32 [12], replicated
Inputs may be any that keep to these rules, and one draw needn't show every extreme that they name: `state`: the perturbation is noise plus a combination of the basis vectors.
All inputs are finite; a program needn't handle non-finite values. No bound on the sum of `land_mask` on one device may be relied on, other than what follows from the above.
Results may differ from a plain program's by a relative error of at most 0.0003.
Values sent between devices are 32-bit elements; how exact they have to be, the bound alone decides.
No kernel may reach another device: no remote copies, remote signals or barrier semaphores. Data moves between devices by JAX's collectives and lax.ppermute only.
A program may use at most 64 MiB of HBM per device.

v0:
```python
import jax
import jax.numpy as jnp
from jax import lax
from jax.sharding import PartitionSpec as P

FLUX = 4
VECS = 12


def extended(cells, sides, width):
    for axis, dim in sides:
        count = lax.axis_size(axis)
        ends = count - 1
        head = lax.slice_in_dim(cells, 0, width, axis=dim)
        tail = lax.slice_in_dim(cells, cells.shape[dim] - width, cells.shape[dim], axis=dim)
        cells = jnp.concatenate(
            [
                lax.ppermute(tail, axis, [(i, (i + 1) % count) for i in range(ends)]),
                cells,
                lax.ppermute(head, axis, [((i + 1) % count, i) for i in range(ends)]),
            ],
            axis=dim,
        )
    return cells


def from_partner(block, axis, stride):
    count = lax.axis_size(axis)
    route = []
    for low in range(count):
        high = low | 1 << stride
        if high != low and high < count:
            route += [(low, high), (high, low)]
    return lax.ppermute(block, axis, route)


def advance(x, kap, vert_mat, maskf, forced):
    padded = extended(x, (("tile", 1),), 1)
    lap = padded[:, 2:] + padded[:, :-2] + jnp.roll(x, 1, -1) + jnp.roll(x, -1, -1) - 4.0 * x
    vert = jnp.einsum("lm,mrq->lrq", vert_mat, x, precision=lax.Precision.HIGHEST)
    return maskf * (x + kap * lap + vert + forced)


def body(state, basis, kappa, vmix, land_mask, send_rows, recv_slots, recv_weights):
    comp_id = lax.axis_index("comp")
    x = state[0]
    levels, rows, cols = x.shape
    nblk = rows * cols // 128
    surface = x[:FLUX].reshape(FLUX, nblk, 128)
    bucket = surface[:, send_rows[0, 0]]
    moved = lax.all_to_all(bucket, "tile", split_axis=1, concat_axis=1, tiled=True)
    arrived = from_partner(moved, "comp", 0)
    flat = arrived.reshape(FLUX, -1, 128)
    picked = flat[:, recv_slots[0, 0]]
    imported = jnp.einsum(
        "ek,fekq->feq", recv_weights[0, 0], picked, precision=lax.Precision.HIGHEST
    )
    imported = imported.reshape(FLUX, rows, cols)
    forced = jnp.concatenate([imported, jnp.zeros((levels - FLUX, rows, cols), jnp.float32)], 0)
    maskf = jnp.where(comp_id == 0, land_mask.astype(jnp.float32), jnp.float32(1.0))
    for step in range(2):
        x = advance(x, kappa[0], vmix[0], maskf, forced)
    total = float(levels * rows * cols * lax.axis_size("comp") * lax.axis_size("tile"))
    vflat = x.reshape(-1)
    qmat = basis[:, 0].reshape(VECS, -1)
    local_dots = jnp.dot(
        qmat, vflat, precision=lax.Precision.HIGHEST, preferred_element_type=jnp.float32
    )
    local_gram = jnp.dot(qmat, qmat.T, preferred_element_type=jnp.float32)
    dots, squares, gram = lax.psum(
        (local_dots, jnp.sum(vflat * vflat), local_gram), ("comp", "tile")
    )
    coefs = dots / total
    remain = vflat - jnp.dot(
        coefs, qmat, precision=lax.Precision.HIGHEST, preferred_element_type=jnp.float32
    )
    normsq = (
        squares
        - 2.0 * total * jnp.sum(coefs * coefs)
        + jnp.dot(
            coefs,
            jnp.dot(gram, coefs, precision=lax.Precision.HIGHEST),
            precision=lax.Precision.HIGHEST,
        )
    )
    direction = remain / jnp.sqrt(normsq / total + 1e-06)
    return (direction.reshape(1, levels, rows, cols), coefs)


def solution(mesh):
    return jax.shard_map(
        body,
        mesh=mesh,
        in_specs=(
            P("comp", None, "tile", None),
            P(None, "comp", None, "tile", None),
            P("comp", "tile", None),
            P("comp", None, None),
            P("tile", None),
            P("comp", "tile", None, None),
            P("comp", "tile", None, None),
            P("comp", "tile", None, None),
        ),
        out_specs=(P("comp", None, "tile", None), P()),
        check_vma=False,
    )
```

profile of v0, /device:TPU:0, one launch (start us, length us, event | category | flops | bytes accessed | tf_op | source)
XLA Modules:
  0.0 113.7 jit_solution(10225340703240517486)
XLA Ops:
  0.7 1.4 %copy.38 = f32[1,8,16,1024]{3,1,2,0:T(8,128)S(1)} copy(f32[1,8,16,1024]{3,2,1,0:T(8,128)} %param.8) | data formatting | bytes 1048576 | tf_op args[0]
  2.0 1.3 %collective-permute-start = (f32[8,1,1024]{2,0,1:T(8,128)S(1)}, f32[8,1,1024]{2,0,1:T(8,128)S(1)}, u32[]{:S(2)}, u32[]{:S(2)}) collective-permute-start(f32[8,1,1024]{2,0,1:T(8,128)S(1)} %get-tuple-element.17), channel_id=1, source_target_pairs={{1,0},{2,1},{3,2},{4,3},{5,4},{6,5},{7,6},{8,7},{9,8},{10,9},{11,1... | collective-permute-start | bytes 98312 | tf_op jit(solution)/shard_map/ppermute | solution.py:20
  3.3 5.5 %collective-permute-start.1 = (f32[8,1,1024]{2,0,1:T(8,128)S(1)}, f32[8,1,1024]{2,0,1:T(8,128)S(1)}, u32[]{:S(2)}, u32[]{:S(2)}) collective-permute-start(f32[8,1,1024]{2,0,1:T(8,128)S(1)} %get-tuple-element.18), channel_id=1, source_target_pairs={{0,1},{1,2},{2,3},{3,4},{4,5},{5,6},{6,7},{7,8},{8,9},{9,10},{10,1... | collective-permute-start | bytes 98312 | tf_op jit(solution)/shard_map/ppermute | solution.py:18
  8.8 1.0 slice.68
  10.0 0.7 compare_select_fusion
  10.9 1.4 %gather_fusion = f32[128,4,128]{2,1,0:T(4,128)} fusion(f32[4,128,128]{2,0,1:T(4,128)S(1)} %copy.18, s32[1024]{0:T(1024)S(1)} %pad_clamp_fusion.1), kind=kCustom, calls=%fused_computation | custom fusion | bytes 524800 | tf_op jit(solution)/shard_map/gather | solution.py:50
  12.4 8.2 %all-to-all-start = ((f32[4,16,8,128]{3,0,2,1:T(4,128)}), f32[4,16,8,128]{3,0,2,1:T(4,128)S(1)}, u32[]{:S(2)}, u32[]{:S(2)}) async-start(f32[4,16,8,128]{3,0,2,1:T(4,128)} %bitcast.6), calls=%async_computation | async-start | bytes 524288 | tf_op jit(solution)/shard_map/all_to_all | solution.py:51
  20.6 0.7 compare_select_fusion.1
  21.7 2.3 %pad.27 = bf16[16,128,1024]{2,1,0:T(8,128)(2,1)S(1)} pad(bf16[12,128,1024]{2,1,0:T(8,128)(2,1)} %bitcast.89, bf16[]{:T(256)} %constant.53), padding=0_4x0_0x0_0 | pad | bytes 7340034
  24.0 4.3 %copy.30 = bf16[2,8,128,1024]{3,1,2,0:T(8,128)(2,1)} copy(bf16[2,8,128,1024]{3,2,1,0:T(8,128)(2,1)S(1)} %bitcast.81) | data formatting | bytes 8388608
  28.3 9.4 %fusion.7 = f32[12,12]{1,0:T(8,128)S(1)} fusion(bf16[12,8,16,1024]{3,2,1,0:T(8,128)(2,1)} %bitcast.90), kind=kOutput, calls=%fused_computation.11 | convolution fusion | flops 37748736 | bytes 3146304 | tf_op jit(solution)/shard_map/dot_general | solution.py:69
  38.0 1.3 %collective-permute-done.2 = f32[4,16,8,128]{3,0,2,1:T(4,128)S(1)} collective-permute-done((f32[4,16,8,128]{3,0,2,1:T(4,128)S(1)}, f32[4,16,8,128]{3,0,2,1:T(4,128)S(1)}, u32[]{:S(2)}, u32[]{:S(2)}) %collective-permute-start.2) | collective-permute-done | bytes 262176 | tf_op jit(solution)/shard_map/ppermute | solution.py:34
  39.3 2.3 %gather_fusion.1 = f32[512,4,128]{2,1,0:T(4,128)S(1)} fusion(f32[4,128,128]{2,0,1:T(4,128)S(1)} %bitcast.88, s32[1024]{0:T(1024)S(1)} %pad_clamp_fusion), kind=kCustom, calls=%fused_computation.1 | custom fusion | bytes 2099200 | tf_op jit(solution)/shard_map/gather | solution.py:54
  41.6 2.0 %fusion.11 = f32[128,1,4,128]{3,1,2,0:T(1,128)S(1)} fusion(f32[128,4,1,1]{1,2,3,0:T(1,128)S(1)} %copy.24, f32[4,128,4,128]{3,0,2,1:T(4,128)S(1)} %bitcast.87), kind=kOutput, calls=%fused_computation.15 | convolution fusion | flops 3145728 | bytes 1312768 | tf_op jit(solution)/shard_map/ek,fekq->feq/dot_general | solution.py:55
  43.7 0.9 fusion.6
  44.8 1.3 %collective-permute-start.3 = (f32[8,1,1024]{2,0,1:T(8,128)S(1)}, f32[8,1,1024]{2,0,1:T(8,128)S(1)}, u32[]{:S(2)}, u32[]{:S(2)}) collective-permute-start(f32[8,1,1024]{2,0,1:T(8,128)S(1)} %get-tuple-element.11), channel_id=1, source_target_pairs={{1,0},{2,1},{3,2},{4,3},{5,4},{6,5},{7,6},{8,7},{9,8},{10,9},{11,1... | collective-permute-start | bytes 98312 | tf_op jit(solution)/shard_map/ppermute | solution.py:20
  46.1 4.5 %collective-permute-start.4 = (f32[8,1,1024]{2,0,1:T(8,128)S(1)}, f32[8,1,1024]{2,0,1:T(8,128)S(1)}, u32[]{:S(2)}, u32[]{:S(2)}) collective-permute-start(f32[8,1,1024]{2,0,1:T(8,128)S(1)} %get-tuple-element.12), channel_id=1, source_target_pairs={{0,1},{1,2},{2,3},{3,4},{4,5},{5,6},{6,7},{7,8},{8,9},{9,10},{10,1... | collective-permute-start | bytes 98312 | tf_op jit(solution)/shard_map/ppermute | solution.py:18
  50.7 1.5 %collective-permute-done.4 = f32[8,1,1024]{2,0,1:T(8,128)S(1)} collective-permute-done((f32[8,1,1024]{2,0,1:T(8,128)S(1)}, f32[8,1,1024]{2,0,1:T(8,128)S(1)}, u32[]{:S(2)}, u32[]{:S(2)}) %collective-permute-start.4) | collective-permute-done | bytes 32800 | tf_op jit(solution)/shard_map/ppermute | solution.py:18
  52.2 1.4 %multiply_reduce_fusion = (f32[]{:T(128)}, f32[8,16,1024]{2,0,1:T(8,128)S(1)}) fusion(f32[4,16,1024]{2,0,1:T(4,128)S(1)} %bitcast.94, f32[8,16,1024]{2,0,1:T(8,128)S(1)} %fusion.6, f32[1,8,8]{2,1,0:T(8,128)S(1)} %copy-done, f32[8,16,1]{2,0,1:T(8,128)S(1)} %get-tuple-element.9, f32[8,16,1023]{2,0,1:T(8,128)S(1)} %get-tuple-element.7, ...), kind=kOutput, calls=%fused_computation.35 | convolution fusion | flops 14680063 | bytes 2556164 | tf_op jit(solution)/shard_map/lm,mrq->lrq/dot_general | solution.py:40
  54.6 6.5 %convolution_bitcast_fusion.1 = f32[12]{0:T(128)S(1)} fusion(f32[131072,1]{0,1:T(1,128)S(1)} %reshape.109, bf16[12,131072]{1,0:T(8,128)(2,1)} %bitcast.79), kind=kOutput, calls=%fused_computation.12 | convolution fusion | flops 18874368 | bytes 3670064 | tf_op jit(solution)/shard_map/dot_general | solution.py:66
  61.1 44.3 %all-reduce.1 = (f32[12]{0:T(128)S(1)}, f32[]{:T(128)}, f32[12,12]{1,0:T(8,128)S(1)}) all-reduce(f32[12]{0:T(128)S(1)} %convolution_bitcast_fusion.1, f32[]{:T(128)} %get-tuple-element.19, f32[12,12]{1,0:T(8,128)S(1)} %fusion.7), channel_id=1, replica_groups=mesh['comp'=2,'tile'=16] {'comp','tile'}, use_global_device_ids=true, to_apply=%region_0.1 | all-reduce | flops 157 | bytes 1256 | tf_op jit(solution)/shard_map/psum | solution.py:70
  106.0 4.0 %fusion.29 = f32[1,131072]{1,0:T(1,128)S(1)} fusion(bf16[12,131072]{1,0:T(8,128)(2,1)} %bitcast.80, f32[12]{0:T(128)S(1)} %get-tuple-element.6), kind=kOutput, calls=%fused_computation.45 | convolution fusion | flops 18874368 | bytes 3670064 | tf_op jit(solution)/shard_map/dot_general | solution.py:74
  110.0 0.8 fusion.13
  112.8 0.9 reshape.87
  (36 shorter events, 3.1 us)
Async XLA Ops:
  0.6 43.0 %copy-start = (f32[1,8,8]{2,1,0:T(8,128)S(1)}, f32[1,8,8]{2,1,0:T(8,128)}, u32[]{:S(2)}) copy-start(f32[1,8,8]{2,1,0:T(8,128)} %param.11) | copy-start | bytes 772
  0.6 20.9 %copy-start.3 = (f32[1,1,128,4]{2,3,1,0:T(4,128)S(1)}, f32[1,1,128,4]{2,3,1,0:T(4,128)}, u32[]{:S(2)}) copy-start(f32[1,1,128,4]{2,3,1,0:T(4,128)} %param.15) | copy-start | bytes 6148
  2.0 41.6 %collective-permute-start = (f32[8,1,1024]{2,0,1:T(8,128)S(1)}, f32[8,1,1024]{2,0,1:T(8,128)S(1)}, u32[]{:S(2)}, u32[]{:S(2)}) collective-permute-start(f32[8,1,1024]{2,0,1:T(8,128)S(1)} %get-tuple-element.17), channel_id=1, source_target_pairs={{1,0},{2,1},{3,2},{4,3},{5,4},{6,5},{7,6},{8,7},{9,8},{10,9},{11,1... | collective-permute-start | bytes 98312 | tf_op jit(solution)/shard_map/ppermute | solution.py:20
  3.3 40.3 %collective-permute-start.1 = (f32[8,1,1024]{2,0,1:T(8,128)S(1)}, f32[8,1,1024]{2,0,1:T(8,128)S(1)}, u32[]{:S(2)}, u32[]{:S(2)}) collective-permute-start(f32[8,1,1024]{2,0,1:T(8,128)S(1)} %get-tuple-element.18), channel_id=1, source_target_pairs={{0,1},{1,2},{2,3},{3,4},{4,5},{5,6},{6,7},{7,8},{8,9},{9,10},{10,1... | collective-permute-start | bytes 98312 | tf_op jit(solution)/shard_map/ppermute | solution.py:18
  12.4 25.4 %all-to-all-start = ((f32[4,16,8,128]{3,0,2,1:T(4,128)}), f32[4,16,8,128]{3,0,2,1:T(4,128)S(1)}, u32[]{:S(2)}, u32[]{:S(2)}) async-start(f32[4,16,8,128]{3,0,2,1:T(4,128)} %bitcast.6), calls=%async_computation | async-start | bytes 524288 | tf_op jit(solution)/shard_map/all_to_all | solution.py:51
  24.0 4.3 %copy-start.1 = (s32[16,1024]{1,0:T(8,128)S(1)}, s32[16,1024]{1,0:T(8,128)}, u32[]{:S(2)}) copy-start(s32[16,1024]{1,0:T(8,128)} %param.12) | copy-start | bytes 196612
  37.7 5.9 %copy-start.4 = (f32[1,16,1024]{2,1,0:T(8,128)S(1)}, f32[1,16,1024]{2,1,0:T(8,128)}, u32[]{:S(2)}) copy-start(f32[1,16,1024]{2,1,0:T(8,128)} %param.10) | copy-start | bytes 196612
  37.7 1.6 %collective-permute-start.2 = (f32[4,16,8,128]{3,0,2,1:T(4,128)S(1)}, f32[4,16,8,128]{3,0,2,1:T(4,128)S(1)}, u32[]{:S(2)}, u32[]{:S(2)}) collective-permute-start(f32[4,16,8,128]{3,0,2,1:T(4,128)S(1)} %all-to-all-done), channel_id=1, source_target_pairs={{0,16},{16,0},{1,17},{17,1},{2,18},{18,2},{3,19},{19,3},{4,20},{20... | collective-permute-start | bytes 786440 | tf_op jit(solution)/shard_map/ppermute | solution.py:34
  44.8 5.9 %collective-permute-start.3 = (f32[8,1,1024]{2,0,1:T(8,128)S(1)}, f32[8,1,1024]{2,0,1:T(8,128)S(1)}, u32[]{:S(2)}, u32[]{:S(2)}) collective-permute-start(f32[8,1,1024]{2,0,1:T(8,128)S(1)} %get-tuple-element.11), channel_id=1, source_target_pairs={{1,0},{2,1},{3,2},{4,3},{5,4},{6,5},{7,6},{8,7},{9,8},{10,9},{11,1... | collective-permute-start | bytes 98312 | tf_op jit(solution)/shard_map/ppermute | solution.py:20
  46.1 6.1 %collective-permute-start.4 = (f32[8,1,1024]{2,0,1:T(8,128)S(1)}, f32[8,1,1024]{2,0,1:T(8,128)S(1)}, u32[]{:S(2)}, u32[]{:S(2)}) collective-permute-start(f32[8,1,1024]{2,0,1:T(8,128)S(1)} %get-tuple-element.12), channel_id=1, source_target_pairs={{0,1},{1,2},{2,3},{3,4},{4,5},{5,6},{6,7},{7,8},{8,9},{9,10},{10,1... | collective-permute-start | bytes 98312 | tf_op jit(solution)/shard_map/ppermute | solution.py:18
  106.0 6.8 %copy-start.2 = (f32[12]{0:T(128)}, f32[12]{0:T(128)S(1)}, u32[]{:S(2)}) copy-start(f32[12]{0:T(128)S(1)} %get-tuple-element.6) | copy-start | bytes 148
where the time goes:
time: 114 us
  blocking collectives  44.3 us (39%)
  matrix products  25 us (22%)
  starting transfers between devices  20.9 us (18%)
  local copies, waits for them, and re-layouts  15.8 us (14%)
  waiting for transfers between devices  2.82 us (2%)
  between operations  2.77 us (2%)
  other arithmetic  2.05 us (2%)
    psum x1, blocking collectives, body(): lax.psum((local_dots, jnp.sum(vflat * vflat), local_gram), ('comp', 'tile'))  44.3 us
    ppermute x2, starting transfers between devices, extended(): lax.ppermute(tail, axis, [(i, (i + 1) % count) for i in range(ends)])  10 us
    dot_general x1, matrix products, body(): local_gram = jnp.dot(qmat, qmat.T, preferred_element_type=jnp.float32)  9.43 us
    all_to_all x1, starting transfers between devices, body(): lax.all_to_all(bucket, 'tile', split_axis=1, concat_axis=1, tiled=True)  8.18 us
    unnamed x14, local copies, waits for them, and re-layouts  8.08 us
    dot_general x1, matrix products, body(): jnp.dot(qmat, vflat, precision=lax.Precision.HIGHEST, preferred_element_t...  6.49 us
    dot_general x1, matrix products, body(): jnp.dot(coefs, qmat, precision=lax.Precision.HIGHEST, preferred_element_t...  4 us
    ppermute x2, starting transfers between devices, extended(): lax.ppermute(head, axis, [((i + 1) % count, i) for i in range(ends)])  2.58 us
  transfers between devices with their start and end apart: 6, of which 2 were waited for; matrix products, arithmetic and copies ran while one was open for 22% of the time, Pallas kernels for 0%

commit v1 on v0

v1 whole, which is shorter than its diff:
```python
import functools

import jax
import jax.numpy as jnp
from jax import lax
from jax.experimental import pallas as pl
from jax.experimental.pallas import tpu as pltpu
from jax.sharding import PartitionSpec as P

FLUX = 4
LANES = 128
VMEM = pl.BlockSpec(memory_space=pltpu.VMEM)
SMEM = pl.BlockSpec(memory_space=pltpu.SMEM)
LIMIT = 24 << 20


def call(kernel, outs, in_specs, out_specs, scratch=(), cost=None):
    return pl.pallas_call(
        kernel,
        out_shape=outs,
        in_specs=in_specs,
        out_specs=out_specs,
        scratch_shapes=list(scratch),
        cost_estimate=cost,
        compiler_params=pltpu.CompilerParams(vmem_limit_bytes=LIMIT),
    )


def split(a):
    high = a.astype(jnp.bfloat16)
    return high, (a - high.astype(jnp.float32)).astype(jnp.bfloat16)


def gather_kernel(rows, rows_ref, state_ref, out_ref, x_ref, sems):
    cap, bands = rows_ref.shape
    per = x_ref.shape[0]
    top = FLUX * rows
    copies = []
    for part, (lo, hi) in enumerate(((0, top), (top, x_ref.shape[1]))):
        for c in range(per):
            copy = pltpu.make_async_copy(
                state_ref.at[lo:hi, c * LANES : (c + 1) * LANES],
                x_ref.at[c, lo:hi, :],
                sems.at[part * per + c],
            )
            copy.start()
            copies.append(copy)
    for copy in copies[:per]:
        copy.wait()

    def band(d, carry):
        for j in range(cap):
            b = rows_ref[j, d]
            r = lax.div(b, per)
            piece = x_ref[lax.rem(b, per), pl.ds(r, FLUX, stride=rows), :]
            out_ref[pl.ds(d * (cap * FLUX) + j, FLUX, stride=cap), :] = piece
        return carry

    lax.fori_loop(0, bands, band, 0)
    for copy in copies[per:]:
        copy.wait()


def early_kernel(slots_ref, weights_ref, basis_ref, matrix_ref, gram_ref):
    over, blocks = slots_ref.shape
    slots = matrix_ref.shape[2]
    row = lax.broadcasted_iota(jnp.int32, (slots, blocks), 0)
    mat = jnp.zeros((slots, blocks), jnp.float32)
    for k in range(over):
        mat = mat + jnp.where(slots_ref[k : k + 1, :] == row, weights_ref[k : k + 1, :], 0.0)
    high, low = split(mat.T)
    matrix_ref[0] = high
    matrix_ref[1] = low

    vecs, levels, rows, cols = basis_ref.shape
    n = vecs * rows
    total = jnp.zeros((n, n), jnp.float32)
    for l in range(levels):
        a = basis_ref[:, l].reshape(n, cols)
        total = total + lax.dot_general(
            a, a, (((1,), (1,)), ((), ())), preferred_element_type=jnp.float32
        )
    i0 = lax.broadcasted_iota(jnp.int32, (n, n), 0)
    i1 = lax.broadcasted_iota(jnp.int32, (n, n), 1)
    total = jnp.where(lax.rem(i0, rows) == lax.rem(i1, rows), total, 0.0)
    part = jnp.sum(total.reshape(vecs, rows, n), axis=1)
    j0 = lax.broadcasted_iota(jnp.int32, (n, LANES), 0)
    j1 = lax.broadcasted_iota(jnp.int32, (n, LANES), 1)
    fold = jnp.where(lax.div(j0, rows) == j1, 1.0, 0.0)
    gram = jnp.dot(part, fold, precision=lax.Precision.HIGHEST)
    packed = [jnp.zeros((1, LANES), jnp.float32), jnp.zeros((1, LANES), jnp.float32)]
    for i in range(vecs):
        shift = 16 * (i % 8)
        line = gram[i : i + 1, :]
        packed[i // 8] = packed[i // 8] + (pltpu.roll(line, shift, 1) if shift else line)
    gram_ref[...] = jnp.concatenate(packed, axis=0)


def shifted(parts, up):
    n = len(parts)
    lane = lax.broadcasted_iota(jnp.int32, parts[0].shape, 1)
    rolled = [pltpu.roll(p, 1 if up else LANES - 1, 1) for p in parts]
    edge = 0 if up else LANES - 1
    step = -1 if up else 1
    return [jnp.where(lane == edge, rolled[(c + step) % n], rolled[c]) for c in range(n)]


def regrid_kernel(
    rows, buf_ref, matrix_ref, x_ref, kappa_ref, mask_ref, vmix_ref, f_ref, p1_ref, p2_ref
):
    slots = matrix_ref.shape[2]
    per = x_ref.shape[0]
    levels = x_ref.shape[1] // rows
    cap = buf_ref.shape[1] // FLUX
    wide = jnp.concatenate(
        [buf_ref[:, f * cap : (f + 1) * cap, :].reshape(slots, LANES) for f in range(FLUX)], axis=1
    )
    bh, bl = split(wide)
    wh, wl = matrix_ref[0], matrix_ref[1]
    dot = functools.partial(jnp.dot, preferred_element_type=jnp.float32)
    out = dot(wh, bh) + (dot(wh, bl) + dot(wl, bh))
    for f in range(FLUX):
        for c in range(per):
            f_ref[c, f * rows : (f + 1) * rows, :] = out[
                c * rows : (c + 1) * rows, f * LANES : (f + 1) * LANES
            ]
    ocean = lax.axis_index("comp") == 0
    even = lax.rem(lax.axis_index("tile"), 2) == 0
    vmix = vmix_ref[...]
    pays = []
    for edge, inner in ((0, 1), (rows - 1, rows - 2)):
        xs = [x_ref[c, pl.ds(edge, levels, stride=rows), :] for c in range(per)]
        left, right = shifted(xs, True), shifted(xs, False)
        pay = []
        for c in range(per):
            s = slice(c * LANES, (c + 1) * LANES)
            x = xs[c]
            xi = x_ref[c, pl.ds(inner, levels, stride=rows), :]
            fe = f_ref[c, pl.ds(edge, FLUX, stride=rows), :]
            k = kappa_ref[edge : edge + 1, s]
            m = jnp.where(ocean, mask_ref[edge : edge + 1, s].astype(jnp.float32), 1.0)
            acc = x + k * (xi + left[c] + right[c] - 4.0 * x)
            for q in range(levels):
                acc = acc + vmix[:, q : q + 1] * x[q : q + 1, :]
            acc = acc + jnp.concatenate([fe, jnp.zeros((levels - FLUX, LANES), jnp.float32)], axis=0)
            pay.append((m * acc, x, m * k))
        pays.append(pay)
    for ref, flag in ((p1_ref, even), (p2_ref, jnp.logical_not(even))):
        for c in range(per):
            a, x, b = [jnp.where(flag, v, u) for u, v in zip(pays[0][c], pays[1][c])]
            ref[c * levels : (c + 1) * levels, :] = a
            ref[(per + c) * levels : (per + c + 1) * levels, :] = x
            ref[2 * per * levels + c : 2 * per * levels + c + 1, :] = b


def step_kernel(
    rows, x0_ref, f_ref, h1_ref, h2_ref, kappa_ref, mask_ref, vmix_ref, basis_ref, gram_ref,
    x_ref, sums_ref, x1_ref, halo_ref,
):
    per = x0_ref.shape[0]
    levels = x0_ref.shape[1] // rows
    vecs = basis_ref.shape[0]
    ocean = lax.axis_index("comp") == 0
    even = lax.rem(lax.axis_index("tile"), 2) == 0
    for side in range(2):
        flag = even if side == 1 else jnp.logical_not(even)

        def take(lo, n):
            return jnp.where(flag, h1_ref[lo : lo + n, :], h2_ref[lo : lo + n, :])

        for c in range(per):
            edge = x0_ref[c, pl.ds(side * (rows - 1), levels, stride=rows), :]
            a = take(c * levels, levels)
            b = take(2 * per * levels + c, 1)
            halo_ref[side, c] = take((per + c) * levels, levels)
            halo_ref[2 + side, c] = a + b * edge
    row = lax.broadcasted_iota(jnp.int32, (rows, LANES), 0)

    def advance(src, dst, base):
        for l in range(levels):
            part = slice(l * rows, (l + 1) * rows)
            xs = [src[c, part, :] for c in range(per)]
            left, right = shifted(xs, True), shifted(xs, False)
            for c in range(per):
                s = slice(c * LANES, (c + 1) * LANES)
                x = xs[c]
                prev = halo_ref[base, c, l : l + 1, :]
                nxt = halo_ref[base + 1, c, l : l + 1, :]
                up = jnp.where(row == 0, prev, pltpu.roll(x, 1, 0))
                down = jnp.where(row == rows - 1, nxt, pltpu.roll(x, rows - 1, 0))
                acc = x + kappa_ref[:, s] * (up + down + left[c] + right[c] - 4.0 * x)
                for q in range(levels):
                    acc = acc + vmix_ref[l, q] * src[c, q * rows : (q + 1) * rows, :]
                if l < FLUX:
                    acc = acc + f_ref[c, part, :]
                mask = jnp.where(ocean, mask_ref[:, s].astype(jnp.float32), 1.0)
                dst[c, part, :] = mask * acc

    advance(x0_ref, x1_ref, 0)
    advance(x1_ref, x_ref, 2)

    def level(l, accs):
        accs = list(accs)
        for c in range(per):
            s = slice(c * LANES, (c + 1) * LANES)
            x = x_ref[c, pl.ds(l * rows, rows), :]
            for i in range(vecs):
                t = x * basis_ref[i, l, :, s].astype(jnp.float32)
                accs[i] = accs[i] + t.reshape(rows // 8, 8, LANES).sum(0)
            accs[vecs] = accs[vecs] + (x * x).reshape(rows // 8, 8, LANES).sum(0)
        return tuple(accs)

    zero = jnp.zeros((8, LANES), jnp.float32)
    accs = lax.fori_loop(0, levels, level, (zero,) * (vecs + 1))
    lane = lax.broadcasted_iota(jnp.int32, (1, LANES), 1)
    line = jnp.zeros((1, LANES), jnp.float32)
    for i in range(vecs + 1):
        tot = jnp.sum(jnp.sum(accs[i], axis=0, keepdims=True), axis=1, keepdims=True)
        line = line + jnp.where(lane == 64 + i, tot, 0.0)
    block = gram_ref[...] + jnp.concatenate([jnp.zeros((1, LANES), jnp.float32), line], axis=0)
    for d in range(sums_ref.shape[0]):
        sums_ref[d] = block


def finish_kernel(rows, total, x_ref, basis_ref, sums_ref, out_ref, coef_ref):
    per = x_ref.shape[0]
    levels = x_ref.shape[1] // rows
    vecs = basis_ref.shape[0]
    sums = jnp.sum(sums_ref[...], axis=0)
    lane = lax.broadcasted_iota(jnp.int32, (1, LANES), 1)
    tail = pltpu.roll(sums[1:2, :], 64, 1)
    coef = jnp.where(lane < vecs, tail, 0.0) / total
    coef_ref[...] = coef[:, :vecs]
    square = jnp.sum(jnp.where(lane == vecs, tail, 0.0), axis=1, keepdims=True)
    splat = [jnp.sum(jnp.where(lane == i, coef, 0.0), axis=1, keepdims=True) for i in range(vecs)]
    quad = jnp.zeros((1, LANES), jnp.float32)
    for i in range(vecs):
        shift = (LANES - 16 * (i % 8)) % LANES
        line = sums[i // 8 : i // 8 + 1, :]
        line = pltpu.roll(line, shift, 1) if shift else line
        quad = quad + splat[i] * jnp.where(lane < vecs, line, 0.0)
    extra = jnp.sum(coef * (quad - 2.0 * total * coef), axis=1, keepdims=True)
    scale = 1.0 / jnp.sqrt((square + extra) / total + 1e-06)
    wide = [jnp.broadcast_to(scale * s, (8, LANES)) for s in splat]
    scale = jnp.broadcast_to(scale, (8, LANES))

    def level(l, carry):
        for c in range(per):
            s = slice(c * LANES, (c + 1) * LANES)
            x = x_ref[c, pl.ds(l * rows, rows), :].reshape(rows // 8, 8, LANES) * scale
            for i in range(vecs):
                b = basis_ref[i, l, :, s].astype(jnp.float32).reshape(rows // 8, 8, LANES)
                x = x - wide[i] * b
            out_ref[pl.ds(l * rows, rows), s] = x.reshape(rows, LANES)
        return carry

    lax.fori_loop(0, levels, level, 0)


def body(state, basis, kappa, vmix, land_mask, send_rows, recv_slots, recv_weights):
    _, levels, rows, cols = state.shape
    vecs = basis.shape[0]
    bands, cap = send_rows.shape[2:]
    blocks, over = recv_slots.shape[2:]
    per = cols // LANES
    comps = lax.axis_size("comp")
    devices = comps * bands
    total = float(levels * rows * cols * devices)
    f32 = jnp.float32
    flat = state.reshape(levels * rows, cols)
    vectors = basis[:, 0]
    kap, vm = kappa[0], vmix[0]

    field = jax.ShapeDtypeStruct((per, levels * rows, LANES), f32)
    bucket, columns = call(
        functools.partial(gather_kernel, rows),
        (jax.ShapeDtypeStruct((bands * FLUX * cap, LANES), f32), field),
        [SMEM, pl.BlockSpec(memory_space=pl.ANY)],
        (VMEM, VMEM),
        scratch=(pltpu.SemaphoreType.DMA((2 * per,)),),
    )(send_rows[0, 0].T, flat)
    moved = lax.all_to_all(bucket.reshape(bands, FLUX * cap, LANES), "tile", 0, 0)

    def by_column(a):
        return a[0, 0].reshape(rows, per, over).transpose(2, 1, 0).reshape(over, blocks)

    matrix, gram = call(
        early_kernel,
        (
            jax.ShapeDtypeStruct((2, blocks, bands * cap), jnp.bfloat16),
            jax.ShapeDtypeStruct((2, LANES), f32),
        ),
        [VMEM] * 3,
        (VMEM, VMEM),
        cost=pl.CostEstimate(flops=10**9, bytes_accessed=4 << 20, transcendentals=0),
    )(by_column(recv_slots), by_column(recv_weights), vectors)

    arrived = lax.ppermute(moved, "comp", [(i, i ^ 1) for i in range(comps)])
    pay = jax.ShapeDtypeStruct((2 * levels * per + per, LANES), f32)
    imported, pay1, pay2 = call(
        functools.partial(regrid_kernel, rows),
        (jax.ShapeDtypeStruct((per, FLUX * rows, LANES), f32), pay, pay),
        [VMEM] * 6,
        (VMEM,) * 3,
    )(arrived, matrix, columns, kap, land_mask, vm)
    pairs1 = [(i, i ^ 1) for i in range(bands)]
    pairs2 = [p for i in range(1, bands - 1, 2) for p in ((i, i + 1), (i + 1, i))]
    got1 = lax.ppermute(pay1, "tile", pairs1)
    got2 = lax.ppermute(pay2, "tile", pairs2)
    x, sums = call(
        functools.partial(step_kernel, rows),
        (field, jax.ShapeDtypeStruct((devices, 2, LANES), f32)),
        [VMEM] * 6 + [SMEM] + [VMEM] * 2,
        (VMEM, VMEM),
        scratch=(
            pltpu.VMEM((per, levels * rows, LANES), f32),
            pltpu.VMEM((4, per, levels, LANES), f32),
        ),
    )(columns, imported, got1, got2, kap, land_mask, vm, vectors, gram)
    sums = lax.all_to_all(sums, ("comp", "tile"), 0, 0)
    direction, coefs = call(
        functools.partial(finish_kernel, rows, total),
        (
            jax.ShapeDtypeStruct((levels * rows, cols), f32),
            jax.ShapeDtypeStruct((1, vecs), f32),
        ),
        [VMEM] * 3,
        (VMEM, VMEM),
    )(x, vectors, sums)
    return direction.reshape(1, levels, rows, cols), coefs.reshape(vecs)


def solution(mesh):
    return jax.shard_map(
        body,
        mesh=mesh,
        in_specs=(
            P("comp", None, "tile", None),
            P(None, "comp", None, "tile", None),
            P("comp", "tile", None),
            P("comp", None, None),
            P("tile", None),
            P("comp", "tile", None, None),
            P("comp", "tile", None, None),
            P("comp", "tile", None, None),
        ),
        out_specs=(P("comp", None, "tile", None), P()),
        check_vma=False,
    )
```

time: 114 us -> 50.5 us (0.44)
  matrix products: 25 us -> 0 us
  starting transfers between devices: 20.9 us -> 1.49 us
  blocking collectives: 44.3 us -> 31.5 us
  local copies, waits for them, and re-layouts: 15.8 us -> 5.47 us
  Pallas kernels: 0 us -> 7.76 us
  other arithmetic: 2.05 us -> 0 us
  between operations: 2.77 us -> 0.73 us
    psum x1 -> x0, blocking collectives: 44.3 us -> none  [body(): lax.psum((local_dots, jnp.sum(vflat * vflat), local_gram), ('comp', 'tile'))]
    all_to_all x0 -> x2, blocking collectives: none -> 31.5 us  [the longest x1 18 us: body(): lax.all_to_all(bucket.reshape(bands, FLUX * cap, LANES), 'tile', 0, 0)]
    dot_general x7 -> x0, matrix products: 25 us -> none  [the longest x1 9.43 us: body(): local_gram = jnp.dot(qmat, qmat.T, preferred_element_type=jnp.float32)]
    ppermute x5 -> x3, starting transfers between devices: 12.7 us -> 1.49 us  [the longest x1 0.83 us: body(): got1 = lax.ppermute(pay1, 'tile', pairs1)]
    all_to_all x1 -> x0, starting transfers between devices: 8.18 us -> none  [body(): lax.all_to_all(bucket, 'tile', split_axis=1, concat_axis=1, tiled=True)]
    pallas_call x0 -> x5, Pallas kernels: none -> 7.76 us  [the longest x1 2.7 us: body(): call(functools.partial(step_kernel, rows), (field, jax.ShapeDtypeStruct((...]
    unnamed x14, local copies, waits for them, and re-layouts: 8.08 us -> 3.63 us
    gather x2 -> x0, local copies, waits for them, and re-layouts: 3.69 us -> none  [the longest x1 2.25 us: body(): picked = flat[:, recv_slots[0, 0]]]
  transfers between devices with their start and end apart: 6 -> 3, of which waited for: 2 -> 1; matrix products, arithmetic and copies ran while one was open for 22% -> 4% of each run, Pallas kernels for 0% -> 3%
where the time goes in v1:
time: 50.5 us; the launch traced here: 50.1 us
  blocking collectives  31.5 us (62%)
  Pallas kernels  7.76 us (15%)
  local copies, waits for them, and re-layouts  5.47 us (11%)
  waiting for transfers between devices  3.16 us (6%)
  starting transfers between devices  1.49 us (3%)
  between operations  0.73 us (1%)
    all_to_all x1, blocking collectives, body(): lax.all_to_all(bucket.reshape(bands, FLUX * cap, LANES), 'tile', 0, 0)  18 us
    all_to_all x1, blocking collectives, body(): sums = lax.all_to_all(sums, ('comp', 'tile'), 0, 0)  13.5 us
    unnamed x14, local copies, waits for them, and re-layouts  3.63 us
    ppermute x1, waiting for transfers between devices, body(): got1 = lax.ppermute(pay1, 'tile', pairs1)  3.16 us
    pallas_call x1, Pallas kernels, body(): call(functools.partial(step_kernel, rows), (field, jax.ShapeDtypeStruct((...  2.7 us
    pallas_call x1, Pallas kernels, body(): call(functools.partial(finish_kernel, rows, total), (jax.ShapeDtypeStruct...  1.85 us
    another operation x2, local copies, waits for them, and re-layouts, by_column(): a[0, 0].reshape(rows, per, over).transpose(2, 1, 0).reshape(over, blocks)  1.54 us
    pallas_call x1, Pallas kernels, body(): call(functools.partial(gather_kernel, rows), (jax.ShapeDtypeStruct((bands...  1.47 us
  transfers between devices with their start and end apart: 3, of which 1 were waited for; matrix products, arithmetic and copies ran while one was open for 4% of the time, Pallas kernels for 3%

profile of v1, /device:TPU:0, one launch (start us, length us, event | category | flops | bytes accessed | tf_op | source)
XLA Modules:
  0.0 50.1 jit_solution(9801894912659443230)
XLA Ops:
  0.6 0.0 copy-start.2
  0.6 1.0 %copy-done.2 = f32[1,8,16,1024]{3,2,1,0:T(8,128)S(1)} copy-done((f32[1,8,16,1024]{3,2,1,0:T(8,128)S(1)}, f32[1,8,16,1024]{3,2,1,0:T(8,128)}, u32[]{:S(2)}) %copy-start.2) | copy-done | bytes 524312
  1.7 0.7 %copy-done.6 = s32[1,1,16,8]{2,3,1,0:T(8,128)S(1)} copy-done((s32[1,1,16,8]{2,3,1,0:T(8,128)S(1)}, s32[1,1,16,8]{2,3,1,0:T(8,128)}, u32[]{:S(2)}) %copy-start.6) | copy-done | bytes 536
  2.4 1.5 %shard_map.95 = (f32[512,128]{1,0:T(8,128)S(1)}, f32[8,128,128]{2,1,0:T(8,128)S(1)}) custom-call(s32[8,16]{1,0:T(8,128)S(1)} %bitcast.25, f32[128,1024]{1,0:T(8,128)S(1)} %bitcast.19), custom_call_target="tpu_custom_call" | custom-call | tf_op jit(solution)/shard_map/pallas_call | solution.py:275
  3.8 18.0 %all_to_all.10 = f32[16,32,128]{2,1,0:T(8,128)S(1)} all-to-all(f32[16,32,128]{2,1,0:T(8,128)S(1)} %bitcast.22), channel_id=1, replica_groups=mesh['comp'=2,'tile'=16] {'tile'}, dimensions={0} | all-to-all | bytes 524288 | tf_op jit(solution)/shard_map/all_to_all | solution.py:282
  21.9 0.0 collective-permute-start
  21.9 0.8 %reshape_squeeze.6 = s32[16,8,4]{1,0,2:T(8,128)S(1)} reshape(s32[1,1,128,4]{2,3,1,0:T(4,128)} %param.14) | data formatting | bytes 4096 | tf_op jit(solution)/shard_map/reshape;squeeze | solution.py:285
  22.6 0.1 copy.12
  22.7 0.1 reshape.24.slots_ref
  22.8 0.8 %reshape_squeeze.7 = f32[16,8,4]{1,0,2:T(8,128)S(1)} reshape(f32[1,1,128,4]{2,3,1,0:T(4,128)} %param.15) | data formatting | bytes 4096 | tf_op jit(solution)/shard_map/reshape;squeeze | solution.py:285
  23.6 0.1 copy.13
  23.6 0.1 reshape.25.weights_ref
  23.7 1.9 %copy-done = bf16[12,1,8,16,1024]{4,3,2,1,0:T(8,128)(2,1)S(1)} copy-done((bf16[12,1,8,16,1024]{4,3,2,1,0:T(8,128)(2,1)S(1)}, bf16[12,1,8,16,1024]{4,3,2,1,0:T(8,128)(2,1)}, u32[]{:S(2)}) %copy-start) | copy-done | bytes 3145752
  25.6 1.4 %shard_map.96 = (bf16[2,128,128]{2,1,0:T(8,128)(2,1)S(1)}, f32[2,128]{1,0:T(2,128)S(1)}) custom-call(s32[4,128]{1,0:T(4,128)S(1)} %reshape.24.slots_ref, f32[4,128]{1,0:T(4,128)S(1)} %reshape.25.weights_ref, bf16[12,8,16,1024]{3,2,1,0:T(8,128)(2,1)S(1)} %bitcast.16), custom_call_target="tpu_custom_call" | custom-call | flops 1000000000 | bytes 4194304 | tf_op jit(solution)/shard_map/pallas_call | solution.py:287
  27.1 0.0 collective-permute-done.buf_ref
  27.1 0.0 copy-done.3
  27.1 0.3 shard_map.97
  27.4 0.8 %collective-permute-start.1 = (f32[136,128]{1,0:T(8,128)S(1)}, f32[136,128]{1,0:T(8,128)S(1)}, u32[]{:S(2)}, u32[]{:S(2)}) collective-permute-start(f32[136,128]{1,0:T(8,128)S(1)} %get-tuple-element.17), channel_id=1, source_target_pairs={{0,1},{1,0},{2,3},{3,2},{4,5},{5,4},{6,7},{7,6},{8,9},{9,8},{10,11... | collective-permute-start | bytes 208904 | tf_op jit(solution)/shard_map/ppermute | solution.py:308
  28.2 0.7 %collective-permute-start.2 = (f32[136,128]{1,0:T(8,128)S(1)}, f32[136,128]{1,0:T(8,128)S(1)}, u32[]{:S(2)}, u32[]{:S(2)}) collective-permute-start(f32[136,128]{1,0:T(8,128)S(1)} %get-tuple-element.18), channel_id=1, source_target_pairs={{1,2},{2,1},{3,4},{4,3},{5,6},{6,5},{7,8},{8,7},{9,10},{10,9},{11,... | collective-permute-start | bytes 208904 | tf_op jit(solution)/shard_map/ppermute | solution.py:309
  28.9 3.2 %collective-permute-done.1.h1_ref = f32[136,128]{1,0:T(8,128)S(1)} collective-permute-done((f32[136,128]{1,0:T(8,128)S(1)}, f32[136,128]{1,0:T(8,128)S(1)}, u32[]{:S(2)}, u32[]{:S(2)}) %collective-permute-start.1) | collective-permute-done | bytes 69664 | tf_op jit(solution)/shard_map/ppermute | solution.py:308
  32.1 0.0 collective-permute-done.2.h2_ref
  32.1 2.7 %shard_map.98 = (f32[8,128,128]{2,1,0:T(8,128)S(1)}, f32[32,2,128]{2,1,0:T(2,128)S(1)}) custom-call(f32[8,128,128]{2,1,0:T(8,128)S(1)} %get-tuple-element.13.x_ref.x0_ref, f32[8,64,128]{2,1,0:T(8,128)S(1)} %get-tuple-element.16.f_ref, f32[136,128]{1,0:T(8,128)S(1)} %collective-permute-done.1.h1_ref, f32[136,128]{1,0:T(8,128)S(1)} %collective-permute-done.2.h2_ref, ...), custom_call_target="tpu_custom_call" | custom-call | tf_op jit(solution)/shard_map/pallas_call | solution.py:310
  34.8 13.5 %all_to_all.11.sums_ref = f32[32,2,128]{2,1,0:T(2,128)S(1)} all-to-all(f32[32,2,128]{2,1,0:T(2,128)S(1)} %get-tuple-element.21), channel_id=1, replica_groups=mesh['comp'=2,'tile'=16] {'comp','tile'}, dimensions={0} | all-to-all | bytes 65536 | tf_op jit(solution)/shard_map/all_to_all | solution.py:320
  48.3 1.8 %shard_map.99 = (f32[128,1024]{1,0:T(8,128)}, f32[1,12]{1,0:T(1,128)}) custom-call(f32[8,128,128]{2,1,0:T(8,128)S(1)} %get-tuple-element.20.x_ref, bf16[12,8,16,1024]{3,2,1,0:T(8,128)(2,1)S(1)} %bitcast.18, f32[32,2,128]{2,1,0:T(2,128)S(1)} %all_to_all.11.sums_ref), custom_call_target="tpu_custom_call" | custom-call | tf_op jit(solution)/shard_map/pallas_call | solution.py:321
  (9 shorter events, 0.0 us)
Async XLA Ops:
  0.6 1.0 %copy-start.2 = (f32[1,8,16,1024]{3,2,1,0:T(8,128)S(1)}, f32[1,8,16,1024]{3,2,1,0:T(8,128)}, u32[]{:S(2)}) copy-start(f32[1,8,16,1024]{3,2,1,0:T(8,128)} %param.8) | copy-start | bytes 1572868
  1.7 0.7 %copy-start.6 = (s32[1,1,16,8]{2,3,1,0:T(8,128)S(1)}, s32[1,1,16,8]{2,3,1,0:T(8,128)}, u32[]{:S(2)}) copy-start(s32[1,1,16,8]{2,3,1,0:T(8,128)} %param.13) | copy-start | bytes 1540
  2.4 24.7 %copy-start.3 = (f32[1,16,1024]{2,1,0:T(8,128)S(1)}, f32[1,16,1024]{2,1,0:T(8,128)}, u32[]{:S(2)}) copy-start(f32[1,16,1024]{2,1,0:T(8,128)} %param.10) | copy-start | bytes 196612
  2.4 24.7 %copy-start.4 = (s32[16,1024]{1,0:T(8,128)S(1)}, s32[16,1024]{1,0:T(8,128)}, u32[]{:S(2)}) copy-start(s32[16,1024]{1,0:T(8,128)} %mask_ref.3) | copy-start | bytes 196612
  2.4 24.7 %copy-start.5 = (f32[1,8,8]{2,1,0:T(8,128)S(1)}, f32[1,8,8]{2,1,0:T(8,128)}, u32[]{:S(2)}) copy-start(f32[1,8,8]{2,1,0:T(8,128)} %param.11) | copy-start | bytes 772
  21.9 5.2 %collective-permute-start = (f32[16,32,128]{2,1,0:T(8,128)S(1)}, f32[16,32,128]{2,1,0:T(8,128)S(1)}, u32[]{:S(2)}, u32[]{:S(2)}) collective-permute-start(f32[16,32,128]{2,1,0:T(8,128)S(1)} %all_to_all.10), channel_id=1, source_target_pairs={{0,16},{16,0},{1,17},{17,1},{2,18},{18,2},{3,19},{19,3},{4,20},{20... | collective-permute-start | bytes 786440 | tf_op jit(solution)/shard_map/ppermute | solution.py:298
  23.7 1.9 %copy-start = (bf16[12,1,8,16,1024]{4,3,2,1,0:T(8,128)(2,1)S(1)}, bf16[12,1,8,16,1024]{4,3,2,1,0:T(8,128)(2,1)}, u32[]{:S(2)}) copy-start(bf16[12,1,8,16,1024]{4,3,2,1,0:T(8,128)(2,1)} %param.9) | copy-start | bytes 9437188
  25.6 6.4 %copy-start.1 = (bf16[12,1,8,16,1024]{4,3,2,1,0:T(8,128)(2,1)S(1)}, bf16[12,1,8,16,1024]{4,3,2,1,0:T(8,128)(2,1)}, u32[]{:S(2)}) copy-start(bf16[12,1,8,16,1024]{4,3,2,1,0:T(8,128)(2,1)} %param.9) | copy-start | bytes 9437188
  27.4 4.7 %collective-permute-start.1 = (f32[136,128]{1,0:T(8,128)S(1)}, f32[136,128]{1,0:T(8,128)S(1)}, u32[]{:S(2)}, u32[]{:S(2)}) collective-permute-start(f32[136,128]{1,0:T(8,128)S(1)} %get-tuple-element.17), channel_id=1, source_target_pairs={{0,1},{1,0},{2,3},{3,2},{4,5},{5,4},{6,7},{7,6},{8,9},{9,8},{10,11... | collective-permute-start | bytes 208904 | tf_op jit(solution)/shard_map/ppermute | solution.py:308
  28.2 3.8 %collective-permute-start.2 = (f32[136,128]{1,0:T(8,128)S(1)}, f32[136,128]{1,0:T(8,128)S(1)}, u32[]{:S(2)}, u32[]{:S(2)}) collective-permute-start(f32[136,128]{1,0:T(8,128)S(1)} %get-tuple-element.18), channel_id=1, source_target_pairs={{1,2},{2,1},{3,4},{4,3},{5,6},{6,5},{7,8},{8,7},{9,10},{10,9},{11,... | collective-permute-start | bytes 208904 | tf_op jit(solution)/shard_map/ppermute | solution.py:309

commit v2 on v1

--- a/solution.py
+++ b/solution.py
@@ -7,8 +7,10 @@
 from jax.experimental.pallas import tpu as pltpu
 from jax.sharding import PartitionSpec as P
 
+
 FLUX = 4
 LANES = 128
+HBM = pl.BlockSpec(memory_space=pltpu.HBM)
 VMEM = pl.BlockSpec(memory_space=pltpu.VMEM)
 SMEM = pl.BlockSpec(memory_space=pltpu.SMEM)
 LIMIT = 24 << 20
@@ -26,15 +28,21 @@
     )
 
 
+def in_hbm(a):
+    return pltpu.with_memory_space_constraint(a, pltpu.HBM)
+
+
 def split(a):
     high = a.astype(jnp.bfloat16)
     return high, (a - high.astype(jnp.float32)).astype(jnp.bfloat16)
 
 
-def gather_kernel(rows, rows_ref, state_ref, out_ref, x_ref, sems):
+def gather_kernel(rows, index_ref, state_ref, out_ref, x_ref, rows_ref, sems):
     cap, bands = rows_ref.shape
     per = x_ref.shape[0]
     top = FLUX * rows
+    index = pltpu.make_async_copy(index_ref, rows_ref, sems.at[2 * per])
+    index.start()
     copies = []
     for part, (lo, hi) in enumerate(((0, top), (top, x_ref.shape[1]))):
         for c in range(per):
@@ -45,6 +53,7 @@
             )
             copy.start()
             copies.append(copy)
+    index.wait()
     for copy in copies[:per]:
         copy.wait()
 
@@ -61,21 +70,18 @@
         copy.wait()
 
 
-def early_kernel(slots_ref, weights_ref, basis_ref, matrix_ref, gram_ref):
-    over, blocks = slots_ref.shape
-    slots = matrix_ref.shape[2]
-    row = lax.broadcasted_iota(jnp.int32, (slots, blocks), 0)
-    mat = jnp.zeros((slots, blocks), jnp.float32)
-    for k in range(over):
-        mat = mat + jnp.where(slots_ref[k : k + 1, :] == row, weights_ref[k : k + 1, :], 0.0)
-    high, low = split(mat.T)
-    matrix_ref[0] = high
-    matrix_ref[1] = low
-
+def gram_kernel(basis_hbm, gram_ref, basis_ref, sems):
     vecs, levels, rows, cols = basis_ref.shape
+    copies = [
+        pltpu.make_async_copy(basis_hbm.at[:, l], basis_ref.at[:, l], sems.at[l])
+        for l in range(levels)
+    ]
+    for copy in copies:
+        copy.start()
     n = vecs * rows
     total = jnp.zeros((n, n), jnp.float32)
     for l in range(levels):
+        copies[l].wait()
         a = basis_ref[:, l].reshape(n, cols)
         total = total + lax.dot_general(
             a, a, (((1,), (1,)), ((), ())), preferred_element_type=jnp.float32
@@ -105,25 +111,22 @@
     return [jnp.where(lane == edge, rolled[(c + step) % n], rolled[c]) for c in range(n)]
 
 
-def regrid_kernel(
-    rows, buf_ref, matrix_ref, x_ref, kappa_ref, mask_ref, vmix_ref, f_ref, p1_ref, p2_ref
+def early_kernel(
+    rows, slots_ref, weights_ref, x_ref, kappa_ref, mask_ref, vmix_ref, matrix_ref, p1_ref, p2_ref
 ):
-    slots = matrix_ref.shape[2]
+    over, blocks = slots_ref.shape
+    slots = matrix_ref.shape[1]
     per = x_ref.shape[0]
     levels = x_ref.shape[1] // rows
-    cap = buf_ref.shape[1] // FLUX
-    wide = jnp.concatenate(
-        [buf_ref[:, f * cap : (f + 1) * cap, :].reshape(slots, LANES) for f in range(FLUX)], axis=1
-    )
-    bh, bl = split(wide)
-    wh, wl = matrix_ref[0], matrix_ref[1]
-    dot = functools.partial(jnp.dot, preferred_element_type=jnp.float32)
-    out = dot(wh, bh) + (dot(wh, bl) + dot(wl, bh))
-    for f in range(FLUX):
-        for c in range(per):
-            f_ref[c, f * rows : (f + 1) * rows, :] = out[
-                c * rows : (c + 1) * rows, f * LANES : (f + 1) * LANES
-            ]
+    row = lax.broadcasted_iota(jnp.int32, (slots, blocks), 0)
+    mat = jnp.zeros((slots, blocks), jnp.float32)
+    for k in range(over):
+        mat = mat + jnp.where(slots_ref[k : k + 1, :] == row, weights_ref[k : k + 1, :], 0.0)
+    b0 = lax.broadcasted_iota(jnp.int32, (blocks, blocks), 0)
+    b1 = lax.broadcasted_iota(jnp.int32, (blocks, blocks), 1)
+    order = jnp.where(lax.rem(b0, rows) * per + lax.div(b0, rows) == b1, 1.0, 0.0)
+    matrix_ref[...] = jnp.dot(order, mat.T, precision=lax.Precision.HIGHEST)
+
     ocean = lax.axis_index("comp") == 0
     even = lax.rem(lax.axis_index("tile"), 2) == 0
     vmix = vmix_ref[...]
@@ -136,13 +139,11 @@
             s = slice(c * LANES, (c + 1) * LANES)
             x = xs[c]
             xi = x_ref[c, pl.ds(inner, levels, stride=rows), :]
-            fe = f_ref[c, pl.ds(edge, FLUX, stride=rows), :]
             k = kappa_ref[edge : edge + 1, s]
             m = jnp.where(ocean, mask_ref[edge : edge + 1, s].astype(jnp.float32), 1.0)
             acc = x + k * (xi + left[c] + right[c] - 4.0 * x)
             for q in range(levels):
                 acc = acc + vmix[:, q : q + 1] * x[q : q + 1, :]
-            acc = acc + jnp.concatenate([fe, jnp.zeros((levels - FLUX, LANES), jnp.float32)], axis=0)
             pay.append((m * acc, x, m * k))
         pays.append(pay)
     for ref, flag in ((p1_ref, even), (p2_ref, jnp.logical_not(even))):
@@ -153,13 +154,61 @@
             ref[2 * per * levels + c : 2 * per * levels + c + 1, :] = b
 
 
-def step_kernel(
-    rows, x0_ref, f_ref, h1_ref, h2_ref, kappa_ref, mask_ref, vmix_ref, basis_ref, gram_ref,
-    x_ref, sums_ref, x1_ref, halo_ref,
+def regrid_kernel(rows, buf_ref, matrix_ref, mask_ref, f_ref, e1_ref, e2_ref):
+    slots = matrix_ref.shape[1]
+    per = f_ref.shape[0]
+    cap = buf_ref.shape[1] // FLUX
+    wide = jnp.concatenate(
+        [buf_ref[:, f * cap : (f + 1) * cap, :].reshape(slots, LANES) for f in range(FLUX)], axis=1
+    )
+    bh, bl = split(wide)
+    wh, wl = split(matrix_ref[...])
+    dot = functools.partial(jnp.dot, preferred_element_type=jnp.float32)
+    out = dot(wh, bh) + (dot(wh, bl) + dot(wl, bh))
+    for f in range(FLUX):
+        for c in range(per):
+            f_ref[c, f * rows : (f + 1) * rows, :] = out[
+                c * rows : (c + 1) * rows, f * LANES : (f + 1) * LANES
+            ]
+    ocean = lax.axis_index("comp") != 0
+    even = lax.rem(lax.axis_index("tile"), 2) == 0
+    for c in range(per):
+        s = slice(c * LANES, (c + 1) * LANES)
+        edges = []
+        for edge in (0, rows - 1):
+            m = jnp.where(ocean, mask_ref[edge : edge + 1, s].astype(jnp.float32), 1.0)
+            edges.append(m * f_ref[c, pl.ds(edge, FLUX, stride=rows), :])
+        e1_ref[c * FLUX : (c + 1) * FLUX, :] = jnp.where(even, edges[1], edges[0])
+        e2_ref[c * FLUX : (c + 1) * FLUX, :] = jnp.where(even, edges[0], edges[1])
+
+
+def fetch_kernel(after_ref, basis_hbm, basis_ref, sems):
+    copies = [
+        pltpu.make_async_copy(basis_hbm.at[i], basis_ref.at[i], sems.at[i])
+        for i in range(basis_ref.shape[0])
+    ]
+    for copy in copies:
+        copy.start()
+    for copy in copies:
+        copy.wait()
+
+
+def stencil(xs, kappa_ref, rows, prev, nxt, row):
+    left, right = shifted(xs, True), shifted(xs, False)
+    out = []
+    for c, x in enumerate(xs):
+        up = jnp.where(row == 0, prev(c), pltpu.roll(x, 1, 0))
+        down = jnp.where(row == rows - 1, nxt(c), pltpu.roll(x, rows - 1, 0))
+        k = kappa_ref[:, c * LANES : (c + 1) * LANES]
+        out.append(k * (up + down + left[c] + right[c] - 4.0 * x))
+    return out
+
+
+def still_kernel(
+    rows, x0_ref, h1_ref, h2_ref, kappa_ref, mask_ref, vmix_ref, x_ref, x1_ref, halo_ref
 ):
     per = x0_ref.shape[0]
     levels = x0_ref.shape[1] // rows
-    vecs = basis_ref.shape[0]
     ocean = lax.axis_index("comp") == 0
     even = lax.rem(lax.axis_index("tile"), 2) == 0
     for side in range(2):
@@ -180,24 +229,62 @@
         for l in range(levels):
             part = slice(l * rows, (l + 1) * rows)
             xs = [src[c, part, :] for c in range(per)]
-            left, right = shifted(xs, True), shifted(xs, False)
+            moved = stencil(
+                xs, kappa_ref, rows,
+                lambda c: halo_ref[base, c, l : l + 1, :],
+                lambda c: halo_ref[base + 1, c, l : l + 1, :],
+                row,
+            )
             for c in range(per):
-                s = slice(c * LANES, (c + 1) * LANES)
-                x = xs[c]
-                prev = halo_ref[base, c, l : l + 1, :]
-                nxt = halo_ref[base + 1, c, l : l + 1, :]
-                up = jnp.where(row == 0, prev, pltpu.roll(x, 1, 0))
-                down = jnp.where(row == rows - 1, nxt, pltpu.roll(x, rows - 1, 0))
-                acc = x + kappa_ref[:, s] * (up + down + left[c] + right[c] - 4.0 * x)
+                acc = xs[c] + moved[c]
                 for q in range(levels):
                     acc = acc + vmix_ref[l, q] * src[c, q * rows : (q + 1) * rows, :]
-                if l < FLUX:
-                    acc = acc + f_ref[c, part, :]
+                s = slice(c * LANES, (c + 1) * LANES)
                 mask = jnp.where(ocean, mask_ref[:, s].astype(jnp.float32), 1.0)
                 dst[c, part, :] = mask * acc
 
     advance(x0_ref, x1_ref, 0)
     advance(x1_ref, x_ref, 2)
+
+
+def step_kernel(
+    rows, still_ref, f_ref, e1_ref, e2_ref, kappa_ref, mask_ref, vmix_ref, basis_ref, gram_ref,
+    x_ref, sums_ref, f1_ref,
+):
+    per = still_ref.shape[0]
+    levels = still_ref.shape[1] // rows
+    vecs = basis_ref.shape[0]
+    ocean = lax.axis_index("comp") == 0
+    even = lax.rem(lax.axis_index("tile"), 2) == 0
+    row = lax.broadcasted_iota(jnp.int32, (rows, LANES), 0)
+
+    def mask(c):
+        m = mask_ref[:, c * LANES : (c + 1) * LANES].astype(jnp.float32)
+        return jnp.where(ocean, m, 1.0)
+
+    for c in range(per):
+        m = mask(c)
+        for f in range(FLUX):
+            part = slice(f * rows, (f + 1) * rows)
+            f1_ref[c, part, :] = m * f_ref[c, part, :]
+    for l in range(levels):
+        part = slice(l * rows, (l + 1) * rows)
+        if l < FLUX:
+            fs = [f1_ref[c, part, :] for c in range(per)]
+
+            def edge(c, flag):
+                i = slice(c * FLUX + l, c * FLUX + l + 1)
+                return jnp.where(flag, e1_ref[i, :], e2_ref[i, :])
+
+            moved = stencil(
+                fs, kappa_ref, rows,
+                lambda c: edge(c, jnp.logical_not(even)), lambda c: edge(c, even), row,
+            )
+        for c in range(per):
+            acc = fs[c] + moved[c] + f_ref[c, part, :] if l < FLUX else 0.0
+            for q in range(FLUX):
+                acc = acc + vmix_ref[l, q] * f1_ref[c, q * rows : (q + 1) * rows, :]
+            x_ref[c, part, :] = still_ref[c, part, :] + mask(c) * acc
 
     def level(l, accs):
         accs = list(accs)
@@ -261,7 +348,7 @@
     _, levels, rows, cols = state.shape
     vecs = basis.shape[0]
     bands, cap = send_rows.shape[2:]
-    blocks, over = recv_slots.shape[2:]
+    blocks, _ = recv_slots.shape[2:]
     per = cols // LANES
     comps = lax.axis_size("comp")
     devices = comps * bands
@@ -272,51 +359,78 @@
     kap, vm = kappa[0], vmix[0]
 
     field = jax.ShapeDtypeStruct((per, levels * rows, LANES), f32)
+    import_field = jax.ShapeDtypeStruct((per, FLUX * rows, LANES), f32)
+    pay = jax.ShapeDtypeStruct((2 * levels * per + per, LANES), f32)
+    fringe = jax.ShapeDtypeStruct((per * FLUX, LANES), f32)
+    pairs1 = [(i, i ^ 1) for i in range(bands)]
+    pairs2 = [p for i in range(1, bands - 1, 2) for p in ((i, i + 1), (i + 1, i))]
+    swap = [(i, i ^ 1) for i in range(comps)]
+
+    def crossed(pairs):
+        return [((c * bands) + i, (c ^ 1) * bands + k) for c in range(comps) for i, k in pairs]
+
     bucket, columns = call(
         functools.partial(gather_kernel, rows),
         (jax.ShapeDtypeStruct((bands * FLUX * cap, LANES), f32), field),
-        [SMEM, pl.BlockSpec(memory_space=pl.ANY)],
+        [HBM, HBM],
         (VMEM, VMEM),
-        scratch=(pltpu.SemaphoreType.DMA((2 * per,)),),
-    )(send_rows[0, 0].T, flat)
+        scratch=(pltpu.SMEM((cap, bands), jnp.int32), pltpu.SemaphoreType.DMA((2 * per + 1,))),
+    )(in_hbm(send_rows[0, 0].T), in_hbm(flat))
     moved = lax.all_to_all(bucket.reshape(bands, FLUX * cap, LANES), "tile", 0, 0)
-
-    def by_column(a):
-        return a[0, 0].reshape(rows, per, over).transpose(2, 1, 0).reshape(over, blocks)
-
-    matrix, gram = call(
-        early_kernel,
-        (
-            jax.ShapeDtypeStruct((2, blocks, bands * cap), jnp.bfloat16),
-            jax.ShapeDtypeStruct((2, LANES), f32),
-        ),
-        [VMEM] * 3,
-        (VMEM, VMEM),
-        cost=pl.CostEstimate(flops=10**9, bytes_accessed=4 << 20, transcendentals=0),
-    )(by_column(recv_slots), by_column(recv_weights), vectors)
-
-    arrived = lax.ppermute(moved, "comp", [(i, i ^ 1) for i in range(comps)])
-    pay = jax.ShapeDtypeStruct((2 * levels * per + per, LANES), f32)
-    imported, pay1, pay2 = call(
-        functools.partial(regrid_kernel, rows),
-        (jax.ShapeDtypeStruct((per, FLUX * rows, LANES), f32), pay, pay),
+    matrix, pay1, pay2 = call(
+        functools.partial(early_kernel, rows),
+        (jax.ShapeDtypeStruct((blocks, bands * cap), f32), pay, pay),
         [VMEM] * 6,
         (VMEM,) * 3,
-    )(arrived, matrix, columns, kap, land_mask, vm)
-    pairs1 = [(i, i ^ 1) for i in range(bands)]
-    pairs2 = [p for i in range(1, bands - 1, 2) for p in ((i, i + 1), (i + 1, i))]
+    )(recv_slots[0, 0].T, recv_weights[0, 0].T, columns, kap, land_mask, vm)
+    matrix = lax.ppermute(matrix, "comp", swap)
     got1 = lax.ppermute(pay1, "tile", pairs1)
     got2 = lax.ppermute(pay2, "tile", pairs2)
+    gram = call(
+        gram_kernel,
+        jax.ShapeDtypeStruct((2, LANES), f32),
+        [HBM],
+        VMEM,
+        scratch=(
+            pltpu.VMEM(vectors.shape, vectors.dtype),
+            pltpu.SemaphoreType.DMA((levels,)),
+        ),
+        cost=pl.CostEstimate(flops=10**9, bytes_accessed=4 << 20, transcendentals=0),
+    )(in_hbm(vectors))
+    still = call(
+        functools.partial(still_kernel, rows),
+        field,
+        [VMEM] * 5 + [SMEM],
+        VMEM,
+        scratch=(
+            pltpu.VMEM((per, levels * rows, LANES), f32),
+            pltpu.VMEM((4, per, levels, LANES), f32),
+        ),
+    )(columns, got1, got2, kap, land_mask, vm)
+
+    foreign, edge1, edge2 = call(
+        functools.partial(regrid_kernel, rows),
+        (import_field, fringe, fringe),
+        [VMEM] * 3,
+        (VMEM,) * 3,
+    )(moved, matrix, land_mask)
+    vectors = call(
+        fetch_kernel,
+        jax.ShapeDtypeStruct(vectors.shape, vectors.dtype),
+        [pl.BlockSpec(memory_space=pl.ANY), HBM],
+        VMEM,
+        scratch=(pltpu.SemaphoreType.DMA((vecs,)),),
+    )(edge1, in_hbm(vectors))
+    imported = lax.ppermute(foreign, "comp", swap)
+    edge1 = lax.ppermute(edge1, ("comp", "tile"), crossed(pairs1))
+    edge2 = lax.ppermute(edge2, ("comp", "tile"), crossed(pairs2))
     x, sums = call(
         functools.partial(step_kernel, rows),
         (field, jax.ShapeDtypeStruct((devices, 2, LANES), f32)),
         [VMEM] * 6 + [SMEM] + [VMEM] * 2,
         (VMEM, VMEM),
-        scratch=(
-            pltpu.VMEM((per, levels * rows, LANES), f32),
-            pltpu.VMEM((4, per, levels, LANES), f32),
-        ),
-    )(columns, imported, got1, got2, kap, land_mask, vm, vectors, gram)
+        scratch=(pltpu.VMEM((per, FLUX * rows, LANES), f32),),
+    )(still, imported, edge1, edge2, kap, land_mask, vm, vectors, gram)
     sums = lax.all_to_all(sums, ("comp", "tile"), 0, 0)
     direction, coefs = call(
         functools.partial(finish_kernel, rows, total),

time: 50.5 us -> 52.9 us (1.048)
  blocking collectives: 31.5 us -> 10.1 us
  starting transfers between devices: 1.49 us -> 17.1 us
  Pallas kernels: 7.76 us -> 13.9 us
  waiting for transfers between devices: 3.16 us -> 5.8 us
  local copies, waits for them, and re-layouts: 5.47 us -> 4.58 us
    all_to_all x1 -> x0, blocking collectives: 18 us -> none  [body(): lax.all_to_all(bucket.reshape(bands, FLUX * cap, LANES), 'tile', 0, 0)]
    all_to_all x0 -> x1, starting transfers between devices: none -> 8.35 us  [body(): lax.all_to_all(bucket.reshape(bands, FLUX * cap, LANES), 'tile', 0, 0)]
    ppermute x1 -> x4, starting transfers between devices: 0.01 us -> 7.26 us  [the longest x1 6.46 us: body(): edge1 = lax.ppermute(edge1, ('comp', 'tile'), crossed(pairs1))]
    pallas_call x2 -> x5, Pallas kernels: 1.74 us -> 7.91 us  [the longest x1 3.61 us: body(): call(gram_kernel, jax.ShapeDtypeStruct((2, LANES), f32), [HBM], VMEM, scr...]
    all_to_all x0 -> x1, waiting for transfers between devices: none -> 4.54 us  [body(): lax.all_to_all(bucket.reshape(bands, FLUX * cap, LANES), 'tile', 0, 0)]
    all_to_all x1, blocking collectives: 13.5 us -> 10.1 us  [body(): sums = lax.all_to_all(sums, ('comp', 'tile'), 0, 0)]
    ppermute x1, waiting for transfers between devices: 3.16 us -> 0.01 us  [body(): got1 = lax.ppermute(pay1, 'tile', pairs1)]
    another operation x2 -> x0, local copies, waits for them, and re-layouts: 1.54 us -> none  [by_column(): a[0, 0].reshape(rows, per, over).transpose(2, 1, 0).reshape(over, blocks)]
  transfers between devices with their start and end apart: 3 -> 7, of which waited for: 1 -> 2; matrix products, arithmetic and copies ran while one was open for 4% -> 0% of each run, Pallas kernels for 3% -> 15%
where the time goes in v2:
time: 52.9 us; the launch traced here: 52.3 us
  starting transfers between devices  17.1 us (32%)
  Pallas kernels  13.9 us (26%)
  blocking collectives  10.1 us (19%)
  waiting for transfers between devices  5.8 us (11%)
  local copies, waits for them, and re-layouts  4.58 us (9%)
  between operations  0.82 us (2%)
    all_to_all x1, blocking collectives, body(): sums = lax.all_to_all(sums, ('comp', 'tile'), 0, 0)  10.1 us
    all_to_all x1, starting transfers between devices, body(): lax.all_to_all(bucket.reshape(bands, FLUX * cap, LANES), 'tile', 0, 0)  8.35 us
    ppermute x1, starting transfers between devices, body(): edge1 = lax.ppermute(edge1, ('comp', 'tile'), crossed(pairs1))  6.46 us
    unnamed x18, local copies, waits for them, and re-layouts  4.58 us
    all_to_all x1, waiting for transfers between devices, body(): lax.all_to_all(bucket.reshape(bands, FLUX * cap, LANES), 'tile', 0, 0)  4.54 us
    pallas_call x1, Pallas kernels, body(): call(gram_kernel, jax.ShapeDtypeStruct((2, LANES), f32), [HBM], VMEM, scr...  3.61 us
    pallas_call x1, Pallas kernels, body(): call(functools.partial(gather_kernel, rows), (jax.ShapeDtypeStruct((bands...  2.37 us
    pallas_call x1, Pallas kernels, body(): call(fetch_kernel, jax.ShapeDtypeStruct(vectors.shape, vectors.dtype), [p...  1.93 us
  transfers between devices with their start and end apart: 7, of which 2 were waited for; matrix products, arithmetic and copies ran while one was open for 0% of the time, Pallas kernels for 15%

profile of v2, /device:TPU:0, one launch (start us, length us, event | category | flops | bytes accessed | tf_op | source)
XLA Modules:
  0.0 52.3 jit_solution(8378588739741264698)
XLA Ops:
  0.7 2.4 %shard_map.95 = (f32[512,128]{1,0:T(8,128)}, f32[8,128,128]{2,1,0:T(8,128)S(1)}) custom-call(s32[8,16]{1,0:T(8,128)} %bitcast.27, f32[128,1024]{1,0:T(8,128)} %bitcast.26), custom_call_target="tpu_custom_call" | custom-call | tf_op jit(solution)/shard_map/pallas_call | solution.py:372
  3.0 8.4 %all-to-all-start = ((f32[16,32,128]{2,1,0:T(8,128)}), f32[16,32,128]{2,1,0:T(8,128)S(1)}, u32[]{:S(2)}, u32[]{:S(2)}) async-start(f32[16,32,128]{2,1,0:T(8,128)} %bitcast.9), calls=%async_computation | async-start | bytes 524288 | tf_op jit(solution)/shard_map/all_to_all | solution.py:379
  11.4 0.8 %copy-done = s32[16,1024]{1,0:T(8,128)S(1)} copy-done((s32[16,1024]{1,0:T(8,128)S(1)}, s32[16,1024]{1,0:T(8,128)}, u32[]{:S(2)}) %copy-start) | copy-done | bytes 65560
  12.3 0.8 %copy-done.3 = f32[1,16,1024]{2,1,0:T(8,128)S(1)} copy-done((f32[1,16,1024]{2,1,0:T(8,128)S(1)}, f32[1,16,1024]{2,1,0:T(8,128)}, u32[]{:S(2)}) %copy-start.3) | copy-done | bytes 65560
  13.1 0.7 %copy-done.5 = f32[1,8,8]{2,1,0:T(8,128)S(1)} copy-done((f32[1,8,8]{2,1,0:T(8,128)S(1)}, f32[1,8,8]{2,1,0:T(8,128)}, u32[]{:S(2)}) %copy-start.5) | copy-done | bytes 280
  13.8 0.7 %copy-done.7 = s32[1,1,128,4]{2,3,1,0:T(4,128)S(1)} copy-done((s32[1,1,128,4]{2,3,1,0:T(4,128)S(1)}, s32[1,1,128,4]{2,3,1,0:T(4,128)}, u32[]{:S(2)}) %copy-start.7) | copy-done | bytes 2072
  14.5 0.7 %copy-done.8 = f32[1,1,128,4]{2,3,1,0:T(4,128)S(1)} copy-done((f32[1,1,128,4]{2,3,1,0:T(4,128)S(1)}, f32[1,1,128,4]{2,3,1,0:T(4,128)}, u32[]{:S(2)}) %copy-start.8) | copy-done | bytes 2072
  15.1 0.3 shard_map.96
  15.4 0.1 collective-permute-start.2
  15.5 1.2 %collective-permute-done.2.matrix_ref = f32[128,128]{1,0:T(8,128)S(1)} collective-permute-done((f32[128,128]{1,0:T(8,128)S(1)}, f32[128,128]{1,0:T(8,128)S(1)}, u32[]{:S(2)}, u32[]{:S(2)}) %collective-permute-start.2) | collective-permute-done | bytes 65568 | tf_op jit(solution)/shard_map/ppermute | solution.py:386
  16.7 4.5 %all-to-all-done.buf_ref = f32[16,32,128]{2,1,0:T(8,128)S(1)} async-done(((f32[16,32,128]{2,1,0:T(8,128)}), f32[16,32,128]{2,1,0:T(8,128)S(1)}, u32[]{:S(2)}, u32[]{:S(2)}) %all-to-all-start) | async-done | bytes 262176 | tf_op jit(solution)/shard_map/all_to_all | solution.py:379
  21.3 0.8 %copy-done.1 = s32[16,1024]{1,0:T(8,128)S(1)} copy-done((s32[16,1024]{1,0:T(8,128)S(1)}, s32[16,1024]{1,0:T(8,128)}, u32[]{:S(2)}) %copy-start.1) | copy-done | bytes 65560
  22.1 0.3 shard_map.98
  22.4 0.1 collective-permute-start.3
  22.5 0.8 %collective-permute-start = (f32[136,128]{1,0:T(8,128)S(1)}, f32[136,128]{1,0:T(8,128)S(1)}, u32[]{:S(2)}, u32[]{:S(2)}) collective-permute-start(f32[136,128]{1,0:T(8,128)S(1)} %get-tuple-element.15), channel_id=1, source_target_pairs={{0,1},{1,0},{2,3},{3,2},{4,5},{5,4},{6,7},{7,6},{8,9},{9,8},{10,11... | collective-permute-start | bytes 208904 | tf_op jit(solution)/shard_map/ppermute | solution.py:387
  23.3 0.7 %collective-permute-start.1 = (f32[136,128]{1,0:T(8,128)S(1)}, f32[136,128]{1,0:T(8,128)S(1)}, u32[]{:S(2)}, u32[]{:S(2)}) collective-permute-start(f32[136,128]{1,0:T(8,128)S(1)} %get-tuple-element.16), channel_id=1, source_target_pairs={{1,2},{2,1},{3,4},{4,3},{5,6},{6,5},{7,8},{8,7},{9,10},{10,9},{11,... | collective-permute-start | bytes 208904 | tf_op jit(solution)/shard_map/ppermute | solution.py:388
  24.0 0.7 %collective-permute-start.5 = (f32[32,128]{1,0:T(8,128)S(1)}, f32[32,128]{1,0:T(8,128)S(1)}, u32[]{:S(2)}, u32[]{:S(2)}) collective-permute-start(f32[32,128]{1,0:T(8,128)S(1)} %get-tuple-element.21), channel_id=1, source_target_pairs={{1,18},{2,17},{3,20},{4,19},{5,22},{6,21},{7,24},{8,23},{9,26},{10... | collective-permute-start | bytes 49160 | tf_op jit(solution)/shard_map/ppermute | solution.py:426
  24.6 6.5 %collective-permute-start.4 = (f32[32,128]{1,0:T(8,128)S(1)}, f32[32,128]{1,0:T(8,128)S(1)}, u32[]{:S(2)}, u32[]{:S(2)}) collective-permute-start(f32[32,128]{1,0:T(8,128)S(1)} %get-tuple-element.20.after_ref), channel_id=1, source_target_pairs={{0,17},{1,16},{2,19},{3,18},{4,21},{5,20},{6,23},{7,22},{8,25},{9,... | collective-permute-start | bytes 49160 | tf_op jit(solution)/shard_map/ppermute | solution.py:425
  31.1 3.6 %shard_map.100.gram_ref = f32[2,128]{1,0:T(2,128)S(1)} custom-call(bf16[12,8,16,1024]{3,2,1,0:T(8,128)(2,1)} %bitcast.24), custom_call_target="tpu_custom_call" | custom-call | flops 1000000000 | bytes 4194304 | tf_op jit(solution)/shard_map/pallas_call | solution.py:389
  34.8 1.8 %shard_map.97.still_ref = f32[8,128,128]{2,1,0:T(8,128)S(1)} custom-call(f32[8,128,128]{2,1,0:T(8,128)S(1)} %get-tuple-element.14.x_ref.x0_ref, f32[136,128]{1,0:T(8,128)S(1)} %collective-permute-done.h1_ref, f32[136,128]{1,0:T(8,128)S(1)} %collective-permute-done.1.h2_ref, f32[16,1024]{1,0:T(8,128)S(1)} %bitcast.17, s32[16,1024]{1,0:T(8,128)S(1)} %copy-done.2, ...), custom_call_target="tpu_custom_call" | custom-call | tf_op jit(solution)/shard_map/pallas_call | solution.py:400
  36.6 1.9 %shard_map.99.basis_ref = bf16[12,8,16,1024]{3,2,1,0:T(8,128)(2,1)S(1)} custom-call(f32[32,128]{1,0:T(8,128)S(1)} %get-tuple-element.20.after_ref, bf16[12,8,16,1024]{3,2,1,0:T(8,128)(2,1)} %bitcast.25), custom_call_target="tpu_custom_call" | custom-call | tf_op jit(solution)/shard_map/pallas_call | solution.py:417
  38.6 1.8 %shard_map.101 = (f32[8,128,128]{2,1,0:T(8,128)S(1)}, f32[32,2,128]{2,1,0:T(2,128)S(1)}) custom-call(f32[8,128,128]{2,1,0:T(8,128)S(1)} %shard_map.97.still_ref, f32[8,64,128]{2,1,0:T(8,128)S(1)} %collective-permute-done.3.f_ref, f32[32,128]{1,0:T(8,128)S(1)} %collective-permute-done.4.e1_ref, f32[32,128]{1,0:T(8,128)S(1)} %collective-permute-done.5.e2_ref, ...), custom_call_target="tpu_custom_call" | custom-call | tf_op jit(solution)/shard_map/pallas_call | solution.py:427
  40.4 10.1 %all_to_all.10.sums_ref = f32[32,2,128]{2,1,0:T(2,128)S(1)} all-to-all(f32[32,2,128]{2,1,0:T(2,128)S(1)} %get-tuple-element.23), channel_id=1, replica_groups=mesh['comp'=2,'tile'=16] {'comp','tile'}, dimensions={0} | all-to-all | bytes 65536 | tf_op jit(solution)/shard_map/all_to_all | solution.py:434
  50.5 1.8 %shard_map.102 = (f32[128,1024]{1,0:T(8,128)}, f32[1,12]{1,0:T(1,128)}) custom-call(f32[8,128,128]{2,1,0:T(8,128)S(1)} %get-tuple-element.22.x_ref, bf16[12,8,16,1024]{3,2,1,0:T(8,128)(2,1)S(1)} %shard_map.99.basis_ref, f32[32,2,128]{2,1,0:T(2,128)S(1)} %all_to_all.10.sums_ref), custom_call_target="tpu_custom_call" | custom-call | tf_op jit(solution)/shard_map/pallas_call | solution.py:435
  (17 shorter events, 0.0 us)
Async XLA Ops:
  0.6 34.1 %copy-start.2 = (s32[16,1024]{1,0:T(8,128)S(1)}, s32[16,1024]{1,0:T(8,128)}, u32[]{:S(2)}) copy-start(s32[16,1024]{1,0:T(8,128)} %mask_ref.7) | copy-start | bytes 196612
  0.6 34.1 %copy-start.6 = (f32[1,8,8]{2,1,0:T(8,128)S(1)}, f32[1,8,8]{2,1,0:T(8,128)}, u32[]{:S(2)}) copy-start(f32[1,8,8]{2,1,0:T(8,128)} %param.11) | copy-start | bytes 772
  0.7 34.1 %copy-start.4 = (f32[1,16,1024]{2,1,0:T(8,128)S(1)}, f32[1,16,1024]{2,1,0:T(8,128)}, u32[]{:S(2)}) copy-start(f32[1,16,1024]{2,1,0:T(8,128)} %param.10) | copy-start | bytes 196612
  3.0 18.2 %all-to-all-start = ((f32[16,32,128]{2,1,0:T(8,128)}), f32[16,32,128]{2,1,0:T(8,128)S(1)}, u32[]{:S(2)}, u32[]{:S(2)}) async-start(f32[16,32,128]{2,1,0:T(8,128)} %bitcast.9), calls=%async_computation | async-start | bytes 524288 | tf_op jit(solution)/shard_map/all_to_all | solution.py:379
  11.4 0.8 %copy-start = (s32[16,1024]{1,0:T(8,128)S(1)}, s32[16,1024]{1,0:T(8,128)}, u32[]{:S(2)}) copy-start(s32[16,1024]{1,0:T(8,128)} %mask_ref.7) | copy-start | bytes 196612
  12.3 0.8 %copy-start.3 = (f32[1,16,1024]{2,1,0:T(8,128)S(1)}, f32[1,16,1024]{2,1,0:T(8,128)}, u32[]{:S(2)}) copy-start(f32[1,16,1024]{2,1,0:T(8,128)} %param.10) | copy-start | bytes 196612
  13.1 0.7 %copy-start.5 = (f32[1,8,8]{2,1,0:T(8,128)S(1)}, f32[1,8,8]{2,1,0:T(8,128)}, u32[]{:S(2)}) copy-start(f32[1,8,8]{2,1,0:T(8,128)} %param.11) | copy-start | bytes 772
  13.8 0.7 %copy-start.7 = (s32[1,1,128,4]{2,3,1,0:T(4,128)S(1)}, s32[1,1,128,4]{2,3,1,0:T(4,128)}, u32[]{:S(2)}) copy-start(s32[1,1,128,4]{2,3,1,0:T(4,128)} %param.14) | copy-start | bytes 6148
  14.5 0.7 %copy-start.8 = (f32[1,1,128,4]{2,3,1,0:T(4,128)S(1)}, f32[1,1,128,4]{2,3,1,0:T(4,128)}, u32[]{:S(2)}) copy-start(f32[1,1,128,4]{2,3,1,0:T(4,128)} %param.15) | copy-start | bytes 6148
  15.4 1.3 %collective-permute-start.2 = (f32[128,128]{1,0:T(8,128)S(1)}, f32[128,128]{1,0:T(8,128)S(1)}, u32[]{:S(2)}, u32[]{:S(2)}) collective-permute-start(f32[128,128]{1,0:T(8,128)S(1)} %get-tuple-element.18), channel_id=1, source_target_pairs={{0,16},{16,0},{1,17},{17,1},{2,18},{18,2},{3,19},{19,3},{4,20},{20... | collective-permute-start | bytes 196616 | tf_op jit(solution)/shard_map/ppermute | solution.py:386
  21.3 0.8 %copy-start.1 = (s32[16,1024]{1,0:T(8,128)S(1)}, s32[16,1024]{1,0:T(8,128)}, u32[]{:S(2)}) copy-start(s32[16,1024]{1,0:T(8,128)} %mask_ref.7) | copy-start | bytes 196612
  22.4 16.2 %collective-permute-start.3 = (f32[8,64,128]{2,1,0:T(8,128)S(1)}, f32[8,64,128]{2,1,0:T(8,128)S(1)}, u32[]{:S(2)}, u32[]{:S(2)}) collective-permute-start(f32[8,64,128]{2,1,0:T(8,128)S(1)} %get-tuple-element.19), channel_id=1, source_target_pairs={{0,16},{16,0},{1,17},{17,1},{2,18},{18,2},{3,19},{19,3},{4,20},{20... | collective-permute-start | bytes 786440 | tf_op jit(solution)/shard_map/ppermute | solution.py:424
  22.5 12.2 %collective-permute-start = (f32[136,128]{1,0:T(8,128)S(1)}, f32[136,128]{1,0:T(8,128)S(1)}, u32[]{:S(2)}, u32[]{:S(2)}) collective-permute-start(f32[136,128]{1,0:T(8,128)S(1)} %get-tuple-element.15), channel_id=1, source_target_pairs={{0,1},{1,0},{2,3},{3,2},{4,5},{5,4},{6,7},{7,6},{8,9},{9,8},{10,11... | collective-permute-start | bytes 208904 | tf_op jit(solution)/shard_map/ppermute | solution.py:387
  23.3 11.4 %collective-permute-start.1 = (f32[136,128]{1,0:T(8,128)S(1)}, f32[136,128]{1,0:T(8,128)S(1)}, u32[]{:S(2)}, u32[]{:S(2)}) collective-permute-start(f32[136,128]{1,0:T(8,128)S(1)} %get-tuple-element.16), channel_id=1, source_target_pairs={{1,2},{2,1},{3,4},{4,3},{5,6},{6,5},{7,8},{8,7},{9,10},{10,9},{11,... | collective-permute-start | bytes 208904 | tf_op jit(solution)/shard_map/ppermute | solution.py:388
  24.0 14.6 %collective-permute-start.5 = (f32[32,128]{1,0:T(8,128)S(1)}, f32[32,128]{1,0:T(8,128)S(1)}, u32[]{:S(2)}, u32[]{:S(2)}) collective-permute-start(f32[32,128]{1,0:T(8,128)S(1)} %get-tuple-element.21), channel_id=1, source_target_pairs={{1,18},{2,17},{3,20},{4,19},{5,22},{6,21},{7,24},{8,23},{9,26},{10... | collective-permute-start | bytes 49160 | tf_op jit(solution)/shard_map/ppermute | solution.py:426
  24.6 13.9 %collective-permute-start.4 = (f32[32,128]{1,0:T(8,128)S(1)}, f32[32,128]{1,0:T(8,128)S(1)}, u32[]{:S(2)}, u32[]{:S(2)}) collective-permute-start(f32[32,128]{1,0:T(8,128)S(1)} %get-tuple-element.20.after_ref), channel_id=1, source_target_pairs={{0,17},{1,16},{2,19},{3,18},{4,21},{5,20},{6,23},{7,22},{8,25},{9,... | collective-permute-start | bytes 49160 | tf_op jit(solution)/shard_map/ppermute | solution.py:425

commit v3 on v2

--- a/solution.py
+++ b/solution.py
@@ -12,7 +12,6 @@
 LANES = 128
 HBM = pl.BlockSpec(memory_space=pltpu.HBM)
 VMEM = pl.BlockSpec(memory_space=pltpu.VMEM)
-SMEM = pl.BlockSpec(memory_space=pltpu.SMEM)
 LIMIT = 24 << 20
 
 
@@ -37,7 +36,17 @@
     return high, (a - high.astype(jnp.float32)).astype(jnp.bfloat16)
 
 
-def gather_kernel(rows, index_ref, state_ref, out_ref, x_ref, rows_ref, sems):
+def block_place(b, per):
+    if per & (per - 1) == 0:
+        bits = per.bit_length() - 1
+        return lax.shift_right_logical(b, bits), lax.bitwise_and(b, per - 1)
+    return lax.div(b, per), lax.rem(b, per)
+
+
+def gather_kernel(rows, index_ref, state_ref, *refs):
+    small = (len(refs) - 4) // 2
+    sides, out_ref, x_ref = refs[:small], refs[small], refs[small + 1]
+    side_outs, (rows_ref, sems) = refs[small + 2 : 2 * small + 2], refs[2 * small + 2 :]
     cap, bands = rows_ref.shape
     per = x_ref.shape[0]
     top = FLUX * rows
@@ -46,42 +55,48 @@
     copies = []
     for part, (lo, hi) in enumerate(((0, top), (top, x_ref.shape[1]))):
         for c in range(per):
-            copy = pltpu.make_async_copy(
-                state_ref.at[lo:hi, c * LANES : (c + 1) * LANES],
-                x_ref.at[c, lo:hi, :],
-                sems.at[part * per + c],
+            copies.append(
+                pltpu.make_async_copy(
+                    state_ref.at[lo:hi, c * LANES : (c + 1) * LANES],
+                    x_ref.at[c, lo:hi, :],
+                    sems.at[part * per + c],
+                )
             )
-            copy.start()
-            copies.append(copy)
+    for k, (src, dst) in enumerate(zip(sides, side_outs)):
+        copies.append(pltpu.make_async_copy(src, dst, sems.at[2 * per + 1 + k]))
+    for copy in copies:
+        copy.start()
     index.wait()
     for copy in copies[:per]:
         copy.wait()
 
     def band(d, carry):
         for j in range(cap):
-            b = rows_ref[j, d]
-            r = lax.div(b, per)
-            piece = x_ref[lax.rem(b, per), pl.ds(r, FLUX, stride=rows), :]
+            r, c = block_place(rows_ref[j, d], per)
+            piece = x_ref[c, pl.ds(r, FLUX, stride=rows), :]
             out_ref[pl.ds(d * (cap * FLUX) + j, FLUX, stride=cap), :] = piece
         return carry
 
-    lax.fori_loop(0, bands, band, 0)
+    lax.fori_loop(0, bands, band, 0, unroll=2)
     for copy in copies[per:]:
         copy.wait()
 
 
 def gram_kernel(basis_hbm, gram_ref, basis_ref, sems):
     vecs, levels, rows, cols = basis_ref.shape
+    ahead = 3
     copies = [
         pltpu.make_async_copy(basis_hbm.at[:, l], basis_ref.at[:, l], sems.at[l])
         for l in range(levels)
     ]
-    for copy in copies:
+    for copy in copies[:ahead]:
         copy.start()
     n = vecs * rows
     total = jnp.zeros((n, n), jnp.float32)
     for l in range(levels):
         copies[l].wait()
+        if l + ahead < levels:
+            copies[l + ahead].start()
         a = basis_ref[:, l].reshape(n, cols)
         total = total + lax.dot_general(
             a, a, (((1,), (1,)), ((), ())), preferred_element_type=jnp.float32
@@ -112,7 +127,8 @@
 
 
 def early_kernel(
-    rows, slots_ref, weights_ref, x_ref, kappa_ref, mask_ref, vmix_ref, matrix_ref, p1_ref, p2_ref
+    rows, slots_ref, weights_ref, x_ref, kappa_ref, mask_ref, vmix_ref,
+    matrix_ref, p1_ref, p2_ref, table_ref,
 ):
     over, blocks = slots_ref.shape
     slots = matrix_ref.shape[1]
@@ -130,6 +146,11 @@
     ocean = lax.axis_index("comp") == 0
     even = lax.rem(lax.axis_index("tile"), 2) == 0
     vmix = vmix_ref[...]
+    d0 = lax.broadcasted_iota(jnp.int32, (levels, levels), 0)
+    d1 = lax.broadcasted_iota(jnp.int32, (levels, levels), 1)
+    for l in range(levels):
+        column = jnp.sum(jnp.where(d0 == d1, vmix[l : l + 1, :], 0.0), axis=1, keepdims=True)
+        table_ref[l * levels : (l + 1) * levels, :] = jnp.broadcast_to(column, (levels, LANES))
     pays = []
     for edge, inner in ((0, 1), (rows - 1, rows - 2)):
         xs = [x_ref[c, pl.ds(edge, levels, stride=rows), :] for c in range(per)]
@@ -154,7 +175,7 @@
             ref[2 * per * levels + c : 2 * per * levels + c + 1, :] = b
 
 
-def regrid_kernel(rows, buf_ref, matrix_ref, mask_ref, f_ref, e1_ref, e2_ref):
+def regrid_kernel(rows, after1_ref, after2_ref, buf_ref, matrix_ref, mask_ref, f_ref, e1_ref, e2_ref):
     slots = matrix_ref.shape[1]
     per = f_ref.shape[0]
     cap = buf_ref.shape[1] // FLUX
@@ -182,17 +203,6 @@
         e2_ref[c * FLUX : (c + 1) * FLUX, :] = jnp.where(even, edges[0], edges[1])
 
 
-def fetch_kernel(after_ref, basis_hbm, basis_ref, sems):
-    copies = [
-        pltpu.make_async_copy(basis_hbm.at[i], basis_ref.at[i], sems.at[i])
-        for i in range(basis_ref.shape[0])
-    ]
-    for copy in copies:
-        copy.start()
-    for copy in copies:
-        copy.wait()
-
-
 def stencil(xs, kappa_ref, rows, prev, nxt, row):
     left, right = shifted(xs, True), shifted(xs, False)
     out = []
@@ -205,8 +215,15 @@
 
 
 def still_kernel(
-    rows, x0_ref, h1_ref, h2_ref, kappa_ref, mask_ref, vmix_ref, x_ref, x1_ref, halo_ref
+    rows, after_ref, basis_hbm, x0_ref, h1_ref, h2_ref, kappa_ref, mask_ref, table_ref,
+    x_ref, basis_ref, x1_ref, halo_ref, sems,
 ):
+    copies = [
+        pltpu.make_async_copy(basis_hbm.at[i], basis_ref.at[i], sems.at[i])
+        for i in range(basis_ref.shape[0])
+    ]
+    for copy in copies:
+        copy.start()
     per = x0_ref.shape[0]
     levels = x0_ref.shape[1] // rows
     ocean = lax.axis_index("comp") == 0
@@ -238,17 +255,20 @@
             for c in range(per):
                 acc = xs[c] + moved[c]
                 for q in range(levels):
-                    acc = acc + vmix_ref[l, q] * src[c, q * rows : (q + 1) * rows, :]
+                    v = table_ref[l * levels + q : l * levels + q + 1, :]
+                    acc = acc + v * src[c, q * rows : (q + 1) * rows, :]
                 s = slice(c * LANES, (c + 1) * LANES)
                 mask = jnp.where(ocean, mask_ref[:, s].astype(jnp.float32), 1.0)
                 dst[c, part, :] = mask * acc
 
     advance(x0_ref, x1_ref, 0)
     advance(x1_ref, x_ref, 2)
+    for copy in copies:
+        copy.wait()
 
 
 def step_kernel(
-    rows, still_ref, f_ref, e1_ref, e2_ref, kappa_ref, mask_ref, vmix_ref, basis_ref, gram_ref,
+    rows, still_ref, f_ref, e1_ref, e2_ref, kappa_ref, mask_ref, table_ref, basis_ref, gram_ref,
     x_ref, sums_ref, f1_ref,
 ):
     per = still_ref.shape[0]
@@ -283,7 +303,8 @@
         for c in range(per):
             acc = fs[c] + moved[c] + f_ref[c, part, :] if l < FLUX else 0.0
             for q in range(FLUX):
-                acc = acc + vmix_ref[l, q] * f1_ref[c, q * rows : (q + 1) * rows, :]
+                v = table_ref[l * levels + q : l * levels + q + 1, :]
+                acc = acc + v * f1_ref[c, q * rows : (q + 1) * rows, :]
             x_ref[c, part, :] = still_ref[c, part, :] + mask(c) * acc
 
     def level(l, accs):
@@ -309,7 +330,7 @@
         sums_ref[d] = block
 
 
-def finish_kernel(rows, total, x_ref, basis_ref, sums_ref, out_ref, coef_ref):
+def finish_kernel(rows, total, x_ref, basis_ref, sums_ref, out_hbm, coef_ref, out_ref, sems):
     per = x_ref.shape[0]
     levels = x_ref.shape[1] // rows
     vecs = basis_ref.shape[0]
@@ -331,6 +352,10 @@
     wide = [jnp.broadcast_to(scale * s, (8, LANES)) for s in splat]
     scale = jnp.broadcast_to(scale, (8, LANES))
 
+    def put(l):
+        part = pl.ds(pl.multiple_of(l * rows, rows), rows)
+        return pltpu.make_async_copy(out_ref.at[part, :], out_hbm.at[part, :], sems.at[l])
+
     def level(l, carry):
         for c in range(per):
             s = slice(c * LANES, (c + 1) * LANES)
@@ -339,9 +364,12 @@
                 b = basis_ref[i, l, :, s].astype(jnp.float32).reshape(rows // 8, 8, LANES)
                 x = x - wide[i] * b
             out_ref[pl.ds(l * rows, rows), s] = x.reshape(rows, LANES)
+        put(l).start()
         return carry
 
     lax.fori_loop(0, levels, level, 0)
+    for l in range(levels):
+        put(l).wait()
 
 
 def body(state, basis, kappa, vmix, land_mask, send_rows, recv_slots, recv_weights):
@@ -369,20 +397,30 @@
     def crossed(pairs):
         return [((c * bands) + i, (c ^ 1) * bands + k) for c in range(comps) for i, k in pairs]
 
-    bucket, columns = call(
+    sides = (kap, land_mask, recv_slots[0, 0].T, recv_weights[0, 0].T, vm)
+    bucket, columns, kap, land_mask, slots, weights, vm = call(
         functools.partial(gather_kernel, rows),
-        (jax.ShapeDtypeStruct((bands * FLUX * cap, LANES), f32), field),
-        [HBM, HBM],
-        (VMEM, VMEM),
-        scratch=(pltpu.SMEM((cap, bands), jnp.int32), pltpu.SemaphoreType.DMA((2 * per + 1,))),
-    )(in_hbm(send_rows[0, 0].T), in_hbm(flat))
+        (jax.ShapeDtypeStruct((bands * FLUX * cap, LANES), f32), field)
+        + tuple(jax.ShapeDtypeStruct(a.shape, a.dtype) for a in sides),
+        [HBM] * (2 + len(sides)),
+        (VMEM,) * (2 + len(sides)),
+        scratch=(
+            pltpu.SMEM((cap, bands), jnp.int32),
+            pltpu.SemaphoreType.DMA((2 * per + 1 + len(sides),)),
+        ),
+    )(*[in_hbm(a) for a in (send_rows[0, 0].T, flat) + sides])
     moved = lax.all_to_all(bucket.reshape(bands, FLUX * cap, LANES), "tile", 0, 0)
-    matrix, pay1, pay2 = call(
+    matrix, pay1, pay2, table = call(
         functools.partial(early_kernel, rows),
-        (jax.ShapeDtypeStruct((blocks, bands * cap), f32), pay, pay),
+        (
+            jax.ShapeDtypeStruct((blocks, bands * cap), f32),
+            pay,
+            pay,
+            jax.ShapeDtypeStruct((levels * levels, LANES), f32),
+        ),
         [VMEM] * 6,
-        (VMEM,) * 3,
-    )(recv_slots[0, 0].T, recv_weights[0, 0].T, columns, kap, land_mask, vm)
+        (VMEM,) * 4,
+    )(slots, weights, columns, kap, land_mask, vm)
     matrix = lax.ppermute(matrix, "comp", swap)
     got1 = lax.ppermute(pay1, "tile", pairs1)
     got2 = lax.ppermute(pay2, "tile", pairs2)
@@ -397,40 +435,33 @@
         ),
         cost=pl.CostEstimate(flops=10**9, bytes_accessed=4 << 20, transcendentals=0),
     )(in_hbm(vectors))
-    still = call(
+    foreign, edge1, edge2 = call(
+        functools.partial(regrid_kernel, rows),
+        (import_field, fringe, fringe),
+        [pl.BlockSpec(memory_space=pl.ANY)] * 2 + [VMEM] * 3,
+        (VMEM,) * 3,
+    )(got1, got2, moved, matrix, land_mask)
+    still, vectors = call(
         functools.partial(still_kernel, rows),
-        field,
-        [VMEM] * 5 + [SMEM],
-        VMEM,
+        (field, jax.ShapeDtypeStruct(vectors.shape, vectors.dtype)),
+        [pl.BlockSpec(memory_space=pl.ANY), HBM] + [VMEM] * 6,
+        (VMEM, VMEM),
         scratch=(
             pltpu.VMEM((per, levels * rows, LANES), f32),
             pltpu.VMEM((4, per, levels, LANES), f32),
-        ),
-    )(columns, got1, got2, kap, land_mask, vm)
-
-    foreign, edge1, edge2 = call(
-        functools.partial(regrid_kernel, rows),
-        (import_field, fringe, fringe),
-        [VMEM] * 3,
-        (VMEM,) * 3,
-    )(moved, matrix, land_mask)
-    vectors = call(
-        fetch_kernel,
-        jax.ShapeDtypeStruct(vectors.shape, vectors.dtype),
-        [pl.BlockSpec(memory_space=pl.ANY), HBM],
-        VMEM,
-        scratch=(pltpu.SemaphoreType.DMA((vecs,)),),
-    )(edge1, in_hbm(vectors))
+            pltpu.SemaphoreType.DMA((vecs,)),
+        ),
+    )(edge1, in_hbm(vectors), columns, got1, got2, kap, land_mask, table)
     imported = lax.ppermute(foreign, "comp", swap)
     edge1 = lax.ppermute(edge1, ("comp", "tile"), crossed(pairs1))
     edge2 = lax.ppermute(edge2, ("comp", "tile"), crossed(pairs2))
     x, sums = call(
         functools.partial(step_kernel, rows),
         (field, jax.ShapeDtypeStruct((devices, 2, LANES), f32)),
-        [VMEM] * 6 + [SMEM] + [VMEM] * 2,
+        [VMEM] * 9,
         (VMEM, VMEM),
         scratch=(pltpu.VMEM((per, FLUX * rows, LANES), f32),),
-    )(still, imported, edge1, edge2, kap, land_mask, vm, vectors, gram)
+    )(still, imported, edge1, edge2, kap, land_mask, table, vectors, gram)
     sums = lax.all_to_all(sums, ("comp", "tile"), 0, 0)
     direction, coefs = call(
         functools.partial(finish_kernel, rows, total),
@@ -439,7 +470,11 @@
             jax.ShapeDtypeStruct((1, vecs), f32),
         ),
         [VMEM] * 3,
-        (VMEM, VMEM),
+        (HBM, VMEM),
+        scratch=(
+            pltpu.VMEM((levels * rows, cols), f32),
+            pltpu.SemaphoreType.DMA((levels,)),
+        ),
     )(x, vectors, sums)
     return direction.reshape(1, levels, rows, cols), coefs.reshape(vecs)
 

time: 52.9 us -> 47.7 us (0.902)
  local copies, waits for them, and re-layouts: 4.58 us -> 0 us
  starting transfers between devices: 17.1 us -> 12.7 us
  blocking collectives: 10.1 us -> 14.2 us
  waiting for transfers between devices: 5.8 us -> 6.85 us
  Pallas kernels: 13.9 us -> 12.9 us
    ppermute x1, starting transfers between devices: 6.46 us -> 0.87 us  [body(): edge1 = lax.ppermute(edge1, ('comp', 'tile'), crossed(pairs1))]
    unnamed x18 -> x0, local copies, waits for them, and re-layouts: 4.58 us -> none
    all_to_all x1, blocking collectives: 10.1 us -> 14.2 us  [body(): sums = lax.all_to_all(sums, ('comp', 'tile'), 0, 0)]
    pallas_call x2 -> x1, Pallas kernels: 3.77 us -> 2.6 us  [body(): call(functools.partial(still_kernel, rows), (field, jax.ShapeDtypeStruct(...]
    ppermute x1, starting transfers between devices: 0.83 us -> 1.99 us  [body(): got1 = lax.ppermute(pay1, 'tile', pairs1)]
    ppermute x1, waiting for transfers between devices: 0.01 us -> 0.99 us  [body(): got1 = lax.ppermute(pay1, 'tile', pairs1)]
    pallas_call x1, Pallas kernels: 1.81 us -> 1.21 us  [body(): call(functools.partial(step_kernel, rows), (field, jax.ShapeDtypeStruct((...]
  transfers between devices with their start and end apart: 7 -> 7, of which waited for: 2 -> 3; matrix products, arithmetic and copies ran while one was open for 0% -> 0% of each run, Pallas kernels for 15% -> 15%
where the time goes in v3:
time: 47.7 us; the launch traced here: 47.3 us
  blocking collectives  14.2 us (30%)
  Pallas kernels  12.9 us (27%)
  starting transfers between devices  12.7 us (27%)
  waiting for transfers between devices  6.85 us (14%)
  between operations  0.74 us (2%)
    all_to_all x1, blocking collectives, body(): sums = lax.all_to_all(sums, ('comp', 'tile'), 0, 0)  14.2 us
    all_to_all x1, starting transfers between devices, body(): lax.all_to_all(bucket.reshape(bands, FLUX * cap, LANES), 'tile', 0, 0)  8.35 us
    all_to_all x1, waiting for transfers between devices, body(): lax.all_to_all(bucket.reshape(bands, FLUX * cap, LANES), 'tile', 0, 0)  4.61 us
    pallas_call x1, Pallas kernels, body(): call(gram_kernel, jax.ShapeDtypeStruct((2, LANES), f32), [HBM], VMEM, scr...  4.13 us
    pallas_call x1, Pallas kernels, body(): call(functools.partial(still_kernel, rows), (field, jax.ShapeDtypeStruct(...  2.6 us
    pallas_call x1, Pallas kernels, body(): call(functools.partial(finish_kernel, rows, total), (jax.ShapeDtypeStruct...  2.27 us
    pallas_call x1, Pallas kernels, body(): call(functools.partial(gather_kernel, rows), (jax.ShapeDtypeStruct((bands...  2.12 us
    ppermute x1, starting transfers between devices, body(): got1 = lax.ppermute(pay1, 'tile', pairs1)  1.99 us
  transfers between devices with their start and end apart: 7, of which 3 were waited for; matrix products, arithmetic and copies ran while one was open for 0% of the time, Pallas kernels for 15%

profile of v3, /device:TPU:0, one launch (start us, length us, event | category | flops | bytes accessed | tf_op | source)
XLA Modules:
  0.0 47.3 jit_solution(16430966363706413700)
XLA Ops:
  0.6 2.1 %shard_map.95 = (f32[512,128]{1,0:T(8,128)}, f32[8,128,128]{2,1,0:T(8,128)S(1)}, f32[16,1024]{1,0:T(8,128)S(1)}, s32[16,1024]{1,0:T(8,128)S(1)}, s32[4,128]{1,0:...) custom-call(s32[8,16]{1,0:T(8,128)} %bitcast.20, f32[128,1024]{1,0:T(8,128)} %bitcast.18, f32[16,1024]{1,0:T(8,128)} %bitcast.19, ...), custom_call_target="tpu_custom_call" | custom-call | tf_op jit(solution)/shard_map/pallas_call | solution.py:401
  2.8 8.4 %all-to-all-start = ((f32[16,32,128]{2,1,0:T(8,128)}), f32[16,32,128]{2,1,0:T(8,128)S(1)}, u32[]{:S(2)}, u32[]{:S(2)}) async-start(f32[16,32,128]{2,1,0:T(8,128)} %bitcast.9), calls=%async_computation | async-start | bytes 524288 | tf_op jit(solution)/shard_map/all_to_all | solution.py:412
  11.1 0.3 shard_map.96
  11.4 2.0 %collective-permute-start = (f32[136,128]{1,0:T(8,128)S(1)}, f32[136,128]{1,0:T(8,128)S(1)}, u32[]{:S(2)}, u32[]{:S(2)}) collective-permute-start(f32[136,128]{1,0:T(8,128)S(1)} %get-tuple-element.28), channel_id=1, source_target_pairs={{0,1},{1,0},{2,3},{3,2},{4,5},{5,4},{6,7},{7,6},{8,9},{9,8},{10,11... | collective-permute-start | bytes 208904 | tf_op jit(solution)/shard_map/ppermute | solution.py:425
  13.4 0.7 %collective-permute-start.1 = (f32[136,128]{1,0:T(8,128)S(1)}, f32[136,128]{1,0:T(8,128)S(1)}, u32[]{:S(2)}, u32[]{:S(2)}) collective-permute-start(f32[136,128]{1,0:T(8,128)S(1)} %get-tuple-element.29), channel_id=1, source_target_pairs={{1,2},{2,1},{3,4},{4,3},{5,6},{6,5},{7,8},{8,7},{9,10},{10,9},{11,... | collective-permute-start | bytes 208904 | tf_op jit(solution)/shard_map/ppermute | solution.py:426
  14.1 0.1 collective-permute-start.2
  14.1 1.2 %collective-permute-done.2.matrix_ref = f32[128,128]{1,0:T(8,128)S(1)} collective-permute-done((f32[128,128]{1,0:T(8,128)S(1)}, f32[128,128]{1,0:T(8,128)S(1)}, u32[]{:S(2)}, u32[]{:S(2)}) %collective-permute-start.2) | collective-permute-done | bytes 65568 | tf_op jit(solution)/shard_map/ppermute | solution.py:424
  15.4 1.0 %collective-permute-done.after1_ref.h1_ref = f32[136,128]{1,0:T(8,128)S(1)} collective-permute-done((f32[136,128]{1,0:T(8,128)S(1)}, f32[136,128]{1,0:T(8,128)S(1)}, u32[]{:S(2)}, u32[]{:S(2)}) %collective-permute-start) | collective-permute-done | bytes 69664 | tf_op jit(solution)/shard_map/ppermute | solution.py:425
  16.4 0.0 collective-permute-done.1.after2_ref.h2_ref
  16.4 4.6 %all-to-all-done.buf_ref = f32[16,32,128]{2,1,0:T(8,128)S(1)} async-done(((f32[16,32,128]{2,1,0:T(8,128)}), f32[16,32,128]{2,1,0:T(8,128)S(1)}, u32[]{:S(2)}, u32[]{:S(2)}) %all-to-all-start) | async-done | bytes 262176 | tf_op jit(solution)/shard_map/all_to_all | solution.py:412
  21.0 0.3 shard_map.97
  21.3 0.1 collective-permute-start.3
  21.3 0.9 %collective-permute-start.4 = (f32[32,128]{1,0:T(8,128)S(1)}, f32[32,128]{1,0:T(8,128)S(1)}, u32[]{:S(2)}, u32[]{:S(2)}) collective-permute-start(f32[32,128]{1,0:T(8,128)S(1)} %get-tuple-element.32.after_ref), channel_id=1, source_target_pairs={{0,17},{1,16},{2,19},{3,18},{4,21},{5,20},{6,23},{7,22},{8,25},{9,... | collective-permute-start | bytes 49160 | tf_op jit(solution)/shard_map/ppermute | solution.py:456
  22.2 0.7 %collective-permute-start.5 = (f32[32,128]{1,0:T(8,128)S(1)}, f32[32,128]{1,0:T(8,128)S(1)}, u32[]{:S(2)}, u32[]{:S(2)}) collective-permute-start(f32[32,128]{1,0:T(8,128)S(1)} %get-tuple-element.36), channel_id=1, source_target_pairs={{1,18},{2,17},{3,20},{4,19},{5,22},{6,21},{7,24},{8,23},{9,26},{10... | collective-permute-start | bytes 49160 | tf_op jit(solution)/shard_map/ppermute | solution.py:457
  22.9 4.1 %shard_map.99.gram_ref = f32[2,128]{1,0:T(2,128)S(1)} custom-call(bf16[12,8,16,1024]{3,2,1,0:T(8,128)(2,1)} %bitcast.16), custom_call_target="tpu_custom_call" | custom-call | flops 1000000000 | bytes 4194304 | tf_op jit(solution)/shard_map/pallas_call | solution.py:427
  27.0 2.6 %shard_map.98 = (f32[8,128,128]{2,1,0:T(8,128)S(1)}, bf16[12,8,16,1024]{3,2,1,0:T(8,128)(2,1)S(1)}) custom-call(f32[32,128]{1,0:T(8,128)S(1)} %get-tuple-element.32.after_ref, bf16[12,8,16,1024]{3,2,1,0:T(8,128)(2,1)} %bitcast.17, f32[8,128,128]{2,1,0:T(8,128)S(1)} %get-tuple-element.24.x_ref.x0_ref, f32[136,128]{1,0:T(8,128)S(1)} %collective-permute-done.after1_ref.h1_ref, ...), custom_call_target="tpu_custom_call" | custom-call | tf_op jit(solution)/shard_map/pallas_call | solution.py:444
  29.6 0.0 collective-permute-done.4.e1_ref
  29.6 0.0 collective-permute-done.5.e2_ref
  29.6 0.0 collective-permute-done.3.f_ref
  29.6 1.2 %shard_map.100 = (f32[8,128,128]{2,1,0:T(8,128)S(1)}, f32[32,2,128]{2,1,0:T(2,128)S(1)}) custom-call(f32[8,128,128]{2,1,0:T(8,128)S(1)} %get-tuple-element.34.still_ref, f32[8,64,128]{2,1,0:T(8,128)S(1)} %collective-permute-done.3.f_ref, f32[32,128]{1,0:T(8,128)S(1)} %collective-permute-done.4.e1_ref, f32[32,128]{1,0:T(8,128)S(1)} %collective-permute-done.5.e2_ref, ...), custom_call_target="tpu_custom_call" | custom-call | tf_op jit(solution)/shard_map/pallas_call | solution.py:458
  30.9 14.2 %all_to_all.10.sums_ref = f32[32,2,128]{2,1,0:T(2,128)S(1)} all-to-all(f32[32,2,128]{2,1,0:T(2,128)S(1)} %get-tuple-element.39), channel_id=1, replica_groups=mesh['comp'=2,'tile'=16] {'comp','tile'}, dimensions={0} | all-to-all | bytes 65536 | tf_op jit(solution)/shard_map/all_to_all | solution.py:465
  45.0 2.3 %shard_map.101 = (f32[128,1024]{1,0:T(8,128)}, f32[1,12]{1,0:T(1,128)}) custom-call(f32[8,128,128]{2,1,0:T(8,128)S(1)} %get-tuple-element.38.x_ref, bf16[12,8,16,1024]{3,2,1,0:T(8,128)(2,1)S(1)} %get-tuple-element.37.basis_ref, f32[32,2,128]{2,1,0:T(2,128)S(1)} %all_to_all.10.sums_ref), custom_call_target="tpu_custom_call" | custom-call | tf_op jit(solution)/shard_map/pallas_call | solution.py:466
Async XLA Ops:
  2.8 18.2 %all-to-all-start = ((f32[16,32,128]{2,1,0:T(8,128)}), f32[16,32,128]{2,1,0:T(8,128)S(1)}, u32[]{:S(2)}, u32[]{:S(2)}) async-start(f32[16,32,128]{2,1,0:T(8,128)} %bitcast.9), calls=%async_computation | async-start | bytes 524288 | tf_op jit(solution)/shard_map/all_to_all | solution.py:412
  11.4 5.0 %collective-permute-start = (f32[136,128]{1,0:T(8,128)S(1)}, f32[136,128]{1,0:T(8,128)S(1)}, u32[]{:S(2)}, u32[]{:S(2)}) collective-permute-start(f32[136,128]{1,0:T(8,128)S(1)} %get-tuple-element.28), channel_id=1, source_target_pairs={{0,1},{1,0},{2,3},{3,2},{4,5},{5,4},{6,7},{7,6},{8,9},{9,8},{10,11... | collective-permute-start | bytes 208904 | tf_op jit(solution)/shard_map/ppermute | solution.py:425
  13.4 3.0 %collective-permute-start.1 = (f32[136,128]{1,0:T(8,128)S(1)}, f32[136,128]{1,0:T(8,128)S(1)}, u32[]{:S(2)}, u32[]{:S(2)}) collective-permute-start(f32[136,128]{1,0:T(8,128)S(1)} %get-tuple-element.29), channel_id=1, source_target_pairs={{1,2},{2,1},{3,4},{4,3},{5,6},{6,5},{7,8},{8,7},{9,10},{10,9},{11,... | collective-permute-start | bytes 208904 | tf_op jit(solution)/shard_map/ppermute | solution.py:426
  14.1 1.3 %collective-permute-start.2 = (f32[128,128]{1,0:T(8,128)S(1)}, f32[128,128]{1,0:T(8,128)S(1)}, u32[]{:S(2)}, u32[]{:S(2)}) collective-permute-start(f32[128,128]{1,0:T(8,128)S(1)} %get-tuple-element.31), channel_id=1, source_target_pairs={{0,16},{16,0},{1,17},{17,1},{2,18},{18,2},{3,19},{19,3},{4,20},{20... | collective-permute-start | bytes 196616 | tf_op jit(solution)/shard_map/ppermute | solution.py:424
  21.3 8.4 %collective-permute-start.3 = (f32[8,64,128]{2,1,0:T(8,128)S(1)}, f32[8,64,128]{2,1,0:T(8,128)S(1)}, u32[]{:S(2)}, u32[]{:S(2)}) collective-permute-start(f32[8,64,128]{2,1,0:T(8,128)S(1)} %get-tuple-element.35), channel_id=1, source_target_pairs={{0,16},{16,0},{1,17},{17,1},{2,18},{18,2},{3,19},{19,3},{4,20},{20... | collective-permute-start | bytes 786440 | tf_op jit(solution)/shard_map/ppermute | solution.py:455
  21.3 8.3 %collective-permute-start.4 = (f32[32,128]{1,0:T(8,128)S(1)}, f32[32,128]{1,0:T(8,128)S(1)}, u32[]{:S(2)}, u32[]{:S(2)}) collective-permute-start(f32[32,128]{1,0:T(8,128)S(1)} %get-tuple-element.32.after_ref), channel_id=1, source_target_pairs={{0,17},{1,16},{2,19},{3,18},{4,21},{5,20},{6,23},{7,22},{8,25},{9,... | collective-permute-start | bytes 49160 | tf_op jit(solution)/shard_map/ppermute | solution.py:456
  22.2 7.4 %collective-permute-start.5 = (f32[32,128]{1,0:T(8,128)S(1)}, f32[32,128]{1,0:T(8,128)S(1)}, u32[]{:S(2)}, u32[]{:S(2)}) collective-permute-start(f32[32,128]{1,0:T(8,128)S(1)} %get-tuple-element.36), channel_id=1, source_target_pairs={{1,18},{2,17},{3,20},{4,19},{5,22},{6,21},{7,24},{8,23},{9,26},{10... | collective-permute-start | bytes 49160 | tf_op jit(solution)/shard_map/ppermute | solution.py:457

commit v4 on v3

--- a/solution.py
+++ b/solution.py
@@ -82,21 +82,18 @@
         copy.wait()
 
 
-def gram_kernel(basis_hbm, gram_ref, basis_ref, sems):
+def gram_kernel(after_ref, basis_hbm, basis_ref, gram_ref, sems):
     vecs, levels, rows, cols = basis_ref.shape
-    ahead = 3
     copies = [
         pltpu.make_async_copy(basis_hbm.at[:, l], basis_ref.at[:, l], sems.at[l])
         for l in range(levels)
     ]
-    for copy in copies[:ahead]:
+    for copy in copies:
         copy.start()
     n = vecs * rows
     total = jnp.zeros((n, n), jnp.float32)
     for l in range(levels):
         copies[l].wait()
-        if l + ahead < levels:
-            copies[l + ahead].start()
         a = basis_ref[:, l].reshape(n, cols)
         total = total + lax.dot_general(
             a, a, (((1,), (1,)), ((), ())), preferred_element_type=jnp.float32
@@ -175,7 +172,7 @@
             ref[2 * per * levels + c : 2 * per * levels + c + 1, :] = b
 
 
-def regrid_kernel(rows, after1_ref, after2_ref, buf_ref, matrix_ref, mask_ref, f_ref, e1_ref, e2_ref):
+def regrid_kernel(rows, buf_ref, matrix_ref, mask_ref, f_ref, e1_ref, e2_ref):
     slots = matrix_ref.shape[1]
     per = f_ref.shape[0]
     cap = buf_ref.shape[1] // FLUX
@@ -215,15 +212,8 @@
 
 
 def still_kernel(
-    rows, after_ref, basis_hbm, x0_ref, h1_ref, h2_ref, kappa_ref, mask_ref, table_ref,
-    x_ref, basis_ref, x1_ref, halo_ref, sems,
+    rows, x0_ref, h1_ref, h2_ref, kappa_ref, mask_ref, table_ref, x_ref, x1_ref, halo_ref
 ):
-    copies = [
-        pltpu.make_async_copy(basis_hbm.at[i], basis_ref.at[i], sems.at[i])
-        for i in range(basis_ref.shape[0])
-    ]
-    for copy in copies:
-        copy.start()
     per = x0_ref.shape[0]
     levels = x0_ref.shape[1] // rows
     ocean = lax.axis_index("comp") == 0
@@ -263,8 +253,6 @@
 
     advance(x0_ref, x1_ref, 0)
     advance(x1_ref, x_ref, 2)
-    for copy in copies:
-        copy.wait()
 
 
 def step_kernel(
@@ -330,7 +318,7 @@
         sums_ref[d] = block
 
 
-def finish_kernel(rows, total, x_ref, basis_ref, sums_ref, out_hbm, coef_ref, out_ref, sems):
+def finish_kernel(rows, total, x_ref, basis_ref, sums_ref, out_ref, coef_ref):
     per = x_ref.shape[0]
     levels = x_ref.shape[1] // rows
     vecs = basis_ref.shape[0]
@@ -352,10 +340,6 @@
     wide = [jnp.broadcast_to(scale * s, (8, LANES)) for s in splat]
     scale = jnp.broadcast_to(scale, (8, LANES))
 
-    def put(l):
-        part = pl.ds(pl.multiple_of(l * rows, rows), rows)
-        return pltpu.make_async_copy(out_ref.at[part, :], out_hbm.at[part, :], sems.at[l])
-
     def level(l, carry):
         for c in range(per):
             s = slice(c * LANES, (c + 1) * LANES)
@@ -364,12 +348,9 @@
                 b = basis_ref[i, l, :, s].astype(jnp.float32).reshape(rows // 8, 8, LANES)
                 x = x - wide[i] * b
             out_ref[pl.ds(l * rows, rows), s] = x.reshape(rows, LANES)
-        put(l).start()
         return carry
 
     lax.fori_loop(0, levels, level, 0)
-    for l in range(levels):
-        put(l).wait()
 
 
 def body(state, basis, kappa, vmix, land_mask, send_rows, recv_slots, recv_weights):
@@ -424,34 +405,29 @@
     matrix = lax.ppermute(matrix, "comp", swap)
     got1 = lax.ppermute(pay1, "tile", pairs1)
     got2 = lax.ppermute(pay2, "tile", pairs2)
-    gram = call(
-        gram_kernel,
-        jax.ShapeDtypeStruct((2, LANES), f32),
-        [HBM],
+    still = call(
+        functools.partial(still_kernel, rows),
+        field,
+        [VMEM] * 6,
         VMEM,
         scratch=(
-            pltpu.VMEM(vectors.shape, vectors.dtype),
-            pltpu.SemaphoreType.DMA((levels,)),
+            pltpu.VMEM((per, levels * rows, LANES), f32),
+            pltpu.VMEM((4, per, levels, LANES), f32),
         ),
-        cost=pl.CostEstimate(flops=10**9, bytes_accessed=4 << 20, transcendentals=0),
-    )(in_hbm(vectors))
+    )(columns, got1, got2, kap, land_mask, table)
     foreign, edge1, edge2 = call(
         functools.partial(regrid_kernel, rows),
         (import_field, fringe, fringe),
-        [pl.BlockSpec(memory_space=pl.ANY)] * 2 + [VMEM] * 3,
+        [VMEM] * 3,
         (VMEM,) * 3,
-    )(got1, got2, moved, matrix, land_mask)
-    still, vectors = call(
-        functools.partial(still_kernel, rows),
-        (field, jax.ShapeDtypeStruct(vectors.shape, vectors.dtype)),
-        [pl.BlockSpec(memory_space=pl.ANY), HBM] + [VMEM] * 6,
+    )(moved, matrix, land_mask)
+    vectors, gram = call(
+        gram_kernel,
+        (jax.ShapeDtypeStruct(vectors.shape, vectors.dtype), jax.ShapeDtypeStruct((2, LANES), f32)),
+        [pl.BlockSpec(memory_space=pl.ANY), HBM],
         (VMEM, VMEM),
-        scratch=(
-            pltpu.VMEM((per, levels * rows, LANES), f32),
-            pltpu.VMEM((4, per, levels, LANES), f32),
-            pltpu.SemaphoreType.DMA((vecs,)),
-        ),
-    )(edge1, in_hbm(vectors), columns, got1, got2, kap, land_mask, table)
+        scratch=(pltpu.SemaphoreType.DMA((levels,)),),
+    )(edge1, in_hbm(vectors))
     imported = lax.ppermute(foreign, "comp", swap)
     edge1 = lax.ppermute(edge1, ("comp", "tile"), crossed(pairs1))
     edge2 = lax.ppermute(edge2, ("comp", "tile"), crossed(pairs2))
@@ -470,11 +446,7 @@
             jax.ShapeDtypeStruct((1, vecs), f32),
         ),
         [VMEM] * 3,
-        (HBM, VMEM),
-        scratch=(
-            pltpu.VMEM((levels * rows, cols), f32),
-            pltpu.SemaphoreType.DMA((levels,)),
-        ),
+        (VMEM, VMEM),
     )(x, vectors, sums)
     return direction.reshape(1, levels, rows, cols), coefs.reshape(vecs)
 

time: 47.7 us -> 48.3 us (1.013)
  starting transfers between devices: 12.7 us -> 17.1 us
  blocking collectives: 14.2 us -> 10.1 us
  waiting for transfers between devices: 6.85 us -> 9.5 us
  Pallas kernels: 12.9 us -> 10.6 us
    ppermute x1, starting transfers between devices: 0.87 us -> 6.46 us  [body(): edge1 = lax.ppermute(edge1, ('comp', 'tile'), crossed(pairs1))]
    all_to_all x1, blocking collectives: 14.2 us -> 10.1 us  [body(): sums = lax.all_to_all(sums, ('comp', 'tile'), 0, 0)]
    all_to_all x1, waiting for transfers between devices: 4.61 us -> 8.25 us  [body(): lax.all_to_all(bucket.reshape(bands, FLUX * cap, LANES), 'tile', 0, 0)]
    pallas_call x2, Pallas kernels: 6.73 us -> 4.84 us  [the longest x1 3.62 us: body(): call(gram_kernel, (jax.ShapeDtypeStruct(vectors.shape, vectors.dtype), ja...]
    ppermute x1, starting transfers between devices: 1.99 us -> 0.83 us  [body(): got1 = lax.ppermute(pay1, 'tile', pairs1)]
    ppermute x1, waiting for transfers between devices: 0.99 us -> 0.01 us  [body(): got1 = lax.ppermute(pay1, 'tile', pairs1)]
  transfers between devices with their start and end apart: 7 -> 7, of which waited for: 3 -> 2; matrix products, arithmetic and copies ran while one was open for 0% -> 0% of each run, Pallas kernels for 15% -> 11%
where the time goes in v4:
time: 48.3 us; the launch traced here: 48 us
  starting transfers between devices  17.1 us (35%)
  Pallas kernels  10.6 us (22%)
  blocking collectives  10.1 us (21%)
  waiting for transfers between devices  9.5 us (20%)
  between operations  0.74 us (2%)
    all_to_all x1, blocking collectives, body(): sums = lax.all_to_all(sums, ('comp', 'tile'), 0, 0)  10.1 us
    all_to_all x1, starting transfers between devices, body(): lax.all_to_all(bucket.reshape(bands, FLUX * cap, LANES), 'tile', 0, 0)  8.35 us
    all_to_all x1, waiting for transfers between devices, body(): lax.all_to_all(bucket.reshape(bands, FLUX * cap, LANES), 'tile', 0, 0)  8.25 us
    ppermute x1, starting transfers between devices, body(): edge1 = lax.ppermute(edge1, ('comp', 'tile'), crossed(pairs1))  6.46 us
    pallas_call x1, Pallas kernels, body(): call(gram_kernel, (jax.ShapeDtypeStruct(vectors.shape, vectors.dtype), ja...  3.62 us
    pallas_call x1, Pallas kernels, body(): call(functools.partial(gather_kernel, rows), (jax.ShapeDtypeStruct((bands...  2.12 us
    pallas_call x1, Pallas kernels, body(): call(functools.partial(finish_kernel, rows, total), (jax.ShapeDtypeStruct...  1.85 us
    ppermute x1, waiting for transfers between devices, body(): matrix = lax.ppermute(matrix, 'comp', swap)  1.24 us
  transfers between devices with their start and end apart: 7, of which 2 were waited for; matrix products, arithmetic and copies ran while one was open for 0% of the time, Pallas kernels for 11%

profile of v4, /device:TPU:0, one launch (start us, length us, event | category | flops | bytes accessed | tf_op | source)
XLA Modules:
  0.0 48.0 jit_solution(5607217135030887414)
XLA Ops:
  0.6 2.1 %shard_map.95 = (f32[512,128]{1,0:T(8,128)}, f32[8,128,128]{2,1,0:T(8,128)S(1)}, f32[16,1024]{1,0:T(8,128)S(1)}, s32[16,1024]{1,0:T(8,128)S(1)}, s32[4,128]{1,0:...) custom-call(s32[8,16]{1,0:T(8,128)} %bitcast.19, f32[128,1024]{1,0:T(8,128)} %bitcast.17, f32[16,1024]{1,0:T(8,128)} %bitcast.18, ...), custom_call_target="tpu_custom_call" | custom-call | tf_op jit(solution)/shard_map/pallas_call | solution.py:382
  2.8 8.4 %all-to-all-start = ((f32[16,32,128]{2,1,0:T(8,128)}), f32[16,32,128]{2,1,0:T(8,128)S(1)}, u32[]{:S(2)}, u32[]{:S(2)}) async-start(f32[16,32,128]{2,1,0:T(8,128)} %bitcast.9), calls=%async_computation | async-start | bytes 524288 | tf_op jit(solution)/shard_map/all_to_all | solution.py:393
  11.1 0.3 shard_map.96
  11.4 0.1 collective-permute-start.2
  11.5 1.2 %collective-permute-done.2.matrix_ref = f32[128,128]{1,0:T(8,128)S(1)} collective-permute-done((f32[128,128]{1,0:T(8,128)S(1)}, f32[128,128]{1,0:T(8,128)S(1)}, u32[]{:S(2)}, u32[]{:S(2)}) %collective-permute-start.2) | collective-permute-done | bytes 65568 | tf_op jit(solution)/shard_map/ppermute | solution.py:405
  12.7 8.2 %all-to-all-done.buf_ref = f32[16,32,128]{2,1,0:T(8,128)S(1)} async-done(((f32[16,32,128]{2,1,0:T(8,128)}), f32[16,32,128]{2,1,0:T(8,128)S(1)}, u32[]{:S(2)}, u32[]{:S(2)}) %all-to-all-start) | async-done | bytes 262176 | tf_op jit(solution)/shard_map/all_to_all | solution.py:393
  21.0 0.3 shard_map.98
  21.3 0.1 collective-permute-start.3
  21.3 0.8 %collective-permute-start = (f32[136,128]{1,0:T(8,128)S(1)}, f32[136,128]{1,0:T(8,128)S(1)}, u32[]{:S(2)}, u32[]{:S(2)}) collective-permute-start(f32[136,128]{1,0:T(8,128)S(1)} %get-tuple-element.28), channel_id=1, source_target_pairs={{0,1},{1,0},{2,3},{3,2},{4,5},{5,4},{6,7},{7,6},{8,9},{9,8},{10,11... | collective-permute-start | bytes 208904 | tf_op jit(solution)/shard_map/ppermute | solution.py:406
  22.2 0.7 %collective-permute-start.1 = (f32[136,128]{1,0:T(8,128)S(1)}, f32[136,128]{1,0:T(8,128)S(1)}, u32[]{:S(2)}, u32[]{:S(2)}) collective-permute-start(f32[136,128]{1,0:T(8,128)S(1)} %get-tuple-element.29), channel_id=1, source_target_pairs={{1,2},{2,1},{3,4},{4,3},{5,6},{6,5},{7,8},{8,7},{9,10},{10,9},{11,... | collective-permute-start | bytes 208904 | tf_op jit(solution)/shard_map/ppermute | solution.py:407
  22.8 0.7 %collective-permute-start.5 = (f32[32,128]{1,0:T(8,128)S(1)}, f32[32,128]{1,0:T(8,128)S(1)}, u32[]{:S(2)}, u32[]{:S(2)}) collective-permute-start(f32[32,128]{1,0:T(8,128)S(1)} %get-tuple-element.35), channel_id=1, source_target_pairs={{1,18},{2,17},{3,20},{4,19},{5,22},{6,21},{7,24},{8,23},{9,26},{10... | collective-permute-start | bytes 49160 | tf_op jit(solution)/shard_map/ppermute | solution.py:433
  23.5 6.5 %collective-permute-start.4 = (f32[32,128]{1,0:T(8,128)S(1)}, f32[32,128]{1,0:T(8,128)S(1)}, u32[]{:S(2)}, u32[]{:S(2)}) collective-permute-start(f32[32,128]{1,0:T(8,128)S(1)} %get-tuple-element.34.after_ref), channel_id=1, source_target_pairs={{0,17},{1,16},{2,19},{3,18},{4,21},{5,20},{6,23},{7,22},{8,25},{9,... | collective-permute-start | bytes 49160 | tf_op jit(solution)/shard_map/ppermute | solution.py:432
  30.0 0.0 collective-permute-done.h1_ref
  30.0 0.0 collective-permute-done.1.h2_ref
  30.0 1.2 %shard_map.97.still_ref = f32[8,128,128]{2,1,0:T(8,128)S(1)} custom-call(f32[8,128,128]{2,1,0:T(8,128)S(1)} %get-tuple-element.22.x_ref.x0_ref, f32[136,128]{1,0:T(8,128)S(1)} %collective-permute-done.h1_ref, f32[136,128]{1,0:T(8,128)S(1)} %collective-permute-done.1.h2_ref, f32[16,1024]{1,0:T(8,128)S(1)} %get-tuple-element.25.kappa_ref, ...), custom_call_target="tpu_custom_call" | custom-call | tf_op jit(solution)/shard_map/pallas_call | solution.py:408
  31.2 3.6 %shard_map.99 = (bf16[12,8,16,1024]{3,2,1,0:T(8,128)(2,1)S(1)}, f32[2,128]{1,0:T(2,128)S(1)}) custom-call(f32[32,128]{1,0:T(8,128)S(1)} %get-tuple-element.34.after_ref, bf16[12,8,16,1024]{3,2,1,0:T(8,128)(2,1)} %bitcast.16), custom_call_target="tpu_custom_call" | custom-call | tf_op jit(solution)/shard_map/pallas_call | solution.py:424
  34.8 0.0 collective-permute-done.5.e2_ref
  34.8 0.0 collective-permute-done.4.e1_ref
  34.8 0.0 collective-permute-done.3.f_ref
  34.9 1.2 %shard_map.100 = (f32[8,128,128]{2,1,0:T(8,128)S(1)}, f32[32,2,128]{2,1,0:T(2,128)S(1)}) custom-call(f32[8,128,128]{2,1,0:T(8,128)S(1)} %shard_map.97.still_ref, f32[8,64,128]{2,1,0:T(8,128)S(1)} %collective-permute-done.3.f_ref, f32[32,128]{1,0:T(8,128)S(1)} %collective-permute-done.4.e1_ref, f32[32,128]{1,0:T(8,128)S(1)} %collective-permute-done.5.e2_ref, ...), custom_call_target="tpu_custom_call" | custom-call | tf_op jit(solution)/shard_map/pallas_call | solution.py:434
  36.1 10.1 %all_to_all.10.sums_ref = f32[32,2,128]{2,1,0:T(2,128)S(1)} all-to-all(f32[32,2,128]{2,1,0:T(2,128)S(1)} %get-tuple-element.39), channel_id=1, replica_groups=mesh['comp'=2,'tile'=16] {'comp','tile'}, dimensions={0} | all-to-all | bytes 65536 | tf_op jit(solution)/shard_map/all_to_all | solution.py:441
  46.2 1.8 %shard_map.101 = (f32[128,1024]{1,0:T(8,128)}, f32[1,12]{1,0:T(1,128)}) custom-call(f32[8,128,128]{2,1,0:T(8,128)S(1)} %get-tuple-element.38.x_ref, bf16[12,8,16,1024]{3,2,1,0:T(8,128)(2,1)S(1)} %get-tuple-element.36.basis_ref, f32[32,2,128]{2,1,0:T(2,128)S(1)} %all_to_all.10.sums_ref), custom_call_target="tpu_custom_call" | custom-call | tf_op jit(solution)/shard_map/pallas_call | solution.py:442
Async XLA Ops:
  2.8 18.2 %all-to-all-start = ((f32[16,32,128]{2,1,0:T(8,128)}), f32[16,32,128]{2,1,0:T(8,128)S(1)}, u32[]{:S(2)}, u32[]{:S(2)}) async-start(f32[16,32,128]{2,1,0:T(8,128)} %bitcast.9), calls=%async_computation | async-start | bytes 524288 | tf_op jit(solution)/shard_map/all_to_all | solution.py:393
  11.4 1.3 %collective-permute-start.2 = (f32[128,128]{1,0:T(8,128)S(1)}, f32[128,128]{1,0:T(8,128)S(1)}, u32[]{:S(2)}, u32[]{:S(2)}) collective-permute-start(f32[128,128]{1,0:T(8,128)S(1)} %get-tuple-element.32), channel_id=1, source_target_pairs={{0,16},{16,0},{1,17},{17,1},{2,18},{18,2},{3,19},{19,3},{4,20},{20... | collective-permute-start | bytes 196616 | tf_op jit(solution)/shard_map/ppermute | solution.py:405
  21.3 13.6 %collective-permute-start.3 = (f32[8,64,128]{2,1,0:T(8,128)S(1)}, f32[8,64,128]{2,1,0:T(8,128)S(1)}, u32[]{:S(2)}, u32[]{:S(2)}) collective-permute-start(f32[8,64,128]{2,1,0:T(8,128)S(1)} %get-tuple-element.33), channel_id=1, source_target_pairs={{0,16},{16,0},{1,17},{17,1},{2,18},{18,2},{3,19},{19,3},{4,20},{20... | collective-permute-start | bytes 786440 | tf_op jit(solution)/shard_map/ppermute | solution.py:431
  21.3 8.6 %collective-permute-start = (f32[136,128]{1,0:T(8,128)S(1)}, f32[136,128]{1,0:T(8,128)S(1)}, u32[]{:S(2)}, u32[]{:S(2)}) collective-permute-start(f32[136,128]{1,0:T(8,128)S(1)} %get-tuple-element.28), channel_id=1, source_target_pairs={{0,1},{1,0},{2,3},{3,2},{4,5},{5,4},{6,7},{7,6},{8,9},{9,8},{10,11... | collective-permute-start | bytes 208904 | tf_op jit(solution)/shard_map/ppermute | solution.py:406
  22.2 7.8 %collective-permute-start.1 = (f32[136,128]{1,0:T(8,128)S(1)}, f32[136,128]{1,0:T(8,128)S(1)}, u32[]{:S(2)}, u32[]{:S(2)}) collective-permute-start(f32[136,128]{1,0:T(8,128)S(1)} %get-tuple-element.29), channel_id=1, source_target_pairs={{1,2},{2,1},{3,4},{4,3},{5,6},{6,5},{7,8},{8,7},{9,10},{10,9},{11,... | collective-permute-start | bytes 208904 | tf_op jit(solution)/shard_map/ppermute | solution.py:407
  22.8 12.0 %collective-permute-start.5 = (f32[32,128]{1,0:T(8,128)S(1)}, f32[32,128]{1,0:T(8,128)S(1)}, u32[]{:S(2)}, u32[]{:S(2)}) collective-permute-start(f32[32,128]{1,0:T(8,128)S(1)} %get-tuple-element.35), channel_id=1, source_target_pairs={{1,18},{2,17},{3,20},{4,19},{5,22},{6,21},{7,24},{8,23},{9,26},{10... | collective-permute-start | bytes 49160 | tf_op jit(solution)/shard_map/ppermute | solution.py:433
  23.5 11.3 %collective-permute-start.4 = (f32[32,128]{1,0:T(8,128)S(1)}, f32[32,128]{1,0:T(8,128)S(1)}, u32[]{:S(2)}, u32[]{:S(2)}) collective-permute-start(f32[32,128]{1,0:T(8,128)S(1)} %get-tuple-element.34.after_ref), channel_id=1, source_target_pairs={{0,17},{1,16},{2,19},{3,18},{4,21},{5,20},{6,23},{7,22},{8,25},{9,... | collective-permute-start | bytes 49160 | tf_op jit(solution)/shard_map/ppermute | solution.py:432

commit v5 on v4

--- a/solution.py
+++ b/solution.py
@@ -34,6 +34,10 @@
 def split(a):
     high = a.astype(jnp.bfloat16)
     return high, (a - high.astype(jnp.float32)).astype(jnp.bfloat16)
+
+
+def payload_rows(levels, per):
+    return 2 * levels * per + per
 
 
 def block_place(b, per):
@@ -82,7 +86,18 @@
         copy.wait()
 
 
-def gram_kernel(after_ref, basis_hbm, basis_ref, gram_ref, sems):
+def fetch_kernel(after_ref, basis_hbm, basis_ref, sems):
+    copies = [
+        pltpu.make_async_copy(basis_hbm.at[i], basis_ref.at[i], sems.at[i])
+        for i in range(basis_ref.shape[0])
+    ]
+    for copy in copies:
+        copy.start()
+    for copy in copies:
+        copy.wait()
+
+
+def gram_kernel(basis_hbm, gram_ref, basis_ref, sems):
     vecs, levels, rows, cols = basis_ref.shape
     copies = [
         pltpu.make_async_copy(basis_hbm.at[:, l], basis_ref.at[:, l], sems.at[l])
@@ -125,12 +140,13 @@
 
 def early_kernel(
     rows, slots_ref, weights_ref, x_ref, kappa_ref, mask_ref, vmix_ref,
-    matrix_ref, p1_ref, p2_ref, table_ref,
+    pack_ref, table_ref,
 ):
     over, blocks = slots_ref.shape
-    slots = matrix_ref.shape[1]
     per = x_ref.shape[0]
     levels = x_ref.shape[1] // rows
+    size = payload_rows(levels, per)
+    slots = (pack_ref.shape[0] - 2 * size) // blocks * LANES
     row = lax.broadcasted_iota(jnp.int32, (slots, blocks), 0)
     mat = jnp.zeros((slots, blocks), jnp.float32)
     for k in range(over):
@@ -138,7 +154,9 @@
     b0 = lax.broadcasted_iota(jnp.int32, (blocks, blocks), 0)
     b1 = lax.broadcasted_iota(jnp.int32, (blocks, blocks), 1)
     order = jnp.where(lax.rem(b0, rows) * per + lax.div(b0, rows) == b1, 1.0, 0.0)
-    matrix_ref[...] = jnp.dot(order, mat.T, precision=lax.Precision.HIGHEST)
+    mat = jnp.dot(order, mat.T, precision=lax.Precision.HIGHEST)
+    for p in range(slots // LANES):
+        pack_ref[p * blocks : (p + 1) * blocks, :] = mat[:, p * LANES : (p + 1) * LANES]
 
     ocean = lax.axis_index("comp") == 0
     even = lax.rem(lax.axis_index("tile"), 2) == 0
@@ -164,7 +182,9 @@
                 acc = acc + vmix[:, q : q + 1] * x[q : q + 1, :]
             pay.append((m * acc, x, m * k))
         pays.append(pay)
-    for ref, flag in ((p1_ref, even), (p2_ref, jnp.logical_not(even))):
+    base = slots // LANES * blocks
+    for n, flag in ((0, even), (1, jnp.logical_not(even))):
+        ref = pack_ref.at[base + n * size : base + (n + 1) * size, :]
         for c in range(per):
             a, x, b = [jnp.where(flag, v, u) for u, v in zip(pays[0][c], pays[1][c])]
             ref[c * levels : (c + 1) * levels, :] = a
@@ -172,15 +192,18 @@
             ref[2 * per * levels + c : 2 * per * levels + c + 1, :] = b
 
 
-def regrid_kernel(rows, buf_ref, matrix_ref, mask_ref, f_ref, e1_ref, e2_ref):
-    slots = matrix_ref.shape[1]
+def regrid_kernel(rows, levels, buf_ref, pack_ref, mask_ref, f_ref, e1_ref, e2_ref):
     per = f_ref.shape[0]
     cap = buf_ref.shape[1] // FLUX
+    slots = buf_ref.shape[0] * cap
+    blocks = rows * per
+    size = payload_rows(levels, per)
     wide = jnp.concatenate(
         [buf_ref[:, f * cap : (f + 1) * cap, :].reshape(slots, LANES) for f in range(FLUX)], axis=1
     )
     bh, bl = split(wide)
-    wh, wl = split(matrix_ref[...])
+    pieces = [pack_ref[p * blocks : (p + 1) * blocks, :] for p in range(slots // LANES)]
+    wh, wl = split(jnp.concatenate(pieces, axis=1))
     dot = functools.partial(jnp.dot, preferred_element_type=jnp.float32)
     out = dot(wh, bh) + (dot(wh, bl) + dot(wl, bh))
     for f in range(FLUX):
@@ -190,58 +213,46 @@
             ]
     ocean = lax.axis_index("comp") != 0
     even = lax.rem(lax.axis_index("tile"), 2) == 0
+    base = slots // LANES * blocks
+    for n, ref in enumerate((e1_ref, e2_ref)):
+        ref[per * levels :, :] = pack_ref[base + n * size + per * levels : base + (n + 1) * size, :]
     for c in range(per):
         s = slice(c * LANES, (c + 1) * LANES)
         edges = []
         for edge in (0, rows - 1):
             m = jnp.where(ocean, mask_ref[edge : edge + 1, s].astype(jnp.float32), 1.0)
-            edges.append(m * f_ref[c, pl.ds(edge, FLUX, stride=rows), :])
-        e1_ref[c * FLUX : (c + 1) * FLUX, :] = jnp.where(even, edges[1], edges[0])
-        e2_ref[c * FLUX : (c + 1) * FLUX, :] = jnp.where(even, edges[0], edges[1])
-
-
-def stencil(xs, kappa_ref, rows, prev, nxt, row):
+            forced = m * f_ref[c, pl.ds(edge, FLUX, stride=rows), :]
+            still = jnp.zeros((levels - FLUX, LANES), jnp.float32)
+            edges.append(jnp.concatenate([forced, still], axis=0))
+        for n, (ref, forced) in enumerate(
+            ((e1_ref, jnp.where(even, edges[1], edges[0])), (e2_ref, jnp.where(even, edges[0], edges[1])))
+        ):
+            at = base + n * size + c * levels
+            ref[c * levels : (c + 1) * levels, :] = pack_ref[at : at + levels, :] + forced
+
+
+def stencil(xs, kappa_ref, rows):
     left, right = shifted(xs, True), shifted(xs, False)
+    row = lax.broadcasted_iota(jnp.int32, (rows, LANES), 0)
     out = []
     for c, x in enumerate(xs):
-        up = jnp.where(row == 0, prev(c), pltpu.roll(x, 1, 0))
-        down = jnp.where(row == rows - 1, nxt(c), pltpu.roll(x, rows - 1, 0))
+        up = jnp.where(row == 0, 0.0, pltpu.roll(x, 1, 0))
+        down = jnp.where(row == rows - 1, 0.0, pltpu.roll(x, rows - 1, 0))
         k = kappa_ref[:, c * LANES : (c + 1) * LANES]
         out.append(k * (up + down + left[c] + right[c] - 4.0 * x))
     return out
 
 
-def still_kernel(
-    rows, x0_ref, h1_ref, h2_ref, kappa_ref, mask_ref, table_ref, x_ref, x1_ref, halo_ref
-):
+def still_kernel(rows, x0_ref, kappa_ref, mask_ref, table_ref, x_ref, x1_ref):
     per = x0_ref.shape[0]
     levels = x0_ref.shape[1] // rows
     ocean = lax.axis_index("comp") == 0
-    even = lax.rem(lax.axis_index("tile"), 2) == 0
-    for side in range(2):
-        flag = even if side == 1 else jnp.logical_not(even)
-
-        def take(lo, n):
-            return jnp.where(flag, h1_ref[lo : lo + n, :], h2_ref[lo : lo + n, :])
-
-        for c in range(per):
-            edge = x0_ref[c, pl.ds(side * (rows - 1), levels, stride=rows), :]
-            a = take(c * levels, levels)
-            b = take(2 * per * levels + c, 1)
-            halo_ref[side, c] = take((per + c) * levels, levels)
-            halo_ref[2 + side, c] = a + b * edge
-    row = lax.broadcasted_iota(jnp.int32, (rows, LANES), 0)
-
-    def advance(src, dst, base):
+
+    def advance(src, dst):
         for l in range(levels):
             part = slice(l * rows, (l + 1) * rows)
             xs = [src[c, part, :] for c in range(per)]
-            moved = stencil(
-                xs, kappa_ref, rows,
-                lambda c: halo_ref[base, c, l : l + 1, :],
-                lambda c: halo_ref[base + 1, c, l : l + 1, :],
-                row,
-            )
+            moved = stencil(xs, kappa_ref, rows)
             for c in range(per):
                 acc = xs[c] + moved[c]
                 for q in range(levels):
@@ -251,23 +262,22 @@
                 mask = jnp.where(ocean, mask_ref[:, s].astype(jnp.float32), 1.0)
                 dst[c, part, :] = mask * acc
 
-    advance(x0_ref, x1_ref, 0)
-    advance(x1_ref, x_ref, 2)
+    advance(x0_ref, x1_ref)
+    advance(x1_ref, x_ref)
 
 
 def step_kernel(
-    rows, still_ref, f_ref, e1_ref, e2_ref, kappa_ref, mask_ref, table_ref, basis_ref, gram_ref,
-    x_ref, sums_ref, f1_ref,
+    rows, still_ref, x0_ref, f_ref, h1_ref, h2_ref, kappa_ref, mask_ref, vmix_ref, table_ref,
+    basis_ref, gram_ref, x_ref, sums_ref, f1_ref,
 ):
     per = still_ref.shape[0]
     levels = still_ref.shape[1] // rows
     vecs = basis_ref.shape[0]
     ocean = lax.axis_index("comp") == 0
     even = lax.rem(lax.axis_index("tile"), 2) == 0
-    row = lax.broadcasted_iota(jnp.int32, (rows, LANES), 0)
-
-    def mask(c):
-        m = mask_ref[:, c * LANES : (c + 1) * LANES].astype(jnp.float32)
+
+    def mask(c, part=slice(None)):
+        m = mask_ref[part, c * LANES : (c + 1) * LANES].astype(jnp.float32)
         return jnp.where(ocean, m, 1.0)
 
     for c in range(per):
@@ -279,21 +289,40 @@
         part = slice(l * rows, (l + 1) * rows)
         if l < FLUX:
             fs = [f1_ref[c, part, :] for c in range(per)]
-
-            def edge(c, flag):
-                i = slice(c * FLUX + l, c * FLUX + l + 1)
-                return jnp.where(flag, e1_ref[i, :], e2_ref[i, :])
-
-            moved = stencil(
-                fs, kappa_ref, rows,
-                lambda c: edge(c, jnp.logical_not(even)), lambda c: edge(c, even), row,
-            )
+            moved = stencil(fs, kappa_ref, rows)
         for c in range(per):
             acc = fs[c] + moved[c] + f_ref[c, part, :] if l < FLUX else 0.0
             for q in range(FLUX):
                 v = table_ref[l * levels + q : l * levels + q + 1, :]
                 acc = acc + v * f1_ref[c, q * rows : (q + 1) * rows, :]
             x_ref[c, part, :] = still_ref[c, part, :] + mask(c) * acc
+
+    vmix = vmix_ref[...]
+    for side, edge, inner in ((0, 0, 1), (1, rows - 1, rows - 2)):
+        flag = even if side == 1 else jnp.logical_not(even)
+
+        def take(lo, n):
+            return jnp.where(flag, h1_ref[lo : lo + n, :], h2_ref[lo : lo + n, :])
+
+        def factor(c, r):
+            r = slice(r, r + 1)
+            return mask(c, r), mask(c, r) * kappa_ref[r, c * LANES : (c + 1) * LANES]
+
+        ds = [factor(c, edge)[1] * take((per + c) * levels, levels) for c in range(per)]
+        left, right = shifted(ds, True), shifted(ds, False)
+        for c in range(per):
+            d = ds[c]
+            own = x0_ref[c, pl.ds(edge, levels, stride=rows), :]
+            foreign = take(c * levels, levels) + take(2 * per * levels + c, 1) * own
+            m, mk = factor(c, edge)
+            mixed = d
+            for q in range(levels):
+                mixed = mixed + vmix[:, q : q + 1] * d[q : q + 1, :]
+            at = pl.ds(edge, levels, stride=rows)
+            change = m * mixed + mk * (left[c] + right[c] - 4.0 * d + foreign)
+            x_ref[c, at, :] = x_ref[c, at, :] + change
+            at = pl.ds(inner, levels, stride=rows)
+            x_ref[c, at, :] = x_ref[c, at, :] + factor(c, inner)[1] * d
 
     def level(l, accs):
         accs = list(accs)
@@ -369,8 +398,7 @@
 
     field = jax.ShapeDtypeStruct((per, levels * rows, LANES), f32)
     import_field = jax.ShapeDtypeStruct((per, FLUX * rows, LANES), f32)
-    pay = jax.ShapeDtypeStruct((2 * levels * per + per, LANES), f32)
-    fringe = jax.ShapeDtypeStruct((per * FLUX, LANES), f32)
+    pay = jax.ShapeDtypeStruct((payload_rows(levels, per), LANES), f32)
     pairs1 = [(i, i ^ 1) for i in range(bands)]
     pairs2 = [p for i in range(1, bands - 1, 2) for p in ((i, i + 1), (i + 1, i))]
     swap = [(i, i ^ 1) for i in range(comps)]
@@ -391,42 +419,46 @@
         ),
     )(*[in_hbm(a) for a in (send_rows[0, 0].T, flat) + sides])
     moved = lax.all_to_all(bucket.reshape(bands, FLUX * cap, LANES), "tile", 0, 0)
-    matrix, pay1, pay2, table = call(
+    pack, table = call(
         functools.partial(early_kernel, rows),
         (
-            jax.ShapeDtypeStruct((blocks, bands * cap), f32),
-            pay,
-            pay,
+            jax.ShapeDtypeStruct((bands * cap // LANES * blocks + 2 * pay.shape[0], LANES), f32),
             jax.ShapeDtypeStruct((levels * levels, LANES), f32),
         ),
         [VMEM] * 6,
-        (VMEM,) * 4,
+        (VMEM,) * 2,
     )(slots, weights, columns, kap, land_mask, vm)
-    matrix = lax.ppermute(matrix, "comp", swap)
-    got1 = lax.ppermute(pay1, "tile", pairs1)
-    got2 = lax.ppermute(pay2, "tile", pairs2)
+    pack = lax.ppermute(pack, "comp", swap)
+    gram = call(
+        gram_kernel,
+        jax.ShapeDtypeStruct((2, LANES), f32),
+        [HBM],
+        VMEM,
+        scratch=(
+            pltpu.VMEM(vectors.shape, vectors.dtype),
+            pltpu.SemaphoreType.DMA((levels,)),
+        ),
+    )(in_hbm(vectors))
     still = call(
         functools.partial(still_kernel, rows),
         field,
-        [VMEM] * 6,
+        [VMEM] * 4,
         VMEM,
-        scratch=(
-            pltpu.VMEM((per, levels * rows, LANES), f32),
-            pltpu.VMEM((4, per, levels, LANES), f32),
-        ),
-    )(columns, got1, got2, kap, land_mask, table)
+        scratch=(pltpu.VMEM((per, levels * rows, LANES), f32),),
+    )(columns, kap, land_mask, table)
+
     foreign, edge1, edge2 = call(
-        functools.partial(regrid_kernel, rows),
-        (import_field, fringe, fringe),
+        functools.partial(regrid_kernel, rows, levels),
+        (import_field, pay, pay),
         [VMEM] * 3,
         (VMEM,) * 3,
-    )(moved, matrix, land_mask)
-    vectors, gram = call(
-        gram_kernel,
-        (jax.ShapeDtypeStruct(vectors.shape, vectors.dtype), jax.ShapeDtypeStruct((2, LANES), f32)),
+    )(moved, pack, land_mask)
+    vectors = call(
+        fetch_kernel,
+        jax.ShapeDtypeStruct(vectors.shape, vectors.dtype),
         [pl.BlockSpec(memory_space=pl.ANY), HBM],
-        (VMEM, VMEM),
-        scratch=(pltpu.SemaphoreType.DMA((levels,)),),
+        VMEM,
+        scratch=(pltpu.SemaphoreType.DMA((vecs,)),),
     )(edge1, in_hbm(vectors))
     imported = lax.ppermute(foreign, "comp", swap)
     edge1 = lax.ppermute(edge1, ("comp", "tile"), crossed(pairs1))
@@ -434,10 +466,10 @@
     x, sums = call(
         functools.partial(step_kernel, rows),
         (field, jax.ShapeDtypeStruct((devices, 2, LANES), f32)),
-        [VMEM] * 9,
+        [VMEM] * 11,
         (VMEM, VMEM),
         scratch=(pltpu.VMEM((per, FLUX * rows, LANES), f32),),
-    )(still, imported, edge1, edge2, kap, land_mask, table, vectors, gram)
+    )(still, columns, imported, edge1, edge2, kap, land_mask, vm, table, vectors, gram)
     sums = lax.all_to_all(sums, ("comp", "tile"), 0, 0)
     direction, coefs = call(
         functools.partial(finish_kernel, rows, total),

time: 48.3 us -> 45.7 us (0.946)
  starting transfers between devices: 17.1 us -> 12.6 us
  Pallas kernels: 10.6 us -> 12.7 us
    ppermute x1, starting transfers between devices: 6.46 us -> 3.41 us  [body(): edge1 = lax.ppermute(edge1, ('comp', 'tile'), crossed(pairs1))]
    pallas_call x4 -> x5, Pallas kernels: 5.4 us -> 7.3 us  [the longest x1 3.61 us: body(): call(gram_kernel, jax.ShapeDtypeStruct((2, LANES), f32), [HBM], VMEM, scr...]
    ppermute x3 -> x1, starting transfers between devices: 1.56 us -> 0.07 us  [body(): pack = lax.ppermute(pack, 'comp', swap)]
    ppermute x3 -> x1, waiting for transfers between devices: 1.25 us -> 1.44 us  [body(): pack = lax.ppermute(pack, 'comp', swap)]
  transfers between devices with their start and end apart: 7 -> 5, of which waited for: 2 -> 2; matrix products, arithmetic and copies ran while one was open for 0% -> 0% of each run, Pallas kernels for 11% -> 16%
where the time goes in v5:
time: 45.7 us; the launch traced here: 45.3 us
  Pallas kernels  12.7 us (28%)
  starting transfers between devices  12.6 us (28%)
  blocking collectives  9.83 us (22%)
  waiting for transfers between devices  9.51 us (21%)
  between operations  0.74 us (2%)
    all_to_all x1, blocking collectives, body(): sums = lax.all_to_all(sums, ('comp', 'tile'), 0, 0)  9.83 us
    all_to_all x1, starting transfers between devices, body(): lax.all_to_all(bucket.reshape(bands, FLUX * cap, LANES), 'tile', 0, 0)  8.35 us
    all_to_all x1, waiting for transfers between devices, body(): lax.all_to_all(bucket.reshape(bands, FLUX * cap, LANES), 'tile', 0, 0)  8.06 us
    pallas_call x1, Pallas kernels, body(): call(gram_kernel, jax.ShapeDtypeStruct((2, LANES), f32), [HBM], VMEM, scr...  3.61 us
    ppermute x1, starting transfers between devices, body(): edge1 = lax.ppermute(edge1, ('comp', 'tile'), crossed(pairs1))  3.41 us
    pallas_call x1, Pallas kernels, body(): call(functools.partial(gather_kernel, rows), (jax.ShapeDtypeStruct((bands...  2.12 us
    pallas_call x1, Pallas kernels, body(): call(fetch_kernel, jax.ShapeDtypeStruct(vectors.shape, vectors.dtype), [p...  1.93 us
    pallas_call x1, Pallas kernels, body(): call(functools.partial(finish_kernel, rows, total), (jax.ShapeDtypeStruct...  1.85 us
  transfers between devices with their start and end apart: 5, of which 2 were waited for; matrix products, arithmetic and copies ran while one was open for 0% of the time, Pallas kernels for 16%

profile of v5, /device:TPU:0, one launch (start us, length us, event | category | flops | bytes accessed | tf_op | source)
XLA Modules:
  0.0 45.3 jit_solution(5332335235126516065)
XLA Ops:
  0.6 2.1 %shard_map.95 = (f32[512,128]{1,0:T(8,128)}, f32[8,128,128]{2,1,0:T(8,128)S(1)}, f32[16,1024]{1,0:T(8,128)S(1)}, s32[16,1024]{1,0:T(8,128)S(1)}, s32[4,128]{1,0:...) custom-call(s32[8,16]{1,0:T(8,128)} %bitcast.20, f32[128,1024]{1,0:T(8,128)} %bitcast.18, f32[16,1024]{1,0:T(8,128)} %bitcast.19, ...), custom_call_target="tpu_custom_call" | custom-call | tf_op jit(solution)/shard_map/pallas_call | solution.py:410
  2.8 8.4 %all-to-all-start = ((f32[16,32,128]{2,1,0:T(8,128)}), f32[16,32,128]{2,1,0:T(8,128)S(1)}, u32[]{:S(2)}, u32[]{:S(2)}) async-start(f32[16,32,128]{2,1,0:T(8,128)} %bitcast.9), calls=%async_computation | async-start | bytes 524288 | tf_op jit(solution)/shard_map/all_to_all | solution.py:421
  11.1 0.3 shard_map.96
  11.4 0.1 collective-permute-start
  11.5 1.4 %collective-permute-done.pack_ref = f32[400,128]{1,0:T(8,128)S(1)} collective-permute-done((f32[400,128]{1,0:T(8,128)S(1)}, f32[400,128]{1,0:T(8,128)S(1)}, u32[]{:S(2)}, u32[]{:S(2)}) %collective-permute-start) | collective-permute-done | bytes 204832 | tf_op jit(solution)/shard_map/ppermute | solution.py:431
  12.9 8.1 %all-to-all-done.buf_ref = f32[16,32,128]{2,1,0:T(8,128)S(1)} async-done(((f32[16,32,128]{2,1,0:T(8,128)}), f32[16,32,128]{2,1,0:T(8,128)S(1)}, u32[]{:S(2)}, u32[]{:S(2)}) %all-to-all-start) | async-done | bytes 262176 | tf_op jit(solution)/shard_map/all_to_all | solution.py:421
  21.0 0.3 shard_map.98
  21.3 0.1 collective-permute-start.1
  21.3 0.7 %collective-permute-start.3 = (f32[136,128]{1,0:T(8,128)S(1)}, f32[136,128]{1,0:T(8,128)S(1)}, u32[]{:S(2)}, u32[]{:S(2)}) collective-permute-start(f32[136,128]{1,0:T(8,128)S(1)} %get-tuple-element.29), channel_id=1, source_target_pairs={{1,18},{2,17},{3,20},{4,19},{5,22},{6,21},{7,24},{8,23},{9,26},{10... | collective-permute-start | bytes 208904 | tf_op jit(solution)/shard_map/ppermute | solution.py:465
  22.0 3.4 %collective-permute-start.2 = (f32[136,128]{1,0:T(8,128)S(1)}, f32[136,128]{1,0:T(8,128)S(1)}, u32[]{:S(2)}, u32[]{:S(2)}) collective-permute-start(f32[136,128]{1,0:T(8,128)S(1)} %get-tuple-element.28.after_ref), channel_id=1, source_target_pairs={{0,17},{1,16},{2,19},{3,18},{4,21},{5,20},{6,23},{7,22},{8,25},{9,... | collective-permute-start | bytes 208904 | tf_op jit(solution)/shard_map/ppermute | solution.py:464
  25.4 3.6 %shard_map.100.gram_ref = f32[2,128]{1,0:T(2,128)S(1)} custom-call(bf16[12,8,16,1024]{3,2,1,0:T(8,128)(2,1)} %bitcast.16), custom_call_target="tpu_custom_call" | custom-call | tf_op jit(solution)/shard_map/pallas_call | solution.py:432
  29.0 1.2 %shard_map.97.still_ref = f32[8,128,128]{2,1,0:T(8,128)S(1)} custom-call(f32[8,128,128]{2,1,0:T(8,128)S(1)} %get-tuple-element.18.x_ref.x0_ref, f32[16,1024]{1,0:T(8,128)S(1)} %get-tuple-element.19.kappa_ref, s32[16,1024]{1,0:T(8,128)S(1)} %get-tuple-element.20.mask_ref, f32[64,128]{1,0:T(8,128)S(1)} %get-tuple-element.24.table_ref), custom_call_target="tpu_custom_call" | custom-call | tf_op jit(solution)/shard_map/pallas_call | solution.py:442
  30.3 1.9 %shard_map.99.basis_ref = bf16[12,8,16,1024]{3,2,1,0:T(8,128)(2,1)S(1)} custom-call(f32[136,128]{1,0:T(8,128)S(1)} %get-tuple-element.28.after_ref, bf16[12,8,16,1024]{3,2,1,0:T(8,128)(2,1)} %bitcast.17), custom_call_target="tpu_custom_call" | custom-call | tf_op jit(solution)/shard_map/pallas_call | solution.py:456
  32.2 0.0 collective-permute-done.3.h2_ref
  32.2 0.0 collective-permute-done.2.h1_ref
  32.2 0.0 collective-permute-done.1.f_ref
  32.2 1.4 %shard_map.101 = (f32[8,128,128]{2,1,0:T(8,128)S(1)}, f32[32,2,128]{2,1,0:T(2,128)S(1)}) custom-call(f32[8,128,128]{2,1,0:T(8,128)S(1)} %shard_map.97.still_ref, f32[8,128,128]{2,1,0:T(8,128)S(1)} %get-tuple-element.18.x_ref.x0_ref, f32[8,64,128]{2,1,0:T(8,128)S(1)} %collective-permute-done.1.f_ref, f32[136,128]{1,0:T(8,128)S(1)} %collective-permute-done.2.h1_ref, ...), custom_call_target="tpu_custom_call" | custom-call | tf_op jit(solution)/shard_map/pallas_call | solution.py:466
  33.7 9.8 %all_to_all.10.sums_ref = f32[32,2,128]{2,1,0:T(2,128)S(1)} all-to-all(f32[32,2,128]{2,1,0:T(2,128)S(1)} %get-tuple-element.31), channel_id=1, replica_groups=mesh['comp'=2,'tile'=16] {'comp','tile'}, dimensions={0} | all-to-all | bytes 65536 | tf_op jit(solution)/shard_map/all_to_all | solution.py:473
  43.5 1.8 %shard_map.102 = (f32[128,1024]{1,0:T(8,128)}, f32[1,12]{1,0:T(1,128)}) custom-call(f32[8,128,128]{2,1,0:T(8,128)S(1)} %get-tuple-element.30.x_ref, bf16[12,8,16,1024]{3,2,1,0:T(8,128)(2,1)S(1)} %shard_map.99.basis_ref, f32[32,2,128]{2,1,0:T(2,128)S(1)} %all_to_all.10.sums_ref), custom_call_target="tpu_custom_call" | custom-call | tf_op jit(solution)/shard_map/pallas_call | solution.py:474
Async XLA Ops:
  2.8 18.2 %all-to-all-start = ((f32[16,32,128]{2,1,0:T(8,128)}), f32[16,32,128]{2,1,0:T(8,128)S(1)}, u32[]{:S(2)}, u32[]{:S(2)}) async-start(f32[16,32,128]{2,1,0:T(8,128)} %bitcast.9), calls=%async_computation | async-start | bytes 524288 | tf_op jit(solution)/shard_map/all_to_all | solution.py:421
  11.4 1.5 %collective-permute-start = (f32[400,128]{1,0:T(8,128)S(1)}, f32[400,128]{1,0:T(8,128)S(1)}, u32[]{:S(2)}, u32[]{:S(2)}) collective-permute-start(f32[400,128]{1,0:T(8,128)S(1)} %get-tuple-element.26), channel_id=1, source_target_pairs={{0,16},{16,0},{1,17},{17,1},{2,18},{18,2},{3,19},{19,3},{4,20},{20... | collective-permute-start | bytes 614408 | tf_op jit(solution)/shard_map/ppermute | solution.py:431
  21.3 11.0 %collective-permute-start.1 = (f32[8,64,128]{2,1,0:T(8,128)S(1)}, f32[8,64,128]{2,1,0:T(8,128)S(1)}, u32[]{:S(2)}, u32[]{:S(2)}) collective-permute-start(f32[8,64,128]{2,1,0:T(8,128)S(1)} %get-tuple-element.27), channel_id=1, source_target_pairs={{0,16},{16,0},{1,17},{17,1},{2,18},{18,2},{3,19},{19,3},{4,20},{20... | collective-permute-start | bytes 786440 | tf_op jit(solution)/shard_map/ppermute | solution.py:463
  21.3 10.9 %collective-permute-start.3 = (f32[136,128]{1,0:T(8,128)S(1)}, f32[136,128]{1,0:T(8,128)S(1)}, u32[]{:S(2)}, u32[]{:S(2)}) collective-permute-start(f32[136,128]{1,0:T(8,128)S(1)} %get-tuple-element.29), channel_id=1, source_target_pairs={{1,18},{2,17},{3,20},{4,19},{5,22},{6,21},{7,24},{8,23},{9,26},{10... | collective-permute-start | bytes 208904 | tf_op jit(solution)/shard_map/ppermute | solution.py:465
  22.0 10.2 %collective-permute-start.2 = (f32[136,128]{1,0:T(8,128)S(1)}, f32[136,128]{1,0:T(8,128)S(1)}, u32[]{:S(2)}, u32[]{:S(2)}) collective-permute-start(f32[136,128]{1,0:T(8,128)S(1)} %get-tuple-element.28.after_ref), channel_id=1, source_target_pairs={{0,17},{1,16},{2,19},{3,18},{4,21},{5,20},{6,23},{7,22},{8,25},{9,... | collective-permute-start | bytes 208904 | tf_op jit(solution)/shard_map/ppermute | solution.py:464

commit v6 on v5

--- a/solution.py
+++ b/solution.py
@@ -47,7 +47,7 @@
     return lax.div(b, per), lax.rem(b, per)
 
 
-def gather_kernel(rows, index_ref, state_ref, *refs):
+def gather_kernel(rows, lead, index_ref, state_ref, *refs):
     small = (len(refs) - 4) // 2
     sides, out_ref, x_ref = refs[:small], refs[small], refs[small + 1]
     side_outs, (rows_ref, sems) = refs[small + 2 : 2 * small + 2], refs[2 * small + 2 :]
@@ -74,11 +74,13 @@
     for copy in copies[:per]:
         copy.wait()
 
-    def band(d, carry):
+    def band(n, carry):
+        d = n + lead
+        d = jnp.where(d >= bands, d - bands, d)
         for j in range(cap):
             r, c = block_place(rows_ref[j, d], per)
             piece = x_ref[c, pl.ds(r, FLUX, stride=rows), :]
-            out_ref[pl.ds(d * (cap * FLUX) + j, FLUX, stride=cap), :] = piece
+            out_ref[pl.ds(n * (cap * FLUX) + j, FLUX, stride=cap), :] = piece
         return carry
 
     lax.fori_loop(0, bands, band, 0, unroll=2)
@@ -139,7 +141,7 @@
 
 
 def early_kernel(
-    rows, slots_ref, weights_ref, x_ref, kappa_ref, mask_ref, vmix_ref,
+    rows, skip, slots_ref, weights_ref, x_ref, kappa_ref, mask_ref, vmix_ref,
     pack_ref, table_ref,
 ):
     over, blocks = slots_ref.shape
@@ -147,7 +149,8 @@
     levels = x_ref.shape[1] // rows
     size = payload_rows(levels, per)
     slots = (pack_ref.shape[0] - 2 * size) // blocks * LANES
-    row = lax.broadcasted_iota(jnp.int32, (slots, blocks), 0)
+    row = lax.broadcasted_iota(jnp.int32, (slots, blocks), 0) + skip
+    row = jnp.where(row >= slots, row - slots, row)
     mat = jnp.zeros((slots, blocks), jnp.float32)
     for k in range(over):
         mat = mat + jnp.where(slots_ref[k : k + 1, :] == row, weights_ref[k : k + 1, :], 0.0)
@@ -407,8 +410,9 @@
         return [((c * bands) + i, (c ^ 1) * bands + k) for c in range(comps) for i, k in pairs]
 
     sides = (kap, land_mask, recv_slots[0, 0].T, recv_weights[0, 0].T, vm)
+    lead = bands * 5 // 16
     bucket, columns, kap, land_mask, slots, weights, vm = call(
-        functools.partial(gather_kernel, rows),
+        functools.partial(gather_kernel, rows, lead),
         (jax.ShapeDtypeStruct((bands * FLUX * cap, LANES), f32), field)
         + tuple(jax.ShapeDtypeStruct(a.shape, a.dtype) for a in sides),
         [HBM] * (2 + len(sides)),
@@ -418,9 +422,12 @@
             pltpu.SemaphoreType.DMA((2 * per + 1 + len(sides),)),
         ),
     )(*[in_hbm(a) for a in (send_rows[0, 0].T, flat) + sides])
-    moved = lax.all_to_all(bucket.reshape(bands, FLUX * cap, LANES), "tile", 0, 0)
+    group = [(lead + n) % bands for n in range(bands)]
+    moved = lax.all_to_all(
+        bucket.reshape(bands, FLUX * cap, LANES), "tile", 0, 0, axis_index_groups=[group]
+    )
     pack, table = call(
-        functools.partial(early_kernel, rows),
+        functools.partial(early_kernel, rows, lead * cap),
         (
             jax.ShapeDtypeStruct((bands * cap // LANES * blocks + 2 * pay.shape[0], LANES), f32),
             jax.ShapeDtypeStruct((levels * levels, LANES), f32),

time: 45.7 us -> 44.8 us (0.980)
  waiting for transfers between devices: 9.51 us -> 7.46 us
  blocking collectives: 9.83 us -> 10.7 us
    all_to_all x1, waiting for transfers between devices: 8.06 us -> 6.01 us  [body(): lax.all_to_all(bucket.reshape(bands, FLUX * cap, LANES), 'tile', 0, 0, ax...]
    all_to_all x1, blocking collectives: 9.83 us -> 10.7 us  [body(): sums = lax.all_to_all(sums, ('comp', 'tile'), 0, 0)]
    all_to_all x1, starting transfers between devices: 8.35 us -> 8.83 us  [body(): lax.all_to_all(bucket.reshape(bands, FLUX * cap, LANES), 'tile', 0, 0, ax...]
where the time goes in v6:
time: 44.8 us; the launch traced here: 44.5 us
  starting transfers between devices  12.8 us (29%)
  Pallas kernels  12.7 us (28%)
  blocking collectives  10.7 us (24%)
  waiting for transfers between devices  7.46 us (17%)
  between operations  0.73 us (2%)
    all_to_all x1, blocking collectives, body(): sums = lax.all_to_all(sums, ('comp', 'tile'), 0, 0)  10.7 us
    all_to_all x1, starting transfers between devices, body(): lax.all_to_all(bucket.reshape(bands, FLUX * cap, LANES), 'tile', 0, 0, ax...  8.83 us
    all_to_all x1, waiting for transfers between devices, body(): lax.all_to_all(bucket.reshape(bands, FLUX * cap, LANES), 'tile', 0, 0, ax...  6.01 us
    pallas_call x1, Pallas kernels, body(): call(gram_kernel, jax.ShapeDtypeStruct((2, LANES), f32), [HBM], VMEM, scr...  3.61 us
    ppermute x1, starting transfers between devices, body(): edge1 = lax.ppermute(edge1, ('comp', 'tile'), crossed(pairs1))  3.2 us
    pallas_call x1, Pallas kernels, body(): call(functools.partial(gather_kernel, rows, lead), (jax.ShapeDtypeStruct(...  2.13 us
    pallas_call x1, Pallas kernels, body(): call(fetch_kernel, jax.ShapeDtypeStruct(vectors.shape, vectors.dtype), [p...  1.93 us
    pallas_call x1, Pallas kernels, body(): call(functools.partial(finish_kernel, rows, total), (jax.ShapeDtypeStruct...  1.85 us
  transfers between devices with their start and end apart: 5, of which 2 were waited for; matrix products, arithmetic and copies ran while one was open for 0% of the time, Pallas kernels for 16%

profile of v6, /device:TPU:0, one launch (start us, length us, event | category | flops | bytes accessed | tf_op | source)
XLA Modules:
  0.0 44.5 jit_solution(5215393126123684854)
XLA Ops:
  0.6 2.1 %shard_map.95 = (f32[512,128]{1,0:T(8,128)}, f32[8,128,128]{2,1,0:T(8,128)S(1)}, f32[16,1024]{1,0:T(8,128)S(1)}, s32[16,1024]{1,0:T(8,128)S(1)}, s32[4,128]{1,0:...) custom-call(s32[8,16]{1,0:T(8,128)} %bitcast.20, f32[128,1024]{1,0:T(8,128)} %bitcast.18, f32[16,1024]{1,0:T(8,128)} %bitcast.19, ...), custom_call_target="tpu_custom_call" | custom-call | tf_op jit(solution)/shard_map/pallas_call | solution.py:414
  2.8 8.8 %all-to-all-start = ((f32[16,32,128]{2,1,0:T(8,128)}), f32[16,32,128]{2,1,0:T(8,128)S(1)}, u32[]{:S(2)}, u32[]{:S(2)}) async-start(f32[16,32,128]{2,1,0:T(8,128)} %bitcast.9), calls=%async_computation | async-start | bytes 524288 | tf_op jit(solution)/shard_map/all_to_all | solution.py:426
  11.6 0.3 shard_map.96
  11.9 0.1 collective-permute-start
  12.0 1.4 %collective-permute-done.pack_ref = f32[400,128]{1,0:T(8,128)S(1)} collective-permute-done((f32[400,128]{1,0:T(8,128)S(1)}, f32[400,128]{1,0:T(8,128)S(1)}, u32[]{:S(2)}, u32[]{:S(2)}) %collective-permute-start) | collective-permute-done | bytes 204832 | tf_op jit(solution)/shard_map/ppermute | solution.py:438
  13.4 6.0 %all-to-all-done.buf_ref = f32[16,32,128]{2,1,0:T(8,128)S(1)} async-done(((f32[16,32,128]{2,1,0:T(8,128)}), f32[16,32,128]{2,1,0:T(8,128)S(1)}, u32[]{:S(2)}, u32[]{:S(2)}) %all-to-all-start) | async-done | bytes 262176 | tf_op jit(solution)/shard_map/all_to_all | solution.py:426
  19.4 0.3 shard_map.98
  19.7 0.1 collective-permute-start.1
  19.8 0.7 %collective-permute-start.3 = (f32[136,128]{1,0:T(8,128)S(1)}, f32[136,128]{1,0:T(8,128)S(1)}, u32[]{:S(2)}, u32[]{:S(2)}) collective-permute-start(f32[136,128]{1,0:T(8,128)S(1)} %get-tuple-element.29), channel_id=1, source_target_pairs={{1,18},{2,17},{3,20},{4,19},{5,22},{6,21},{7,24},{8,23},{9,26},{10... | collective-permute-start | bytes 208904 | tf_op jit(solution)/shard_map/ppermute | solution.py:472
  20.4 3.2 %collective-permute-start.2 = (f32[136,128]{1,0:T(8,128)S(1)}, f32[136,128]{1,0:T(8,128)S(1)}, u32[]{:S(2)}, u32[]{:S(2)}) collective-permute-start(f32[136,128]{1,0:T(8,128)S(1)} %get-tuple-element.28.after_ref), channel_id=1, source_target_pairs={{0,17},{1,16},{2,19},{3,18},{4,21},{5,20},{6,23},{7,22},{8,25},{9,... | collective-permute-start | bytes 208904 | tf_op jit(solution)/shard_map/ppermute | solution.py:471
  23.6 3.6 %shard_map.100.gram_ref = f32[2,128]{1,0:T(2,128)S(1)} custom-call(bf16[12,8,16,1024]{3,2,1,0:T(8,128)(2,1)} %bitcast.16), custom_call_target="tpu_custom_call" | custom-call | tf_op jit(solution)/shard_map/pallas_call | solution.py:439
  27.3 1.2 %shard_map.97.still_ref = f32[8,128,128]{2,1,0:T(8,128)S(1)} custom-call(f32[8,128,128]{2,1,0:T(8,128)S(1)} %get-tuple-element.18.x_ref.x0_ref, f32[16,1024]{1,0:T(8,128)S(1)} %get-tuple-element.19.kappa_ref, s32[16,1024]{1,0:T(8,128)S(1)} %get-tuple-element.20.mask_ref, f32[64,128]{1,0:T(8,128)S(1)} %get-tuple-element.24.table_ref), custom_call_target="tpu_custom_call" | custom-call | tf_op jit(solution)/shard_map/pallas_call | solution.py:449
  28.5 1.9 %shard_map.99.basis_ref = bf16[12,8,16,1024]{3,2,1,0:T(8,128)(2,1)S(1)} custom-call(f32[136,128]{1,0:T(8,128)S(1)} %get-tuple-element.28.after_ref, bf16[12,8,16,1024]{3,2,1,0:T(8,128)(2,1)} %bitcast.17), custom_call_target="tpu_custom_call" | custom-call | tf_op jit(solution)/shard_map/pallas_call | solution.py:463
  30.4 0.0 collective-permute-done.3.h2_ref
  30.4 0.0 collective-permute-done.2.h1_ref
  30.4 0.0 collective-permute-done.1.f_ref
  30.4 1.4 %shard_map.101 = (f32[8,128,128]{2,1,0:T(8,128)S(1)}, f32[32,2,128]{2,1,0:T(2,128)S(1)}) custom-call(f32[8,128,128]{2,1,0:T(8,128)S(1)} %shard_map.97.still_ref, f32[8,128,128]{2,1,0:T(8,128)S(1)} %get-tuple-element.18.x_ref.x0_ref, f32[8,64,128]{2,1,0:T(8,128)S(1)} %collective-permute-done.1.f_ref, f32[136,128]{1,0:T(8,128)S(1)} %collective-permute-done.2.h1_ref, ...), custom_call_target="tpu_custom_call" | custom-call | tf_op jit(solution)/shard_map/pallas_call | solution.py:473
  31.9 10.7 %all_to_all.10.sums_ref = f32[32,2,128]{2,1,0:T(2,128)S(1)} all-to-all(f32[32,2,128]{2,1,0:T(2,128)S(1)} %get-tuple-element.31), channel_id=1, replica_groups=mesh['comp'=2,'tile'=16] {'comp','tile'}, dimensions={0} | all-to-all | bytes 65536 | tf_op jit(solution)/shard_map/all_to_all | solution.py:480
  42.6 1.8 %shard_map.102 = (f32[128,1024]{1,0:T(8,128)}, f32[1,12]{1,0:T(1,128)}) custom-call(f32[8,128,128]{2,1,0:T(8,128)S(1)} %get-tuple-element.30.x_ref, bf16[12,8,16,1024]{3,2,1,0:T(8,128)(2,1)S(1)} %shard_map.99.basis_ref, f32[32,2,128]{2,1,0:T(2,128)S(1)} %all_to_all.10.sums_ref), custom_call_target="tpu_custom_call" | custom-call | tf_op jit(solution)/shard_map/pallas_call | solution.py:481
Async XLA Ops:
  2.8 16.6 %all-to-all-start = ((f32[16,32,128]{2,1,0:T(8,128)}), f32[16,32,128]{2,1,0:T(8,128)S(1)}, u32[]{:S(2)}, u32[]{:S(2)}) async-start(f32[16,32,128]{2,1,0:T(8,128)} %bitcast.9), calls=%async_computation | async-start | bytes 524288 | tf_op jit(solution)/shard_map/all_to_all | solution.py:426
  11.9 1.5 %collective-permute-start = (f32[400,128]{1,0:T(8,128)S(1)}, f32[400,128]{1,0:T(8,128)S(1)}, u32[]{:S(2)}, u32[]{:S(2)}) collective-permute-start(f32[400,128]{1,0:T(8,128)S(1)} %get-tuple-element.26), channel_id=1, source_target_pairs={{0,16},{16,0},{1,17},{17,1},{2,18},{18,2},{3,19},{19,3},{4,20},{20... | collective-permute-start | bytes 614408 | tf_op jit(solution)/shard_map/ppermute | solution.py:438
  19.7 10.8 %collective-permute-start.1 = (f32[8,64,128]{2,1,0:T(8,128)S(1)}, f32[8,64,128]{2,1,0:T(8,128)S(1)}, u32[]{:S(2)}, u32[]{:S(2)}) collective-permute-start(f32[8,64,128]{2,1,0:T(8,128)S(1)} %get-tuple-element.27), channel_id=1, source_target_pairs={{0,16},{16,0},{1,17},{17,1},{2,18},{18,2},{3,19},{19,3},{4,20},{20... | collective-permute-start | bytes 786440 | tf_op jit(solution)/shard_map/ppermute | solution.py:470
  19.8 10.7 %collective-permute-start.3 = (f32[136,128]{1,0:T(8,128)S(1)}, f32[136,128]{1,0:T(8,128)S(1)}, u32[]{:S(2)}, u32[]{:S(2)}) collective-permute-start(f32[136,128]{1,0:T(8,128)S(1)} %get-tuple-element.29), channel_id=1, source_target_pairs={{1,18},{2,17},{3,20},{4,19},{5,22},{6,21},{7,24},{8,23},{9,26},{10... | collective-permute-start | bytes 208904 | tf_op jit(solution)/shard_map/ppermute | solution.py:472
  20.4 10.0 %collective-permute-start.2 = (f32[136,128]{1,0:T(8,128)S(1)}, f32[136,128]{1,0:T(8,128)S(1)}, u32[]{:S(2)}, u32[]{:S(2)}) collective-permute-start(f32[136,128]{1,0:T(8,128)S(1)} %get-tuple-element.28.after_ref), channel_id=1, source_target_pairs={{0,17},{1,16},{2,19},{3,18},{4,21},{5,20},{6,23},{7,22},{8,25},{9,... | collective-permute-start | bytes 208904 | tf_op jit(solution)/shard_map/ppermute | solution.py:471

commit v7 on v6

--- a/solution.py
+++ b/solution.py
@@ -13,16 +13,18 @@
 HBM = pl.BlockSpec(memory_space=pltpu.HBM)
 VMEM = pl.BlockSpec(memory_space=pltpu.VMEM)
 LIMIT = 24 << 20
-
-
-def call(kernel, outs, in_specs, out_specs, scratch=(), cost=None):
+PUTS = 4
+OUTPARTS = 4
+
+
+def call(kernel, outs, in_specs, out_specs, scratch=(), aliases={}):
     return pl.pallas_call(
         kernel,
         out_shape=outs,
         in_specs=in_specs,
         out_specs=out_specs,
         scratch_shapes=list(scratch),
-        cost_estimate=cost,
+        input_output_aliases=aliases,
         compiler_params=pltpu.CompilerParams(vmem_limit_bytes=LIMIT),
     )
 
@@ -48,9 +50,9 @@
 
 
 def gather_kernel(rows, lead, index_ref, state_ref, *refs):
-    small = (len(refs) - 4) // 2
-    sides, out_ref, x_ref = refs[:small], refs[small], refs[small + 1]
-    side_outs, (rows_ref, sems) = refs[small + 2 : 2 * small + 2], refs[2 * small + 2 :]
+    small = (len(refs) - 5) // 2
+    sides, out_hbm, x_ref = refs[:small], refs[small], refs[small + 1]
+    side_outs, (rows_ref, out_ref, sems) = refs[small + 2 : 2 * small + 2], refs[2 * small + 2 :]
     cap, bands = rows_ref.shape
     per = x_ref.shape[0]
     top = FLUX * rows
@@ -83,7 +85,16 @@
             out_ref[pl.ds(n * (cap * FLUX) + j, FLUX, stride=cap), :] = piece
         return carry
 
-    lax.fori_loop(0, bands, band, 0, unroll=2)
+    span = bands // OUTPARTS
+    size = span * cap * FLUX
+    for p in range(OUTPARTS):
+        lax.fori_loop(p * span, (p + 1) * span, band, 0, unroll=2)
+        part = slice(p * size, (p + 1) * size)
+        copy = pltpu.make_async_copy(
+            out_ref.at[part, :], out_hbm.at[part, :], sems.at[2 * per + 1 + small + p]
+        )
+        copy.start()
+        copies.append(copy)
     for copy in copies[per:]:
         copy.wait()
 
@@ -269,18 +280,13 @@
     advance(x1_ref, x_ref)
 
 
-def step_kernel(
-    rows, still_ref, x0_ref, f_ref, h1_ref, h2_ref, kappa_ref, mask_ref, vmix_ref, table_ref,
-    basis_ref, gram_ref, x_ref, sums_ref, f1_ref,
-):
+def forced_kernel(rows, still_ref, f_ref, kappa_ref, mask_ref, table_ref, x_ref, f1_ref):
     per = still_ref.shape[0]
     levels = still_ref.shape[1] // rows
-    vecs = basis_ref.shape[0]
     ocean = lax.axis_index("comp") == 0
-    even = lax.rem(lax.axis_index("tile"), 2) == 0
-
-    def mask(c, part=slice(None)):
-        m = mask_ref[part, c * LANES : (c + 1) * LANES].astype(jnp.float32)
+
+    def mask(c):
+        m = mask_ref[:, c * LANES : (c + 1) * LANES].astype(jnp.float32)
         return jnp.where(ocean, m, 1.0)
 
     for c in range(per):
@@ -299,6 +305,21 @@
                 v = table_ref[l * levels + q : l * levels + q + 1, :]
                 acc = acc + v * f1_ref[c, q * rows : (q + 1) * rows, :]
             x_ref[c, part, :] = still_ref[c, part, :] + mask(c) * acc
+
+
+def step_kernel(
+    rows, most_ref, x0_ref, h1_ref, h2_ref, kappa_ref, mask_ref, vmix_ref,
+    basis_ref, gram_ref, x_ref, sums_ref,
+):
+    per = x_ref.shape[0]
+    levels = x_ref.shape[1] // rows
+    vecs = basis_ref.shape[0]
+    ocean = lax.axis_index("comp") == 0
+    even = lax.rem(lax.axis_index("tile"), 2) == 0
+
+    def mask(c, part):
+        m = mask_ref[part, c * LANES : (c + 1) * LANES].astype(jnp.float32)
+        return jnp.where(ocean, m, 1.0)
 
     vmix = vmix_ref[...]
     for side, edge, inner in ((0, 0, 1), (1, rows - 1, rows - 2)):
@@ -350,7 +371,9 @@
         sums_ref[d] = block
 
 
-def finish_kernel(rows, total, x_ref, basis_ref, sums_ref, out_ref, coef_ref):
+def finish_kernel(
+    rows, total, x_ref, basis_ref, sums_ref, out_hbm, coef_hbm, out_ref, coef_ref, sems
+):
     per = x_ref.shape[0]
     levels = x_ref.shape[1] // rows
     vecs = basis_ref.shape[0]
@@ -359,6 +382,8 @@
     tail = pltpu.roll(sums[1:2, :], 64, 1)
     coef = jnp.where(lane < vecs, tail, 0.0) / total
     coef_ref[...] = coef[:, :vecs]
+    copies = [pltpu.make_async_copy(coef_ref, coef_hbm, sems.at[PUTS])]
+    copies[0].start()
     square = jnp.sum(jnp.where(lane == vecs, tail, 0.0), axis=1, keepdims=True)
     splat = [jnp.sum(jnp.where(lane == i, coef, 0.0), axis=1, keepdims=True) for i in range(vecs)]
     quad = jnp.zeros((1, LANES), jnp.float32)
@@ -382,7 +407,15 @@
             out_ref[pl.ds(l * rows, rows), s] = x.reshape(rows, LANES)
         return carry
 
-    lax.fori_loop(0, levels, level, 0)
+    span = levels // PUTS
+    for p in range(PUTS):
+        lax.fori_loop(p * span, (p + 1) * span, level, 0)
+        part = slice(p * span * rows, (p + 1) * span * rows)
+        copy = pltpu.make_async_copy(out_ref.at[part, :], out_hbm.at[part, :], sems.at[p])
+        copy.start()
+        copies.append(copy)
+    for copy in copies:
+        copy.wait()
 
 
 def body(state, basis, kappa, vmix, land_mask, send_rows, recv_slots, recv_weights):
@@ -416,10 +449,11 @@
         (jax.ShapeDtypeStruct((bands * FLUX * cap, LANES), f32), field)
         + tuple(jax.ShapeDtypeStruct(a.shape, a.dtype) for a in sides),
         [HBM] * (2 + len(sides)),
-        (VMEM,) * (2 + len(sides)),
+        (HBM,) + (VMEM,) * (1 + len(sides)),
         scratch=(
             pltpu.SMEM((cap, bands), jnp.int32),
-            pltpu.SemaphoreType.DMA((2 * per + 1 + len(sides),)),
+            pltpu.VMEM((bands * FLUX * cap, LANES), f32),
+            pltpu.SemaphoreType.DMA((2 * per + 1 + len(sides) + OUTPARTS,)),
         ),
     )(*[in_hbm(a) for a in (send_rows[0, 0].T, flat) + sides])
     group = [(lead + n) % bands for n in range(bands)]
@@ -470,13 +504,20 @@
     imported = lax.ppermute(foreign, "comp", swap)
     edge1 = lax.ppermute(edge1, ("comp", "tile"), crossed(pairs1))
     edge2 = lax.ppermute(edge2, ("comp", "tile"), crossed(pairs2))
+    most = call(
+        functools.partial(forced_kernel, rows),
+        field,
+        [VMEM] * 5,
+        VMEM,
+        scratch=(pltpu.VMEM((per, FLUX * rows, LANES), f32),),
+    )(still, imported, kap, land_mask, table)
     x, sums = call(
         functools.partial(step_kernel, rows),
         (field, jax.ShapeDtypeStruct((devices, 2, LANES), f32)),
-        [VMEM] * 11,
+        [VMEM] * 9,
         (VMEM, VMEM),
-        scratch=(pltpu.VMEM((per, FLUX * rows, LANES), f32),),
-    )(still, columns, imported, edge1, edge2, kap, land_mask, vm, table, vectors, gram)
+        aliases={0: 0},
+    )(most, columns, edge1, edge2, kap, land_mask, vm, vectors, gram)
     sums = lax.all_to_all(sums, ("comp", "tile"), 0, 0)
     direction, coefs = call(
         functools.partial(finish_kernel, rows, total),
@@ -485,7 +526,12 @@
             jax.ShapeDtypeStruct((1, vecs), f32),
         ),
         [VMEM] * 3,
-        (VMEM, VMEM),
+        (HBM, HBM),
+        scratch=(
+            pltpu.VMEM((levels * rows, cols), f32),
+            pltpu.VMEM((1, vecs), f32),
+            pltpu.SemaphoreType.DMA((PUTS + 1,)),
+        ),
     )(x, vectors, sums)
     return direction.reshape(1, levels, rows, cols), coefs.reshape(vecs)
 

time: 44.8 us -> 44.6 us (level)
  transfers between devices with their start and end apart: 5 -> 5, of which waited for: 2 -> 2; matrix products, arithmetic and copies ran while one was open for 0% -> 0% of each run, Pallas kernels for 16% -> 17%
where the time goes in v7:
time: 44.6 us; the launch traced here: 44.3 us
  starting transfers between devices  12.8 us (29%)
  Pallas kernels  12.5 us (28%)
  blocking collectives  10.7 us (24%)
  waiting for transfers between devices  7.46 us (17%)
  between operations  0.73 us (2%)
    all_to_all x1, blocking collectives, body(): sums = lax.all_to_all(sums, ('comp', 'tile'), 0, 0)  10.7 us
    all_to_all x1, starting transfers between devices, body(): lax.all_to_all(bucket.reshape(bands, FLUX * cap, LANES), 'tile', 0, 0, ax...  8.83 us
    all_to_all x1, waiting for transfers between devices, body(): lax.all_to_all(bucket.reshape(bands, FLUX * cap, LANES), 'tile', 0, 0, ax...  6.01 us
    pallas_call x1, Pallas kernels, body(): call(gram_kernel, jax.ShapeDtypeStruct((2, LANES), f32), [HBM], VMEM, scr...  3.61 us
    ppermute x1, starting transfers between devices, body(): edge1 = lax.ppermute(edge1, ('comp', 'tile'), crossed(pairs1))  3.2 us
    pallas_call x1, Pallas kernels, body(): call(functools.partial(gather_kernel, rows, lead), (jax.ShapeDtypeStruct(...  2.07 us
    pallas_call x1, Pallas kernels, body(): call(fetch_kernel, jax.ShapeDtypeStruct(vectors.shape, vectors.dtype), [p...  1.93 us
    pallas_call x1, Pallas kernels, body(): call(functools.partial(finish_kernel, rows, total), (jax.ShapeDtypeStruct...  1.73 us
  transfers between devices with their start and end apart: 5, of which 2 were waited for; matrix products, arithmetic and copies ran while one was open for 0% of the time, Pallas kernels for 17%

profile of v7, /device:TPU:0, one launch (start us, length us, event | category | flops | bytes accessed | tf_op | source)
XLA Modules:
  0.0 44.3 jit_solution(2263450350778685713)
XLA Ops:
  0.6 2.1 %shard_map.95 = (f32[512,128]{1,0:T(8,128)}, f32[8,128,128]{2,1,0:T(8,128)S(1)}, f32[16,1024]{1,0:T(8,128)S(1)}, s32[16,1024]{1,0:T(8,128)S(1)}, s32[4,128]{1,0:...) custom-call(s32[8,16]{1,0:T(8,128)} %bitcast.20, f32[128,1024]{1,0:T(8,128)} %bitcast.18, f32[16,1024]{1,0:T(8,128)} %bitcast.19, ...), custom_call_target="tpu_custom_call" | custom-call | tf_op jit(solution)/shard_map/pallas_call | solution.py:447
  2.7 8.8 %all-to-all-start = ((f32[16,32,128]{2,1,0:T(8,128)}), f32[16,32,128]{2,1,0:T(8,128)S(1)}, u32[]{:S(2)}, u32[]{:S(2)}) async-start(f32[16,32,128]{2,1,0:T(8,128)} %bitcast.9), calls=%async_computation | async-start | bytes 524288 | tf_op jit(solution)/shard_map/all_to_all | solution.py:460
  11.5 0.3 shard_map.96
  11.8 0.1 collective-permute-start
  11.9 1.4 %collective-permute-done.pack_ref = f32[400,128]{1,0:T(8,128)S(1)} collective-permute-done((f32[400,128]{1,0:T(8,128)S(1)}, f32[400,128]{1,0:T(8,128)S(1)}, u32[]{:S(2)}, u32[]{:S(2)}) %collective-permute-start) | collective-permute-done | bytes 204832 | tf_op jit(solution)/shard_map/ppermute | solution.py:472
  13.3 6.0 %all-to-all-done.buf_ref = f32[16,32,128]{2,1,0:T(8,128)S(1)} async-done(((f32[16,32,128]{2,1,0:T(8,128)}), f32[16,32,128]{2,1,0:T(8,128)S(1)}, u32[]{:S(2)}, u32[]{:S(2)}) %all-to-all-start) | async-done | bytes 262176 | tf_op jit(solution)/shard_map/all_to_all | solution.py:460
  19.3 0.3 shard_map.98
  19.6 0.1 collective-permute-start.1
  19.7 0.7 %collective-permute-start.3 = (f32[136,128]{1,0:T(8,128)S(1)}, f32[136,128]{1,0:T(8,128)S(1)}, u32[]{:S(2)}, u32[]{:S(2)}) collective-permute-start(f32[136,128]{1,0:T(8,128)S(1)} %get-tuple-element.29), channel_id=1, source_target_pairs={{1,18},{2,17},{3,20},{4,19},{5,22},{6,21},{7,24},{8,23},{9,26},{10... | collective-permute-start | bytes 208904 | tf_op jit(solution)/shard_map/ppermute | solution.py:506
  20.4 3.2 %collective-permute-start.2 = (f32[136,128]{1,0:T(8,128)S(1)}, f32[136,128]{1,0:T(8,128)S(1)}, u32[]{:S(2)}, u32[]{:S(2)}) collective-permute-start(f32[136,128]{1,0:T(8,128)S(1)} %get-tuple-element.28.after_ref), channel_id=1, source_target_pairs={{0,17},{1,16},{2,19},{3,18},{4,21},{5,20},{6,23},{7,22},{8,25},{9,... | collective-permute-start | bytes 208904 | tf_op jit(solution)/shard_map/ppermute | solution.py:505
  23.6 3.6 %shard_map.101.gram_ref = f32[2,128]{1,0:T(2,128)S(1)} custom-call(bf16[12,8,16,1024]{3,2,1,0:T(8,128)(2,1)} %bitcast.16), custom_call_target="tpu_custom_call" | custom-call | tf_op jit(solution)/shard_map/pallas_call | solution.py:473
  27.2 1.2 %shard_map.97.still_ref = f32[8,128,128]{2,1,0:T(8,128)S(1)} custom-call(f32[8,128,128]{2,1,0:T(8,128)S(1)} %get-tuple-element.18.x_ref.x0_ref, f32[16,1024]{1,0:T(8,128)S(1)} %get-tuple-element.19.kappa_ref, s32[16,1024]{1,0:T(8,128)S(1)} %get-tuple-element.20.mask_ref, f32[64,128]{1,0:T(8,128)S(1)} %get-tuple-element.24.table_ref), custom_call_target="tpu_custom_call" | custom-call | tf_op jit(solution)/shard_map/pallas_call | solution.py:483
  28.4 1.9 %shard_map.100.basis_ref = bf16[12,8,16,1024]{3,2,1,0:T(8,128)(2,1)S(1)} custom-call(f32[136,128]{1,0:T(8,128)S(1)} %get-tuple-element.28.after_ref, bf16[12,8,16,1024]{3,2,1,0:T(8,128)(2,1)} %bitcast.17), custom_call_target="tpu_custom_call" | custom-call | tf_op jit(solution)/shard_map/pallas_call | solution.py:497
  30.4 0.0 collective-permute-done.1.f_ref
  30.4 0.4 shard_map.99.most_ref
  30.7 0.0 collective-permute-done.3.h2_ref
  30.7 0.0 collective-permute-done.2.h1_ref
  30.7 1.0 %shard_map.102 = (f32[8,128,128]{2,1,0:T(8,128)S(1)}, f32[32,2,128]{2,1,0:T(2,128)S(1)}) custom-call(f32[8,128,128]{2,1,0:T(8,128)S(1)} %shard_map.99.most_ref, f32[8,128,128]{2,1,0:T(8,128)S(1)} %get-tuple-element.18.x_ref.x0_ref, f32[136,128]{1,0:T(8,128)S(1)} %collective-permute-done.2.h1_ref, ...), custom_call_target="tpu_custom_call", output_to_operand_aliasing={{0}: (0, {})} | custom-call | tf_op jit(solution)/shard_map/pallas_call | solution.py:514
  31.8 10.7 %all_to_all.10.sums_ref = f32[32,2,128]{2,1,0:T(2,128)S(1)} all-to-all(f32[32,2,128]{2,1,0:T(2,128)S(1)} %get-tuple-element.31), channel_id=1, replica_groups=mesh['comp'=2,'tile'=16] {'comp','tile'}, dimensions={0} | all-to-all | bytes 65536 | tf_op jit(solution)/shard_map/all_to_all | solution.py:521
  42.5 1.7 %shard_map.103 = (f32[128,1024]{1,0:T(8,128)}, f32[1,12]{1,0:T(1,128)}) custom-call(f32[8,128,128]{2,1,0:T(8,128)S(1)} %get-tuple-element.30.x_ref, bf16[12,8,16,1024]{3,2,1,0:T(8,128)(2,1)S(1)} %shard_map.100.basis_ref, f32[32,2,128]{2,1,0:T(2,128)S(1)} %all_to_all.10.sums_ref), custom_call_target="tpu_custom_call" | custom-call | tf_op jit(solution)/shard_map/pallas_call | solution.py:522
Async XLA Ops:
  2.7 16.6 %all-to-all-start = ((f32[16,32,128]{2,1,0:T(8,128)}), f32[16,32,128]{2,1,0:T(8,128)S(1)}, u32[]{:S(2)}, u32[]{:S(2)}) async-start(f32[16,32,128]{2,1,0:T(8,128)} %bitcast.9), calls=%async_computation | async-start | bytes 524288 | tf_op jit(solution)/shard_map/all_to_all | solution.py:460
  11.8 1.5 %collective-permute-start = (f32[400,128]{1,0:T(8,128)S(1)}, f32[400,128]{1,0:T(8,128)S(1)}, u32[]{:S(2)}, u32[]{:S(2)}) collective-permute-start(f32[400,128]{1,0:T(8,128)S(1)} %get-tuple-element.26), channel_id=1, source_target_pairs={{0,16},{16,0},{1,17},{17,1},{2,18},{18,2},{3,19},{19,3},{4,20},{20... | collective-permute-start | bytes 614408 | tf_op jit(solution)/shard_map/ppermute | solution.py:472
  19.6 10.7 %collective-permute-start.1 = (f32[8,64,128]{2,1,0:T(8,128)S(1)}, f32[8,64,128]{2,1,0:T(8,128)S(1)}, u32[]{:S(2)}, u32[]{:S(2)}) collective-permute-start(f32[8,64,128]{2,1,0:T(8,128)S(1)} %get-tuple-element.27), channel_id=1, source_target_pairs={{0,16},{16,0},{1,17},{17,1},{2,18},{18,2},{3,19},{19,3},{4,20},{20... | collective-permute-start | bytes 786440 | tf_op jit(solution)/shard_map/ppermute | solution.py:504
  19.7 11.0 %collective-permute-start.3 = (f32[136,128]{1,0:T(8,128)S(1)}, f32[136,128]{1,0:T(8,128)S(1)}, u32[]{:S(2)}, u32[]{:S(2)}) collective-permute-start(f32[136,128]{1,0:T(8,128)S(1)} %get-tuple-element.29), channel_id=1, source_target_pairs={{1,18},{2,17},{3,20},{4,19},{5,22},{6,21},{7,24},{8,23},{9,26},{10... | collective-permute-start | bytes 208904 | tf_op jit(solution)/shard_map/ppermute | solution.py:506
  20.4 10.4 %collective-permute-start.2 = (f32[136,128]{1,0:T(8,128)S(1)}, f32[136,128]{1,0:T(8,128)S(1)}, u32[]{:S(2)}, u32[]{:S(2)}) collective-permute-start(f32[136,128]{1,0:T(8,128)S(1)} %get-tuple-element.28.after_ref), channel_id=1, source_target_pairs={{0,17},{1,16},{2,19},{3,18},{4,21},{5,20},{6,23},{7,22},{8,25},{9,... | collective-permute-start | bytes 208904 | tf_op jit(solution)/shard_map/ppermute | solution.py:505

commit v8 on v7

--- a/solution.py
+++ b/solution.py
@@ -49,7 +49,7 @@
     return lax.div(b, per), lax.rem(b, per)
 
 
-def gather_kernel(rows, lead, index_ref, state_ref, *refs):
+def gather_kernel(rows, group, index_ref, state_ref, *refs):
     small = (len(refs) - 5) // 2
     sides, out_hbm, x_ref = refs[:small], refs[small], refs[small + 1]
     side_outs, (rows_ref, out_ref, sems) = refs[small + 2 : 2 * small + 2], refs[2 * small + 2 :]
@@ -76,19 +76,17 @@
     for copy in copies[:per]:
         copy.wait()
 
-    def band(n, carry):
-        d = n + lead
-        d = jnp.where(d >= bands, d - bands, d)
+    def band(n):
         for j in range(cap):
-            r, c = block_place(rows_ref[j, d], per)
+            r, c = block_place(rows_ref[j, group[n]], per)
             piece = x_ref[c, pl.ds(r, FLUX, stride=rows), :]
             out_ref[pl.ds(n * (cap * FLUX) + j, FLUX, stride=cap), :] = piece
-        return carry
 
     span = bands // OUTPARTS
     size = span * cap * FLUX
     for p in range(OUTPARTS):
-        lax.fori_loop(p * span, (p + 1) * span, band, 0, unroll=2)
+        for n in range(p * span, (p + 1) * span):
+            band(n)
         part = slice(p * size, (p + 1) * size)
         copy = pltpu.make_async_copy(
             out_ref.at[part, :], out_hbm.at[part, :], sems.at[2 * per + 1 + small + p]
@@ -152,7 +150,7 @@
 
 
 def early_kernel(
-    rows, skip, slots_ref, weights_ref, x_ref, kappa_ref, mask_ref, vmix_ref,
+    rows, group, slots_ref, weights_ref, x_ref, kappa_ref, mask_ref, vmix_ref,
     pack_ref, table_ref,
 ):
     over, blocks = slots_ref.shape
@@ -160,11 +158,16 @@
     levels = x_ref.shape[1] // rows
     size = payload_rows(levels, per)
     slots = (pack_ref.shape[0] - 2 * size) // blocks * LANES
-    row = lax.broadcasted_iota(jnp.int32, (slots, blocks), 0) + skip
-    row = jnp.where(row >= slots, row - slots, row)
-    mat = jnp.zeros((slots, blocks), jnp.float32)
-    for k in range(over):
-        mat = mat + jnp.where(slots_ref[k : k + 1, :] == row, weights_ref[k : k + 1, :], 0.0)
+    cap = slots // len(group)
+    row = lax.broadcasted_iota(jnp.int32, (cap, blocks), 0)
+    mat = []
+    for d in group:
+        part = jnp.zeros((cap, blocks), jnp.float32)
+        for k in range(over):
+            hit = slots_ref[k : k + 1, :] == row + d * cap
+            part = part + jnp.where(hit, weights_ref[k : k + 1, :], 0.0)
+        mat.append(part)
+    mat = jnp.concatenate(mat, axis=0)
     b0 = lax.broadcasted_iota(jnp.int32, (blocks, blocks), 0)
     b1 = lax.broadcasted_iota(jnp.int32, (blocks, blocks), 1)
     order = jnp.where(lax.rem(b0, rows) * per + lax.div(b0, rows) == b1, 1.0, 0.0)
@@ -443,9 +446,10 @@
         return [((c * bands) + i, (c ^ 1) * bands + k) for c in range(comps) for i, k in pairs]
 
     sides = (kap, land_mask, recv_slots[0, 0].T, recv_weights[0, 0].T, vm)
-    lead = bands * 5 // 16
+    lead = bands * 7 // 16
+    group = [lead] + [n for n in reversed(range(bands)) if n != lead]
     bucket, columns, kap, land_mask, slots, weights, vm = call(
-        functools.partial(gather_kernel, rows, lead),
+        functools.partial(gather_kernel, rows, group),
         (jax.ShapeDtypeStruct((bands * FLUX * cap, LANES), f32), field)
         + tuple(jax.ShapeDtypeStruct(a.shape, a.dtype) for a in sides),
         [HBM] * (2 + len(sides)),
@@ -456,12 +460,11 @@
             pltpu.SemaphoreType.DMA((2 * per + 1 + len(sides) + OUTPARTS,)),
         ),
     )(*[in_hbm(a) for a in (send_rows[0, 0].T, flat) + sides])
-    group = [(lead + n) % bands for n in range(bands)]
     moved = lax.all_to_all(
         bucket.reshape(bands, FLUX * cap, LANES), "tile", 0, 0, axis_index_groups=[group]
     )
     pack, table = call(
-        functools.partial(early_kernel, rows, lead * cap),
+        functools.partial(early_kernel, rows, group),
         (
             jax.ShapeDtypeStruct((bands * cap // LANES * blocks + 2 * pay.shape[0], LANES), f32),
             jax.ShapeDtypeStruct((levels * levels, LANES), f32),

time: 44.6 us -> 43 us (0.964)
  blocking collectives: 10.7 us -> 9.28 us
    all_to_all x1, blocking collectives: 10.7 us -> 9.28 us  [body(): sums = lax.all_to_all(sums, ('comp', 'tile'), 0, 0)]
where the time goes in v8:
time: 43 us; the launch traced here: 42.7 us
  starting transfers between devices  13.2 us (31%)
  Pallas kernels  12.4 us (29%)
  blocking collectives  9.28 us (22%)
  waiting for transfers between devices  7.05 us (16%)
  between operations  0.73 us (2%)
    all_to_all x1, blocking collectives, body(): sums = lax.all_to_all(sums, ('comp', 'tile'), 0, 0)  9.28 us
    all_to_all x1, starting transfers between devices, body(): lax.all_to_all(bucket.reshape(bands, FLUX * cap, LANES), 'tile', 0, 0, ax...  8.83 us
    all_to_all x1, waiting for transfers between devices, body(): lax.all_to_all(bucket.reshape(bands, FLUX * cap, LANES), 'tile', 0, 0, ax...  5.61 us
    pallas_call x1, Pallas kernels, body(): call(gram_kernel, jax.ShapeDtypeStruct((2, LANES), f32), [HBM], VMEM, scr...  3.61 us
    ppermute x1, starting transfers between devices, body(): edge1 = lax.ppermute(edge1, ('comp', 'tile'), crossed(pairs1))  3.6 us
    pallas_call x1, Pallas kernels, body(): call(functools.partial(gather_kernel, rows, group), (jax.ShapeDtypeStruct...  1.96 us
    pallas_call x1, Pallas kernels, body(): call(fetch_kernel, jax.ShapeDtypeStruct(vectors.shape, vectors.dtype), [p...  1.93 us
    pallas_call x1, Pallas kernels, body(): call(functools.partial(finish_kernel, rows, total), (jax.ShapeDtypeStruct...  1.73 us
  transfers between devices with their start and end apart: 5, of which 2 were waited for; matrix products, arithmetic and copies ran while one was open for 0% of the time, Pallas kernels for 17%

profile of v8, /device:TPU:0, one launch (start us, length us, event | category | flops | bytes accessed | tf_op | source)
XLA Modules:
  0.0 42.7 jit_solution(6760949605775219932)
XLA Ops:
  0.6 2.0 %shard_map.95 = (f32[512,128]{1,0:T(8,128)}, f32[8,128,128]{2,1,0:T(8,128)S(1)}, f32[16,1024]{1,0:T(8,128)S(1)}, s32[16,1024]{1,0:T(8,128)S(1)}, s32[4,128]{1,0:...) custom-call(s32[8,16]{1,0:T(8,128)} %bitcast.20, f32[128,1024]{1,0:T(8,128)} %bitcast.18, f32[16,1024]{1,0:T(8,128)} %bitcast.19, ...), custom_call_target="tpu_custom_call" | custom-call | tf_op jit(solution)/shard_map/pallas_call | solution.py:451
  2.6 8.8 %all-to-all-start = ((f32[16,32,128]{2,1,0:T(8,128)}), f32[16,32,128]{2,1,0:T(8,128)S(1)}, u32[]{:S(2)}, u32[]{:S(2)}) async-start(f32[16,32,128]{2,1,0:T(8,128)} %bitcast.9), calls=%async_computation | async-start | bytes 524288 | tf_op jit(solution)/shard_map/all_to_all | solution.py:463
  11.4 0.3 shard_map.96
  11.7 0.1 collective-permute-start
  11.8 1.4 %collective-permute-done.pack_ref = f32[400,128]{1,0:T(8,128)S(1)} collective-permute-done((f32[400,128]{1,0:T(8,128)S(1)}, f32[400,128]{1,0:T(8,128)S(1)}, u32[]{:S(2)}, u32[]{:S(2)}) %collective-permute-start) | collective-permute-done | bytes 204832 | tf_op jit(solution)/shard_map/ppermute | solution.py:475
  13.2 5.6 %all-to-all-done.buf_ref = f32[16,32,128]{2,1,0:T(8,128)S(1)} async-done(((f32[16,32,128]{2,1,0:T(8,128)}), f32[16,32,128]{2,1,0:T(8,128)S(1)}, u32[]{:S(2)}, u32[]{:S(2)}) %all-to-all-start) | async-done | bytes 262176 | tf_op jit(solution)/shard_map/all_to_all | solution.py:463
  18.8 0.3 shard_map.98
  19.1 0.1 collective-permute-start.1
  19.2 0.7 %collective-permute-start.3 = (f32[136,128]{1,0:T(8,128)S(1)}, f32[136,128]{1,0:T(8,128)S(1)}, u32[]{:S(2)}, u32[]{:S(2)}) collective-permute-start(f32[136,128]{1,0:T(8,128)S(1)} %get-tuple-element.29), channel_id=1, source_target_pairs={{1,18},{2,17},{3,20},{4,19},{5,22},{6,21},{7,24},{8,23},{9,26},{10... | collective-permute-start | bytes 208904 | tf_op jit(solution)/shard_map/ppermute | solution.py:509
  19.9 3.6 %collective-permute-start.2 = (f32[136,128]{1,0:T(8,128)S(1)}, f32[136,128]{1,0:T(8,128)S(1)}, u32[]{:S(2)}, u32[]{:S(2)}) collective-permute-start(f32[136,128]{1,0:T(8,128)S(1)} %get-tuple-element.28.after_ref), channel_id=1, source_target_pairs={{0,17},{1,16},{2,19},{3,18},{4,21},{5,20},{6,23},{7,22},{8,25},{9,... | collective-permute-start | bytes 208904 | tf_op jit(solution)/shard_map/ppermute | solution.py:508
  23.5 3.6 %shard_map.101.gram_ref = f32[2,128]{1,0:T(2,128)S(1)} custom-call(bf16[12,8,16,1024]{3,2,1,0:T(8,128)(2,1)} %bitcast.16), custom_call_target="tpu_custom_call" | custom-call | tf_op jit(solution)/shard_map/pallas_call | solution.py:476
  27.1 1.2 %shard_map.97.still_ref = f32[8,128,128]{2,1,0:T(8,128)S(1)} custom-call(f32[8,128,128]{2,1,0:T(8,128)S(1)} %get-tuple-element.18.x_ref.x0_ref, f32[16,1024]{1,0:T(8,128)S(1)} %get-tuple-element.19.kappa_ref, s32[16,1024]{1,0:T(8,128)S(1)} %get-tuple-element.20.mask_ref, f32[64,128]{1,0:T(8,128)S(1)} %get-tuple-element.24.table_ref), custom_call_target="tpu_custom_call" | custom-call | tf_op jit(solution)/shard_map/pallas_call | solution.py:486
  28.3 1.9 %shard_map.100.basis_ref = bf16[12,8,16,1024]{3,2,1,0:T(8,128)(2,1)S(1)} custom-call(f32[136,128]{1,0:T(8,128)S(1)} %get-tuple-element.28.after_ref, bf16[12,8,16,1024]{3,2,1,0:T(8,128)(2,1)} %bitcast.17), custom_call_target="tpu_custom_call" | custom-call | tf_op jit(solution)/shard_map/pallas_call | solution.py:500
  30.2 0.0 collective-permute-done.1.f_ref
  30.2 0.4 shard_map.99.most_ref
  30.6 0.0 collective-permute-done.3.h2_ref
  30.6 0.0 collective-permute-done.2.h1_ref
  30.6 1.0 %shard_map.102 = (f32[8,128,128]{2,1,0:T(8,128)S(1)}, f32[32,2,128]{2,1,0:T(2,128)S(1)}) custom-call(f32[8,128,128]{2,1,0:T(8,128)S(1)} %shard_map.99.most_ref, f32[8,128,128]{2,1,0:T(8,128)S(1)} %get-tuple-element.18.x_ref.x0_ref, f32[136,128]{1,0:T(8,128)S(1)} %collective-permute-done.2.h1_ref, ...), custom_call_target="tpu_custom_call", output_to_operand_aliasing={{0}: (0, {})} | custom-call | tf_op jit(solution)/shard_map/pallas_call | solution.py:517
  31.7 9.3 %all_to_all.10.sums_ref = f32[32,2,128]{2,1,0:T(2,128)S(1)} all-to-all(f32[32,2,128]{2,1,0:T(2,128)S(1)} %get-tuple-element.31), channel_id=1, replica_groups=mesh['comp'=2,'tile'=16] {'comp','tile'}, dimensions={0} | all-to-all | bytes 65536 | tf_op jit(solution)/shard_map/all_to_all | solution.py:524
  41.0 1.7 %shard_map.103 = (f32[128,1024]{1,0:T(8,128)}, f32[1,12]{1,0:T(1,128)}) custom-call(f32[8,128,128]{2,1,0:T(8,128)S(1)} %get-tuple-element.30.x_ref, bf16[12,8,16,1024]{3,2,1,0:T(8,128)(2,1)S(1)} %shard_map.100.basis_ref, f32[32,2,128]{2,1,0:T(2,128)S(1)} %all_to_all.10.sums_ref), custom_call_target="tpu_custom_call" | custom-call | tf_op jit(solution)/shard_map/pallas_call | solution.py:525
Async XLA Ops:
  2.6 16.2 %all-to-all-start = ((f32[16,32,128]{2,1,0:T(8,128)}), f32[16,32,128]{2,1,0:T(8,128)S(1)}, u32[]{:S(2)}, u32[]{:S(2)}) async-start(f32[16,32,128]{2,1,0:T(8,128)} %bitcast.9), calls=%async_computation | async-start | bytes 524288 | tf_op jit(solution)/shard_map/all_to_all | solution.py:463
  11.7 1.5 %collective-permute-start = (f32[400,128]{1,0:T(8,128)S(1)}, f32[400,128]{1,0:T(8,128)S(1)}, u32[]{:S(2)}, u32[]{:S(2)}) collective-permute-start(f32[400,128]{1,0:T(8,128)S(1)} %get-tuple-element.26), channel_id=1, source_target_pairs={{0,16},{16,0},{1,17},{17,1},{2,18},{18,2},{3,19},{19,3},{4,20},{20... | collective-permute-start | bytes 614408 | tf_op jit(solution)/shard_map/ppermute | solution.py:475
  19.1 11.1 %collective-permute-start.1 = (f32[8,64,128]{2,1,0:T(8,128)S(1)}, f32[8,64,128]{2,1,0:T(8,128)S(1)}, u32[]{:S(2)}, u32[]{:S(2)}) collective-permute-start(f32[8,64,128]{2,1,0:T(8,128)S(1)} %get-tuple-element.27), channel_id=1, source_target_pairs={{0,16},{16,0},{1,17},{17,1},{2,18},{18,2},{3,19},{19,3},{4,20},{20... | collective-permute-start | bytes 786440 | tf_op jit(solution)/shard_map/ppermute | solution.py:507
  19.2 11.4 %collective-permute-start.3 = (f32[136,128]{1,0:T(8,128)S(1)}, f32[136,128]{1,0:T(8,128)S(1)}, u32[]{:S(2)}, u32[]{:S(2)}) collective-permute-start(f32[136,128]{1,0:T(8,128)S(1)} %get-tuple-element.29), channel_id=1, source_target_pairs={{1,18},{2,17},{3,20},{4,19},{5,22},{6,21},{7,24},{8,23},{9,26},{10... | collective-permute-start | bytes 208904 | tf_op jit(solution)/shard_map/ppermute | solution.py:509
  19.9 10.8 %collective-permute-start.2 = (f32[136,128]{1,0:T(8,128)S(1)}, f32[136,128]{1,0:T(8,128)S(1)}, u32[]{:S(2)}, u32[]{:S(2)}) collective-permute-start(f32[136,128]{1,0:T(8,128)S(1)} %get-tuple-element.28.after_ref), channel_id=1, source_target_pairs={{0,17},{1,16},{2,19},{3,18},{4,21},{5,20},{6,23},{7,22},{8,25},{9,... | collective-permute-start | bytes 208904 | tf_op jit(solution)/shard_map/ppermute | solution.py:508

commit v9 on v8

--- a/solution.py
+++ b/solution.py
@@ -363,7 +363,9 @@
         return tuple(accs)
 
     zero = jnp.zeros((8, LANES), jnp.float32)
-    accs = lax.fori_loop(0, levels, level, (zero,) * (vecs + 1))
+    accs = (zero,) * (vecs + 1)
+    for l in range(levels):
+        accs = level(l, accs)
     lane = lax.broadcasted_iota(jnp.int32, (1, LANES), 1)
     line = jnp.zeros((1, LANES), jnp.float32)
     for i in range(vecs + 1):
@@ -397,22 +399,23 @@
         quad = quad + splat[i] * jnp.where(lane < vecs, line, 0.0)
     extra = jnp.sum(coef * (quad - 2.0 * total * coef), axis=1, keepdims=True)
     scale = 1.0 / jnp.sqrt((square + extra) / total + 1e-06)
-    wide = [jnp.broadcast_to(scale * s, (8, LANES)) for s in splat]
+    wide = [jnp.broadcast_to(s, (8, LANES)) for s in splat]
     scale = jnp.broadcast_to(scale, (8, LANES))
 
     def level(l, carry):
         for c in range(per):
             s = slice(c * LANES, (c + 1) * LANES)
-            x = x_ref[c, pl.ds(l * rows, rows), :].reshape(rows // 8, 8, LANES) * scale
+            x = x_ref[c, pl.ds(l * rows, rows), :].reshape(rows // 8, 8, LANES)
             for i in range(vecs):
                 b = basis_ref[i, l, :, s].astype(jnp.float32).reshape(rows // 8, 8, LANES)
                 x = x - wide[i] * b
-            out_ref[pl.ds(l * rows, rows), s] = x.reshape(rows, LANES)
+            out_ref[pl.ds(l * rows, rows), s] = (x * scale).reshape(rows, LANES)
         return carry
 
     span = levels // PUTS
     for p in range(PUTS):
-        lax.fori_loop(p * span, (p + 1) * span, level, 0)
+        for l in range(p * span, (p + 1) * span):
+            level(l, 0)
         part = slice(p * span * rows, (p + 1) * span * rows)
         copy = pltpu.make_async_copy(out_ref.at[part, :], out_hbm.at[part, :], sems.at[p])
         copy.start()

time: 43 us -> 42.7 us (level)
  no operation moved by 1% of the time
where the time goes in v9:
time: 42.7 us; the launch traced here: 42.4 us
  starting transfers between devices  13.2 us (31%)
  Pallas kernels  12.1 us (28%)
  blocking collectives  9.28 us (22%)
  waiting for transfers between devices  7.05 us (17%)
  between operations  0.73 us (2%)
    all_to_all x1, blocking collectives, body(): sums = lax.all_to_all(sums, ('comp', 'tile'), 0, 0)  9.28 us
    all_to_all x1, starting transfers between devices, body(): lax.all_to_all(bucket.reshape(bands, FLUX * cap, LANES), 'tile', 0, 0, ax...  8.83 us
    all_to_all x1, waiting for transfers between devices, body(): lax.all_to_all(bucket.reshape(bands, FLUX * cap, LANES), 'tile', 0, 0, ax...  5.61 us
    pallas_call x1, Pallas kernels, body(): call(gram_kernel, jax.ShapeDtypeStruct((2, LANES), f32), [HBM], VMEM, scr...  3.61 us
    ppermute x1, starting transfers between devices, body(): edge1 = lax.ppermute(edge1, ('comp', 'tile'), crossed(pairs1))  3.6 us
    pallas_call x1, Pallas kernels, body(): call(functools.partial(gather_kernel, rows, group), (jax.ShapeDtypeStruct...  1.96 us
    pallas_call x1, Pallas kernels, body(): call(fetch_kernel, jax.ShapeDtypeStruct(vectors.shape, vectors.dtype), [p...  1.93 us
    pallas_call x1, Pallas kernels, body(): call(functools.partial(finish_kernel, rows, total), (jax.ShapeDtypeStruct...  1.51 us
  transfers between devices with their start and end apart: 5, of which 2 were waited for; matrix products, arithmetic and copies ran while one was open for 0% of the time, Pallas kernels for 17%

profile of v9, /device:TPU:0, one launch (start us, length us, event | category | flops | bytes accessed | tf_op | source)
XLA Modules:
  0.0 42.4 jit_solution(4447639537137453364)
XLA Ops:
  0.6 2.0 %shard_map.95 = (f32[512,128]{1,0:T(8,128)}, f32[8,128,128]{2,1,0:T(8,128)S(1)}, f32[16,1024]{1,0:T(8,128)S(1)}, s32[16,1024]{1,0:T(8,128)S(1)}, s32[4,128]{1,0:...) custom-call(s32[8,16]{1,0:T(8,128)} %bitcast.20, f32[128,1024]{1,0:T(8,128)} %bitcast.18, f32[16,1024]{1,0:T(8,128)} %bitcast.19, ...), custom_call_target="tpu_custom_call" | custom-call | tf_op jit(solution)/shard_map/pallas_call | solution.py:454
  2.6 8.8 %all-to-all-start = ((f32[16,32,128]{2,1,0:T(8,128)}), f32[16,32,128]{2,1,0:T(8,128)S(1)}, u32[]{:S(2)}, u32[]{:S(2)}) async-start(f32[16,32,128]{2,1,0:T(8,128)} %bitcast.9), calls=%async_computation | async-start | bytes 524288 | tf_op jit(solution)/shard_map/all_to_all | solution.py:466
  11.4 0.3 shard_map.96
  11.7 0.1 collective-permute-start
  11.8 1.4 %collective-permute-done.pack_ref = f32[400,128]{1,0:T(8,128)S(1)} collective-permute-done((f32[400,128]{1,0:T(8,128)S(1)}, f32[400,128]{1,0:T(8,128)S(1)}, u32[]{:S(2)}, u32[]{:S(2)}) %collective-permute-start) | collective-permute-done | bytes 204832 | tf_op jit(solution)/shard_map/ppermute | solution.py:478
  13.2 5.6 %all-to-all-done.buf_ref = f32[16,32,128]{2,1,0:T(8,128)S(1)} async-done(((f32[16,32,128]{2,1,0:T(8,128)}), f32[16,32,128]{2,1,0:T(8,128)S(1)}, u32[]{:S(2)}, u32[]{:S(2)}) %all-to-all-start) | async-done | bytes 262176 | tf_op jit(solution)/shard_map/all_to_all | solution.py:466
  18.8 0.3 shard_map.98
  19.1 0.1 collective-permute-start.1
  19.2 0.7 %collective-permute-start.3 = (f32[136,128]{1,0:T(8,128)S(1)}, f32[136,128]{1,0:T(8,128)S(1)}, u32[]{:S(2)}, u32[]{:S(2)}) collective-permute-start(f32[136,128]{1,0:T(8,128)S(1)} %get-tuple-element.29), channel_id=1, source_target_pairs={{1,18},{2,17},{3,20},{4,19},{5,22},{6,21},{7,24},{8,23},{9,26},{10... | collective-permute-start | bytes 208904 | tf_op jit(solution)/shard_map/ppermute | solution.py:512
  19.9 3.6 %collective-permute-start.2 = (f32[136,128]{1,0:T(8,128)S(1)}, f32[136,128]{1,0:T(8,128)S(1)}, u32[]{:S(2)}, u32[]{:S(2)}) collective-permute-start(f32[136,128]{1,0:T(8,128)S(1)} %get-tuple-element.28.after_ref), channel_id=1, source_target_pairs={{0,17},{1,16},{2,19},{3,18},{4,21},{5,20},{6,23},{7,22},{8,25},{9,... | collective-permute-start | bytes 208904 | tf_op jit(solution)/shard_map/ppermute | solution.py:511
  23.5 3.6 %shard_map.101.gram_ref = f32[2,128]{1,0:T(2,128)S(1)} custom-call(bf16[12,8,16,1024]{3,2,1,0:T(8,128)(2,1)} %bitcast.16), custom_call_target="tpu_custom_call" | custom-call | tf_op jit(solution)/shard_map/pallas_call | solution.py:479
  27.1 1.2 %shard_map.97.still_ref = f32[8,128,128]{2,1,0:T(8,128)S(1)} custom-call(f32[8,128,128]{2,1,0:T(8,128)S(1)} %get-tuple-element.18.x_ref.x0_ref, f32[16,1024]{1,0:T(8,128)S(1)} %get-tuple-element.19.kappa_ref, s32[16,1024]{1,0:T(8,128)S(1)} %get-tuple-element.20.mask_ref, f32[64,128]{1,0:T(8,128)S(1)} %get-tuple-element.24.table_ref), custom_call_target="tpu_custom_call" | custom-call | tf_op jit(solution)/shard_map/pallas_call | solution.py:489
  28.3 1.9 %shard_map.100.basis_ref = bf16[12,8,16,1024]{3,2,1,0:T(8,128)(2,1)S(1)} custom-call(f32[136,128]{1,0:T(8,128)S(1)} %get-tuple-element.28.after_ref, bf16[12,8,16,1024]{3,2,1,0:T(8,128)(2,1)} %bitcast.17), custom_call_target="tpu_custom_call" | custom-call | tf_op jit(solution)/shard_map/pallas_call | solution.py:503
  30.2 0.0 collective-permute-done.1.f_ref
  30.2 0.4 shard_map.99.most_ref
  30.6 0.0 collective-permute-done.3.h2_ref
  30.6 0.0 collective-permute-done.2.h1_ref
  30.6 1.0 %shard_map.102 = (f32[8,128,128]{2,1,0:T(8,128)S(1)}, f32[32,2,128]{2,1,0:T(2,128)S(1)}) custom-call(f32[8,128,128]{2,1,0:T(8,128)S(1)} %shard_map.99.most_ref, f32[8,128,128]{2,1,0:T(8,128)S(1)} %get-tuple-element.18.x_ref.x0_ref, f32[136,128]{1,0:T(8,128)S(1)} %collective-permute-done.2.h1_ref, ...), custom_call_target="tpu_custom_call", output_to_operand_aliasing={{0}: (0, {})} | custom-call | tf_op jit(solution)/shard_map/pallas_call | solution.py:520
  31.6 9.3 %all_to_all.10.sums_ref = f32[32,2,128]{2,1,0:T(2,128)S(1)} all-to-all(f32[32,2,128]{2,1,0:T(2,128)S(1)} %get-tuple-element.31), channel_id=1, replica_groups=mesh['comp'=2,'tile'=16] {'comp','tile'}, dimensions={0} | all-to-all | bytes 65536 | tf_op jit(solution)/shard_map/all_to_all | solution.py:527
  40.9 1.5 %shard_map.103 = (f32[128,1024]{1,0:T(8,128)}, f32[1,12]{1,0:T(1,128)}) custom-call(f32[8,128,128]{2,1,0:T(8,128)S(1)} %get-tuple-element.30.x_ref, bf16[12,8,16,1024]{3,2,1,0:T(8,128)(2,1)S(1)} %shard_map.100.basis_ref, f32[32,2,128]{2,1,0:T(2,128)S(1)} %all_to_all.10.sums_ref), custom_call_target="tpu_custom_call" | custom-call | tf_op jit(solution)/shard_map/pallas_call | solution.py:528
Async XLA Ops:
  2.6 16.2 %all-to-all-start = ((f32[16,32,128]{2,1,0:T(8,128)}), f32[16,32,128]{2,1,0:T(8,128)S(1)}, u32[]{:S(2)}, u32[]{:S(2)}) async-start(f32[16,32,128]{2,1,0:T(8,128)} %bitcast.9), calls=%async_computation | async-start | bytes 524288 | tf_op jit(solution)/shard_map/all_to_all | solution.py:466
  11.7 1.5 %collective-permute-start = (f32[400,128]{1,0:T(8,128)S(1)}, f32[400,128]{1,0:T(8,128)S(1)}, u32[]{:S(2)}, u32[]{:S(2)}) collective-permute-start(f32[400,128]{1,0:T(8,128)S(1)} %get-tuple-element.26), channel_id=1, source_target_pairs={{0,16},{16,0},{1,17},{17,1},{2,18},{18,2},{3,19},{19,3},{4,20},{20... | collective-permute-start | bytes 614408 | tf_op jit(solution)/shard_map/ppermute | solution.py:478
  19.1 11.1 %collective-permute-start.1 = (f32[8,64,128]{2,1,0:T(8,128)S(1)}, f32[8,64,128]{2,1,0:T(8,128)S(1)}, u32[]{:S(2)}, u32[]{:S(2)}) collective-permute-start(f32[8,64,128]{2,1,0:T(8,128)S(1)} %get-tuple-element.27), channel_id=1, source_target_pairs={{0,16},{16,0},{1,17},{17,1},{2,18},{18,2},{3,19},{19,3},{4,20},{20... | collective-permute-start | bytes 786440 | tf_op jit(solution)/shard_map/ppermute | solution.py:510
  19.2 11.4 %collective-permute-start.3 = (f32[136,128]{1,0:T(8,128)S(1)}, f32[136,128]{1,0:T(8,128)S(1)}, u32[]{:S(2)}, u32[]{:S(2)}) collective-permute-start(f32[136,128]{1,0:T(8,128)S(1)} %get-tuple-element.29), channel_id=1, source_target_pairs={{1,18},{2,17},{3,20},{4,19},{5,22},{6,21},{7,24},{8,23},{9,26},{10... | collective-permute-start | bytes 208904 | tf_op jit(solution)/shard_map/ppermute | solution.py:512
  19.9 10.8 %collective-permute-start.2 = (f32[136,128]{1,0:T(8,128)S(1)}, f32[136,128]{1,0:T(8,128)S(1)}, u32[]{:S(2)}, u32[]{:S(2)}) collective-permute-start(f32[136,128]{1,0:T(8,128)S(1)} %get-tuple-element.28.after_ref), channel_id=1, source_target_pairs={{0,17},{1,16},{2,19},{3,18},{4,21},{5,20},{6,23},{7,22},{8,25},{9,... | collective-permute-start | bytes 208904 | tf_op jit(solution)/shard_map/ppermute | solution.py:511
